TPU v7x, 256 devices: a whole 4x4x8 slice. The times are simulated.
256 devices in a mesh: morton: 64 (over y, x_hi, z), sub: 4 (over x_lo, core).
Axes of the slice: x: 4 (x_hi: 2, x_lo: 2; x = x_hi * 2 + x_lo), y: 4, z: 8, core: 2. Of those that a mesh axis runs over, the one named last changes fastest.
Arguments:
- multipoles: bfloat16 [16384, 128], P(('morton', 'sub')), may hold values from -6 to 6
- translations: bfloat16 [316, 128, 128], P('sub'), may hold values from -0.0625 to 0.0625
- upward_ops: bfloat16 [8, 128, 128], replicated, may hold values from -0.1875 to 0.1875
- downward_ops: bfloat16 [8, 128, 128], replicated, may hold values from -0.375 to 0.375
- targets_l6: int32 [64, 316, 128], P('morton', 'sub'), may hold values from 0 to 255, as said below
- source_boxes_level6: int32 [64, 316, 128], P('morton', 'sub'), may hold values from 0 to 767, as said below
- counts_l6: int32 [64, 316], P('morton', 'sub'), may hold values from 1 to 128, as said below
- target_boxes_level5: int32 [64, 316, 16], P('morton', 'sub'), may hold values from 0 to 31, as said below
- anchors_l5: int32 [64, 316, 16], P('morton', 'sub'), may hold values from 0 to 255, as said below
- counts_l5: int32 [64, 316], P('morton', 'sub'), may hold values from 1 to 16, as said below
- targets_l4: int32 [64, 316, 2], P('morton', 'sub'), may hold values from 0 to 3, as said below
- anchors_l4: int32 [64, 316, 2], P('morton', 'sub'), may hold values from 0 to 31, as said below
- counts_l4: int32 [64, 316], P('morton', 'sub'), may hold values from 1 to 2, as said below
Outputs:
- local_exp: bfloat16 [16384, 128], P(('morton', 'sub'))
Inputs may be any that keep to these rules, and one draw needn't show every extreme that they name: `targets_l6`: targets of one operator's block within one subtree are its level-6 boxes. `source_boxes_level6`: sources lie in the previous, own or next subtree, at most 256 boxes before or after the target. `counts_l6`: some block of every subtree is full. `target_boxes_level5`: targets are level-5 boxes of the subtree. `anchors_l5`: sources are level-5 boxes of the aligned group of 8 subtrees. `counts_l5`: some block of every subtree is full. `targets_l4`: targets are level-4 boxes of the subtree. `anchors_l4`: sources are level-4 boxes of the aligned group of 8 subtrees. `counts_l4`: some block of every subtree is full.
All inputs are finite; a program needn't handle non-finite values.
Results may differ from a plain program's by a relative error of at most 0.011.
Values may be sent and summed in bfloat16 or wider, within the bound.
No kernel may reach another device: no remote copies, remote signals or barrier semaphores. Data moves between devices by JAX's collectives and lax.ppermute only.
A program may use at most 64 MiB of HBM per device.

v0:
```python
import jax
import jax.numpy as jnp
from jax import lax
from jax.sharding import PartitionSpec as P


def swapped(shard, axis, apart):
    return lax.ppermute(shard, axis, [(i, i ^ 1 << apart) for i in range(lax.axis_size(axis))])


def with_halo(shard, sides, width):
    for axis, dim in sides:
        size, length = (lax.axis_size(axis), shard.shape[dim])
        up = [(i, (i + 1) % size) for i in range(size - 1)]
        down = [(j, i) for i, j in up]
        last = lax.slice_in_dim(shard, length - width, length, axis=dim)
        leading = lax.slice_in_dim(shard, 0, width, axis=dim)
        before = lax.ppermute(last, axis, up)
        after = lax.ppermute(leading, axis, down)
        shard = jnp.concatenate([before, shard, after], axis=dim)
    return shard


def translate_block(expansions, targets, anchors, counts, kernels, row_count, factor):
    operator_matrices, capacity = targets.shape
    coeff_width = expansions.shape[1]
    block_rows = min(capacity, 128)
    turn_count = capacity // block_rows
    target_steps = targets.reshape(operator_matrices, turn_count, block_rows).transpose(1, 0, 2)
    anchor_steps = anchors.reshape(operator_matrices, turn_count, block_rows).transpose(1, 0, 2)
    slot_steps = jnp.arange(capacity, dtype=jnp.int32).reshape(turn_count, block_rows)
    source_ids = jnp.arange(expansions.shape[0], dtype=jnp.int32)
    row_ids = jnp.arange(row_count, dtype=jnp.int32)

    def single_rotation(totals, inputs):
        target_rows, anchor_rows, slot_numbers = inputs
        selector = (anchor_rows.reshape(-1)[:, None] == source_ids[None, :]).astype(jnp.bfloat16)
        picked = jnp.dot(selector, expansions, preferred_element_type=jnp.float32).astype(
            jnp.bfloat16
        )
        picked = picked.reshape(operator_matrices, block_rows, coeff_width)
        product = jnp.einsum("obr,ors->obs", picked, kernels, preferred_element_type=jnp.float32)
        is_live = (slot_numbers[None, :] < counts[:, None]).reshape(-1)
        placing = jnp.logical_and(
            target_rows.reshape(-1)[:, None] == row_ids[None, :], is_live[:, None]
        )
        placing = placing.astype(jnp.float32) * factor
        added = jnp.einsum(
            "kt,kc->tc",
            placing,
            product.reshape(-1, coeff_width),
            precision=lax.Precision.HIGHEST,
            preferred_element_type=jnp.float32,
        )
        return (totals + added, None)

    totals, _ = lax.scan(
        single_rotation,
        jnp.zeros((row_count, coeff_width), jnp.float32),
        (target_steps, anchor_steps, slot_steps),
    )
    return totals


def upward(children, operator_matrices):
    parents = children.shape[0] // 8
    grouped_rows = children.reshape(parents, 8, children.shape[1])
    summed_values = jnp.einsum(
        "duo,uob->db", grouped_rows, operator_matrices, preferred_element_type=jnp.float32
    )
    return summed_values.astype(jnp.bfloat16)


def downward(parent, operator_matrices):
    spread = jnp.einsum(
        "pr,crs->pcs", parent, operator_matrices, preferred_element_type=jnp.float32
    )
    return spread.reshape(-1, parent.shape[1])


def gather_group(pieces):
    joined = (
        lax.all_gather(pieces[0], "sub", axis=0, tiled=True),
        lax.all_gather(pieces[1], "sub", axis=0, tiled=True),
    )
    position = lax.axis_index("morton")
    for level_bit in range(3):
        packed = jnp.concatenate(joined, axis=0)
        partner = swapped(packed, "morton", level_bit)
        is_upper = position >> level_bit & 1 == 1
        offset = 0
        updated = []
        for own_rows in joined:
            theirs = partner[offset : offset + own_rows.shape[0]]
            offset = offset + own_rows.shape[0]
            updated.append(
                jnp.where(
                    is_upper,
                    jnp.concatenate([theirs, own_rows], axis=0),
                    jnp.concatenate([own_rows, theirs], axis=0),
                )
            )
        joined = tuple(updated)
    return joined


def local(
    multipoles,
    translations,
    upward_ops,
    downward_ops,
    targets_l6,
    source_boxes_level6,
    counts_l6,
    target_boxes_level5,
    anchors_l5,
    counts_l5,
    targets_l4,
    anchors_l4,
    counts_l4,
):
    quarter = multipoles.shape[0]
    sub_count = lax.axis_size("sub")
    box_count = quarter * sub_count
    anchor_rows = source_boxes_level6[0]
    owned_rows = lax.all_gather(multipoles, "sub", axis=0, tiled=True)
    nearby = with_halo(owned_rows, (("morton", 0),), box_count)
    partial_six = translate_block(
        nearby, targets_l6[0], anchor_rows, counts_l6[0], translations, box_count, 1.0
    )
    far_six = lax.psum_scatter(
        partial_six.astype(jnp.bfloat16), "sub", scatter_dimension=0, tiled=True
    ).astype(jnp.float32)
    coarse5 = upward(multipoles, upward_ops)
    coarse4 = upward(coarse5, upward_ops)
    group_five, group_four = gather_group((coarse5, coarse4))
    partial_five = translate_block(
        group_five,
        target_boxes_level5[0],
        anchors_l5[0],
        counts_l5[0],
        translations,
        box_count // 8,
        0.5,
    )
    partial_four = translate_block(
        group_four, targets_l4[0], anchors_l4[0], counts_l4[0], translations, box_count // 64, 0.25
    )
    far_five, far_four = (
        lax.psum_scatter(partial_five, "sub", scatter_dimension=0, tiled=True),
        lax.psum_scatter(partial_four, "sub", scatter_dimension=0, tiled=True),
    )
    local4 = far_four.astype(jnp.bfloat16)
    local5 = (far_five + downward(local4, downward_ops)).astype(jnp.bfloat16)
    return (far_six + downward(local5, downward_ops)).astype(jnp.bfloat16)


def solution(mesh):
    placed = (
        P(("morton", "sub"), None),
        P("sub", None, None),
        P(),
        P(),
        P("morton", "sub", None),
        P("morton", "sub", None),
        P("morton", "sub"),
        P("morton", "sub", None),
        P("morton", "sub", None),
        P("morton", "sub"),
        P("morton", "sub", None),
        P("morton", "sub", None),
        P("morton", "sub"),
    )
    return jax.shard_map(
        local, mesh=mesh, in_specs=placed, out_specs=P(("morton", "sub"), None), check_vma=False
    )
```

profile of v0, /device:TPU:9, one launch (start us, length us, event | category | flops | bytes accessed | tf_op | source)
XLA Modules:
  0.0 123.9 jit_solution(2236106345753601395)
XLA Ops:
  6.5 7.3 %all_gather.9 = bf16[256,128]{1,0:T(8,128)(2,1)} all-gather(bf16[64,128]{1,0:T(8,128)(2,1)} %param.13), channel_id=1, replica_groups=mesh['morton'=64,'sub'=4] {'sub'}, dimensions={0}, use_global_device_ids=true | all-gather | bytes 81920 | tf_op jit(solution)/shard_map/all_gather | solution.py:126
  13.8 3.5 %collective-permute-start = (bf16[256,128]{1,0:T(8,128)(2,1)}, bf16[256,128]{1,0:T(8,128)(2,1)}, u32[]{:S(2)}, u32[]{:S(2)}) collective-permute-start(bf16[256,128]{1,0:T(8,128)(2,1)} %all_gather.9), channel_id=1, source_target_pairs={{0,4},{4,8},{8,12},{12,16},{16,20},{20,24},{24,28},{28,32},{32,36}... | collective-permute-start | bytes 196616 | tf_op jit(solution)/shard_map/ppermute | solution.py:18
  17.4 7.9 %collective-permute-start.1 = (bf16[256,128]{1,0:T(8,128)(2,1)}, bf16[256,128]{1,0:T(8,128)(2,1)}, u32[]{:S(2)}, u32[]{:S(2)}) collective-permute-start(bf16[256,128]{1,0:T(8,128)(2,1)} %all_gather.9), channel_id=1, source_target_pairs={{4,0},{8,4},{12,8},{16,12},{20,16},{24,20},{28,24},{32,28},{36,32}... | collective-permute-start | bytes 196616 | tf_op jit(solution)/shard_map/ppermute | solution.py:19
  25.3 1.1 fusion.11
  26.4 5.5 %all_gather.10 = bf16[32,128]{1,0:T(8,128)(2,1)S(1)} all-gather(bf16[8,128]{1,0:T(8,128)(2,1)S(1)} %fusion.11), channel_id=1, replica_groups=mesh['morton'=64,'sub'=4] {'sub'}, dimensions={0}, use_global_device_ids=true | all-gather | bytes 10240 | tf_op jit(solution)/shard_map/all_gather | solution.py:83
  31.9 1.1 fusion.13
  33.0 5.1 %all-gather.1 = bf16[4,1,128]{2,1,0:T(2,128)(2,1)S(1)} all-gather(bf16[1,1,128]{2,1,0:T(2,128)(2,1)S(1)} %fusion.13), channel_id=2, replica_groups=mesh['morton'=64,'sub'=4] {'sub'}, dimensions={0}, use_global_device_ids=true | all-gather | bytes 1280 | tf_op jit(solution)/shard_map/all_gather | solution.py:84
  38.1 0.7 fusion.43
  38.9 1.8 %collective-permute-done.2 = bf16[36,128]{1,0:T(8,128)(2,1)S(1)} collective-permute-done((bf16[36,128]{1,0:T(8,128)(2,1)S(1)}, bf16[36,128]{1,0:T(8,128)(2,1)S(1)}, u32[]{:S(2)}, u32[]{:S(2)}) %collective-permute-start.2) | collective-permute-done | bytes 9248 | tf_op jit(solution)/shard_map/ppermute | solution.py:8
  40.8 0.7 iota_compare_fusion.12
  41.5 2.8 %collective-permute-done.3 = bf16[72,128]{1,0:T(8,128)(2,1)S(1)} collective-permute-done((bf16[72,128]{1,0:T(8,128)(2,1)S(1)}, bf16[72,128]{1,0:T(8,128)(2,1)S(1)}, u32[]{:S(2)}, u32[]{:S(2)}) %collective-permute-start.3) | collective-permute-done | bytes 18464 | tf_op jit(solution)/shard_map/ppermute | solution.py:8
  44.4 2.3 %collective-permute-start.4 = (bf16[144,128]{1,0:T(8,128)(2,1)S(1)}, bf16[144,128]{1,0:T(8,128)(2,1)S(1)}, u32[]{:S(2)}, u32[]{:S(2)}) collective-permute-start(bf16[144,128]{1,0:T(8,128)(2,1)S(1)} %pad_maximum_fusion), channel_id=1, source_target_pairs={{0,16},{4,20},{8,24},{12,28},{16,0},{20,4},{24,8},{28,12},{32,48},... | collective-permute-start | bytes 110600 | tf_op jit(solution)/shard_map/ppermute | solution.py:8
  46.7 0.7 iota_compare_fusion.11
  47.4 0.8 copy.31
  48.3 0.8 copy.30
  49.9 0.8 copy.34
  50.8 0.8 copy.33
  53.0 1.5 %reduce.1 = s32[79,128]{1,0:T(8,128)} reduce(s32[1,79,128]{2,0,1:T(1,128)} %param.18, s32[]{:T(128)} %constant.49.clone.1), dimensions={0}, to_apply=%param.18.reduce_sub_computation | reduce | bytes 80900 | tf_op args[5]
  54.5 1.5 %reduce = s32[79,128]{1,0:T(8,128)} reduce(s32[1,79,128]{2,0,1:T(1,128)} %param.17, s32[]{:T(128)} %constant.49.clone.1), dimensions={0}, to_apply=%param.17.reduce_sub_computation | reduce | bytes 80900 | tf_op args[4]
  56.0 1.3 %dynamic-slice = u32[1]{0:T(128)} dynamic-slice(u32[256]{0:T(256)} %constant.64, u32[]{:T(128)S(6)} %add.27), dynamic_slice_sizes={1} | dynamic-slice | bytes 12
  58.6 0.8 fusion.70
  59.3 1.4 %fusion.71 = f32[79,2,128]{2,1,0:T(2,128)} fusion(bf16[79,2,128]{2,1,0:T(2,128)(2,1)S(1)} %reshape.124, bf16[79,128,128]{2,1,0:T(8,128)(2,1)S(1)} %copy-done), kind=kOutput, calls=%fused_computation.90 | convolution fusion | flops 5177344 | bytes 2710016 | tf_op jit(solution)/shard_map/while/body/eval_jaxpr/obr,ors->obs/dot_general | solution.py:42
  60.8 1.6 %reshape.125 = f32[158,128]{1,0:T(8,128)} reshape(f32[79,2,128]{2,1,0:T(2,128)} %fusion.71) | data formatting | bytes 161792 | tf_op jit(solution)/shard_map/while/body/eval_jaxpr/reshape | solution.py:51
  62.3 1.8 %fusion.15 = f32[32,128]{1,0:T(8,128)S(1)} fusion(f32[1264,128]{1,0:T(8,128)S(1)} %bitcast.59, s32[1264]{0:T(1024)} %eq.149, pred[1264]{0:T(1024)(128)(4,1)S(1)} %lt.99), kind=kOutput, calls=%fused_computation.19 | convolution fusion | flops 62249472 | bytes 669872 | tf_op jit(solution)/shard_map/while/body/eval_jaxpr/kt,kc->tc/dot_general | solution.py:48
  64.2 1.2 fusion.28
  65.4 12.2 %all-reduce.2 = (bf16[4,128]{1,0:T(4,128)(2,1)S(1)}, f32[32,128]{1,0:T(8,128)S(1)}) all-reduce(f32[4,128]{1,0:T(4,128)S(1)} %fusion.28, f32[32,128]{1,0:T(8,128)S(1)} %fusion.15), channel_id=5, replica_groups=mesh['morton'=64,'sub'=4] {'sub'}, use_global_device_ids=true, to_apply=%region_2.3.clone | all-reduce | flops 4608 | bytes 35840
  77.6 0.8 fusion.60
  78.4 7.4 %fusion.2 = bf16[10112,128]{1,0:T(8,128)(2,1)S(1)} fusion(s32[10112]{0:T(1024)} %bitcast.63, bf16[256,128]{1,0:T(8,128)(2,1)} %collective-permute-done.1, bf16[256,128]{1,0:T(8,128)(2,1)} %all_gather.9, bf16[256,128]{1,0:T(8,128)(2,1)} %collective-permute-done), kind=kOutput, calls=%fused_computation.3 | convolution fusion | flops 1997750272 | bytes 2825728 | tf_op jit(solution)/shard_map/while/body/eval_jaxpr/dot_general | solution.py:38
  85.8 0.8 fusion.69
  86.6 11.6 %fusion.8 = bf16[256,128]{1,0:T(8,128)(2,1)} fusion(f32[10112,128]{1,0:T(8,128)S(1)} %bitcast.57, s32[10112]{0:T(1024)S(1)} %bitcast.62, pred[10112]{0:T(1024)(128)(4,1)S(1)} %fusion.43), kind=kOutput, calls=%fused_computation.11 | convolution fusion | flops 3981410304 | bytes 5293440 | tf_op jit(solution)/shard_map/while/body/eval_jaxpr/kt,kc->tc/dot_general | solution.py:48
  98.4 17.3 %reduce-scatter.2.cloned.1.call-done = bf16[64,128]{1,0:T(8,128)(2,1)} async-done(((bf16[256,128]{1,0:T(8,128)(2,1)}), bf16[64,128]{1,0:T(8,128)(2,1)}) %reduce-scatter.2.cloned.1.call-update) | async-done | bytes 16400 | tf_op jit(solution)/shard_map/reduce_scatter | solution.py:131
  115.8 1.3 %fusion.44 = bf16[64,128]{1,0:T(8,128)(2,1)} fusion(f32[8,8,128]{2,0,1:T(8,128)S(1)} %fusion.55, bf16[64,128]{1,0:T(8,128)(2,1)} %reduce-scatter.2.cloned.1.call-done), kind=kLoop, calls=%fused_computation.56 | loop fusion | flops 24576 | bytes 65536 | tf_op jit(solution)/shard_map/convert_element_type | solution.py:155
  (37 shorter events, 3.5 us)
Async XLA Ops:
  6.5 52.0 %copy-start = (bf16[79,128,128]{2,1,0:T(8,128)(2,1)S(1)}, bf16[79,128,128]{2,1,0:T(8,128)(2,1)}, u32[]{:S(2)}) copy-start(bf16[79,128,128]{2,1,0:T(8,128)(2,1)} %param.14) | copy-start | bytes 7766020
  6.5 109.2 %reduce-scatter.2.cloned.1.call-start = ((), (), s32[]{:S(2)}) async-start(), calls=%async_computation.1 | async-start | bytes 81920 | tf_op jit(solution)/shard_map/reduce_scatter | solution.py:131
  13.8 64.5 %collective-permute-start = (bf16[256,128]{1,0:T(8,128)(2,1)}, bf16[256,128]{1,0:T(8,128)(2,1)}, u32[]{:S(2)}, u32[]{:S(2)}) collective-permute-start(bf16[256,128]{1,0:T(8,128)(2,1)} %all_gather.9), channel_id=1, source_target_pairs={{0,4},{4,8},{8,12},{12,16},{16,20},{20,24},{24,28},{28,32},{32,36}... | collective-permute-start | bytes 196616 | tf_op jit(solution)/shard_map/ppermute | solution.py:18
  17.4 61.0 %collective-permute-start.1 = (bf16[256,128]{1,0:T(8,128)(2,1)}, bf16[256,128]{1,0:T(8,128)(2,1)}, u32[]{:S(2)}, u32[]{:S(2)}) collective-permute-start(bf16[256,128]{1,0:T(8,128)(2,1)} %all_gather.9), channel_id=1, source_target_pairs={{4,0},{8,4},{12,8},{16,12},{20,16},{24,20},{28,24},{32,28},{36,32}... | collective-permute-start | bytes 196616 | tf_op jit(solution)/shard_map/ppermute | solution.py:19
  38.0 2.6 %collective-permute-start.2 = (bf16[36,128]{1,0:T(8,128)(2,1)S(1)}, bf16[36,128]{1,0:T(8,128)(2,1)S(1)}, u32[]{:S(2)}, u32[]{:S(2)}) collective-permute-start(bf16[36,128]{1,0:T(8,128)(2,1)S(1)} %pad_maximum_fusion.2), channel_id=1, source_target_pairs={{0,4},{4,0},{8,12},{12,8},{16,20},{20,16},{24,28},{28,24},{32,36},... | collective-permute-start | bytes 27656 | tf_op jit(solution)/shard_map/ppermute | solution.py:8
  40.7 3.6 %collective-permute-start.3 = (bf16[72,128]{1,0:T(8,128)(2,1)S(1)}, bf16[72,128]{1,0:T(8,128)(2,1)S(1)}, u32[]{:S(2)}, u32[]{:S(2)}) collective-permute-start(bf16[72,128]{1,0:T(8,128)(2,1)S(1)} %pad_maximum_fusion.1), channel_id=1, source_target_pairs={{0,8},{4,12},{8,0},{12,4},{16,24},{20,28},{24,16},{28,20},{32,40},... | collective-permute-start | bytes 55304 | tf_op jit(solution)/shard_map/ppermute | solution.py:8
  44.4 13.5 %collective-permute-start.4 = (bf16[144,128]{1,0:T(8,128)(2,1)S(1)}, bf16[144,128]{1,0:T(8,128)(2,1)S(1)}, u32[]{:S(2)}, u32[]{:S(2)}) collective-permute-start(bf16[144,128]{1,0:T(8,128)(2,1)S(1)} %pad_maximum_fusion), channel_id=1, source_target_pairs={{0,16},{4,20},{8,24},{12,28},{16,0},{20,4},{24,8},{28,12},{32,48},... | collective-permute-start | bytes 110600 | tf_op jit(solution)/shard_map/ppermute | solution.py:8
  59.3 18.3 %copy-start.1 = (bf16[8,128,128]{2,1,0:T(8,128)(2,1)S(1)}, bf16[8,128,128]{2,1,0:T(8,128)(2,1)}, u32[]{:S(2)}) copy-start(bf16[8,128,128]{2,1,0:T(8,128)(2,1)} %param.16) | copy-start | bytes 786436
  85.8 0.9 copy-start.2
Sparse Core Ops, SparseCore 0:
  98.4 17.2 reduce-scatter.1
where the time goes:
time: 126 us; the launch traced here: 124 us
  blocking collectives  30 us (24%)
  matrix products  28.9 us (23%)
  waiting for transfers between devices  21.9 us (17%)
  between operations  14.2 us (11%)
  starting transfers between devices  13.9 us (11%)
  local copies, waits for them, and re-layouts  8.5 us (7%)
  other arithmetic  6.55 us (5%)
    reduce_scatter x1, waiting for transfers between devices, local(): lax.psum_scatter(partial_six.astype(jnp.bfloat16), 'sub', scatter_dimensi...  17.3 us
    dot_general x3, matrix products, single_rotation(): jnp.einsum('kt,kc->tc', placing, product.reshape(-1, coeff_width), precis...  14.7 us
    unnamed x1, blocking collectives  12.2 us
    dot_general x3, matrix products, single_rotation(): jnp.dot(selector, expansions, preferred_element_type=jnp.float32)  7.98 us
    ppermute x1, starting transfers between devices, with_halo(): after = lax.ppermute(leading, axis, down)  7.91 us
    all_gather x1, blocking collectives, local(): owned_rows = lax.all_gather(multipoles, 'sub', axis=0, tiled=True)  7.29 us
    all_gather x1, blocking collectives, gather_group(): lax.all_gather(pieces[0], 'sub', axis=0, tiled=True)  5.46 us
    all_gather x1, blocking collectives, gather_group(): lax.all_gather(pieces[1], 'sub', axis=0, tiled=True)  5.05 us
  transfers between devices with their start and end apart: 6, of which 3 were waited for; matrix products, arithmetic and copies ran while one was open for 18% of the time, Pallas kernels for 0%

commit v1 on v0

v1 whole, which is shorter than its diff:
```python
import jax
import jax.numpy as jnp
from jax import lax
from jax.experimental import pallas as pl
from jax.experimental.pallas import tpu as pltpu
from jax.sharding import Mesh
from jax.sharding import PartitionSpec as P

R = 128
NO = 79
G = 4
BF = jnp.bfloat16
F32 = jnp.float32


def iota(shape, dim):
    return lax.broadcasted_iota(jnp.int32, shape, dim)


def prep_kernel(q_ref, m_ref, up_ref, src_ref, c6_ref, a5_ref, c5_ref, a4_ref, c4_ref, t5_ref, t4_ref,
                grp_ref, low6_ref, hi6_ref, low54_ref, hi54_ref, t54_ref, sq_ref, st_ref):
    q = q_ref[0]
    st_ref[pl.ds(0, 64), :] = m_ref[...].astype(F32)
    c5 = jnp.zeros((8, R), F32)
    for c in range(8):
        rows = st_ref[pl.ds(c, 8, stride=8), :].astype(BF)
        c5 = c5 + jnp.dot(rows, up_ref[c], preferred_element_type=F32)
    c5r = c5.astype(BF).astype(F32)
    c4 = jnp.zeros((8, R), F32)
    for c in range(8):
        rows = jnp.broadcast_to(c5r[c : c + 1, :], (8, R)).astype(BF)
        c4 = c4 + jnp.dot(rows, up_ref[c], preferred_element_type=F32)
    both = jnp.concatenate([c5, c4], axis=0).astype(BF)
    grp_ref[...] = jnp.broadcast_to(both[None], (32, 16, R))

    def flipped(x):
        sq_ref[...] = jnp.zeros((R, R), F32)
        sq_ref[0:NO, 0 : x.shape[1]] = x.astype(F32)
        return sq_ref[...].T

    def live(c_ref, rows):
        sq_ref[0:1, :] = jnp.zeros((1, R), F32)
        sq_ref[0:1, 0:NO] = c_ref[...].astype(F32)
        counts = jnp.broadcast_to(sq_ref[0:1, :], (rows, R))
        return iota((rows, R), 0).astype(F32) < counts

    src = src_ref[...]
    low = flipped(jnp.bitwise_xor(jnp.bitwise_and(src, 255), q * 64))
    hi = flipped(jnp.right_shift(src, 8))
    low6_ref[...] = jnp.where(live(c6_ref, R), low, -1.0)
    hi6_ref[...] = hi
    a5 = a5_ref[...]
    code5 = flipped(16 * jnp.right_shift(a5, 3) + jnp.bitwise_and(a5, 7))[0:16]
    code5 = jnp.where(live(c5_ref, 16), code5, -1.0)
    code4 = flipped(16 * a4_ref[...] + 8)[0:16]
    code4 = jnp.where(live(c4_ref, 16), code4, -1.0)
    code = jnp.concatenate([code5, code4], axis=0)
    upper = code >= 256.0
    low54_ref[...] = jnp.where(upper, code - 256.0, code)
    hi54_ref[...] = upper.astype(F32)
    sq_ref[...] = jnp.full((R, R), -1.0, F32)
    sq_ref[0:NO, 0:16] = t5_ref[...].astype(F32)
    sq_ref[0:NO, 16:18] = t4_ref[...].astype(F32) + 32.0
    packed = sq_ref[pl.ds(0, 24, stride=4), :]
    lane = iota((24, R), 1)
    for i in range(1, G):
        part = pltpu.roll(sq_ref[pl.ds(i, 24, stride=4), :], 32 * i, 1)
        packed = jnp.where(lane >= 32 * i, part, packed)
    t54_ref[...] = packed


def main_kernel(q_ref, own_ref, prev_ref, next_ref, grp_ref, t_ref, low6_ref, hi6_ref, low54_ref, hi54_ref,
                tgt_ref, t54_ref, o0_ref, o1_ref, o2_ref, o3_ref, x_ref, x54_ref, acc_ref, acc54_ref, tf_ref):
    x_ref[:, 0:R] = prev_ref[...]
    x_ref[:, R : 2 * R] = own_ref[...]
    x_ref[:, 2 * R : 3 * R] = next_ref[...]
    x54_ref[:, 0:R] = grp_ref[0:16].reshape(256, R)
    x54_ref[:, R : 2 * R] = grp_ref[16:32].reshape(256, R)
    acc_ref[...] = jnp.zeros_like(acc_ref)
    acc54_ref[...] = jnp.zeros_like(acc54_ref)
    tf_ref[0:NO, :] = tgt_ref[...].astype(F32)

    def hot(column, rows):
        wide = jnp.broadcast_to(column, (rows, R)).astype(BF)
        lane = iota((rows, R), 1).astype(BF)
        one = jnp.ones((rows, R), BF)
        zero = jnp.zeros((rows, R), BF)
        left = jnp.where(wide == lane, one, zero)
        right = jnp.where(wide == lane + jnp.asarray(128, BF), one, zero)
        return jnp.concatenate([left, right], axis=1)

    def placing(row, rows, base):
        wide = jnp.broadcast_to(row, (rows, R)).astype(BF)
        down = (iota((rows, R), 0) + base).astype(BF)
        return jnp.where(wide == down, jnp.ones((rows, R), BF), jnp.zeros((rows, R), BF))

    def group(g, count):
        first = g * G
        shift = lax.rem(R - first, R)
        low6 = pltpu.roll(low6_ref[...], shift, 1)
        hi6 = pltpu.roll(hi6_ref[...], shift, 1)
        low54 = pltpu.roll(low54_ref[...], shift, 1)
        hi54 = pltpu.roll(hi54_ref[...], shift, 1)
        ys, y54s, places = [], [], []
        for i in range(count):
            picked = jnp.dot(hot(low6[:, i : i + 1], R), x_ref[...], preferred_element_type=F32)
            seg = jnp.broadcast_to(hi6[:, i : i + 1], (R, R))
            picked = jnp.where(seg == 0.0, picked[:, 0:R], jnp.where(seg == 1.0, picked[:, R : 2 * R], picked[:, 2 * R :]))
            few = jnp.dot(hot(low54[:, i : i + 1], 32), x54_ref[...], preferred_element_type=F32)
            seg = jnp.broadcast_to(hi54[:, i : i + 1], (32, R))
            few = jnp.where(seg == 0.0, few[:, 0:R], few[:, R:])
            rows = jnp.concatenate([picked.astype(BF), few.astype(BF)], axis=0)
            y = jnp.dot(rows, t_ref[first + i], preferred_element_type=F32).astype(BF)
            ys.append(y[0:R])
            y54s.append(y[R:])
            places.append(placing(tf_ref[pl.ds(first + i, 1), :], 256, 0))
        acc_ref[...] += jnp.dot(jnp.concatenate(places, axis=1), jnp.concatenate(ys, axis=0), preferred_element_type=F32)
        if count < G:
            y54s.append(jnp.zeros((32 * (G - count), R), BF))
        acc54_ref[...] += jnp.dot(placing(t54_ref[pl.ds(g, 1), :], 48, 0), jnp.concatenate(y54s, axis=0), preferred_element_type=F32)

    def body(g, carry):
        group(g, G)
        return carry

    lax.fori_loop(0, NO // G, body, 0)
    group(NO // G, NO % G)
    q = q_ref[0]
    acc54_ref[0:32] = acc54_ref[0:32] * 0.5
    acc54_ref[32:48] = acc54_ref[32:48] * 0.25
    for k, out in enumerate((o0_ref, o1_ref, o2_ref, o3_ref)):
        d = jnp.bitwise_xor(q, k)
        out[0:64] = acc_ref[pl.ds(64 * d, 64), :].astype(BF)
        five = acc54_ref[pl.ds(8 * d, 8), :]
        four = jnp.broadcast_to(acc54_ref[pl.ds(32 + d, 1), :], (8, R))
        small = jnp.concatenate([five, four], axis=0)
        top = small.astype(BF)
        out[64:80] = top
        out[80:96] = (small - top.astype(F32)).astype(BF)


def final_kernel(a_ref, b_ref, c_ref, d_ref, dn_ref, out_ref, s_ref):
    total = (a_ref[...].astype(F32) + b_ref[...].astype(F32)) + (c_ref[...].astype(F32) + d_ref[...].astype(F32))
    small = total[64:80] + total[80:96]
    far5 = small[0:8]
    local4 = small[8:16].astype(BF)
    row = iota((8, R), 0)
    local5 = far5
    for c in range(8):
        spread = jnp.dot(local4, dn_ref[c], preferred_element_type=F32)
        local5 = local5 + jnp.where(row == c, spread, 0.0)
    local5 = local5.astype(BF)
    for c in range(8):
        s_ref[pl.ds(c, 8, stride=8), :] = jnp.dot(local5, dn_ref[c], preferred_element_type=F32)
    out_ref[...] = (total[0:64] + s_ref[...]).astype(BF)


VM = pl.BlockSpec(memory_space=pltpu.VMEM)
SM = pl.BlockSpec(memory_space=pltpu.SMEM)


def shape(dims, kind=F32):
    return jax.ShapeDtypeStruct(dims, kind)


def run_prep(q, *args):
    return pl.pallas_call(
        prep_kernel,
        out_shape=(shape((32, 16, R), BF), shape((R, R)), shape((R, R)), shape((32, R)), shape((32, R)), shape((24, R))),
        in_specs=[SM] + [VM] * len(args),
        out_specs=tuple([VM] * 6),
        scratch_shapes=[pltpu.VMEM((R, R), F32), pltpu.VMEM((64, R), F32)],
        name="prep",
    )(q, *args)


def run_main(q, *args):
    return pl.pallas_call(
        main_kernel,
        out_shape=tuple([shape((96, R), BF)] * 4),
        in_specs=[SM] + [VM] * len(args),
        out_specs=tuple([VM] * 4),
        scratch_shapes=[
            pltpu.VMEM((256, 3 * R), BF),
            pltpu.VMEM((256, 2 * R), BF),
            pltpu.VMEM((256, R), F32),
            pltpu.VMEM((48, R), F32),
            pltpu.VMEM((80, R), F32),
        ],
        name="translate",
    )(q, *args)


def run_final(*args):
    return pl.pallas_call(
        final_kernel,
        out_shape=shape((64, R), BF),
        in_specs=[VM] * len(args),
        out_specs=VM,
        scratch_shapes=[pltpu.VMEM((64, R), F32)],
        name="downward",
    )(*args)


SUB = ("x", "c")
MORTON = ("g", "z")


def crossed(value, k):
    return lax.ppermute(value, SUB, [(i, i ^ k) for i in range(4)])


def local(multipoles, translations, upward_ops, downward_ops, targets_l6, source_boxes_level6, counts_l6,
          target_boxes_level5, anchors_l5, counts_l5, targets_l4, anchors_l4, counts_l4):
    q = lax.axis_index(SUB).astype(jnp.int32).reshape(1)
    peers = [crossed(multipoles, k) for k in (1, 2, 3)]
    spread, low6, hi6, low54, hi54, t54 = run_prep(
        q, multipoles, upward_ops, source_boxes_level6[0], counts_l6, anchors_l5[0], counts_l5, anchors_l4[0], counts_l4,
        target_boxes_level5[0], targets_l4[0])
    own = jnp.concatenate([multipoles] + peers, axis=0)
    n = lax.axis_size(MORTON)
    before = lax.ppermute(own, MORTON, [(i, i + 1) for i in range(n - 1)])
    after = lax.ppermute(own, MORTON, [(i + 1, i) for i in range(n - 1)])
    coarse = lax.all_to_all(spread, ("z",) + SUB, 0, 0)
    parts = run_main(q, own, before, after, coarse, translations, low6, hi6, low54, hi54, targets_l6[0], t54)
    received = [crossed(parts[k], k) for k in (1, 2, 3)]
    return run_final(parts[0], *received, downward_ops)


def solution(mesh):
    cut = Mesh(mesh.devices.reshape(8, 8, 2, 2), ("g", "z", "x", "c"))
    both = MORTON + SUB
    placed = (
        P(both, None),
        P(SUB, None, None),
        P(),
        P(),
        P(MORTON, SUB, None),
        P(MORTON, SUB, None),
        P(MORTON, SUB),
        P(MORTON, SUB, None),
        P(MORTON, SUB, None),
        P(MORTON, SUB),
        P(MORTON, SUB, None),
        P(MORTON, SUB, None),
        P(MORTON, SUB),
    )
    return jax.shard_map(local, mesh=cut, in_specs=placed, out_specs=P(both, None), check_vma=False)
```

time: 126 us -> 68 us (0.54); the launches traced: 124 us -> 67.4 us
  blocking collectives: 30 us -> 0 us
  matrix products: 28.9 us -> 0 us
  Pallas kernels: 0 us -> 28.8 us
  waiting for transfers between devices: 21.9 us -> 3.27 us
  between operations: 14.2 us -> 0.11 us
  starting transfers between devices: 13.9 us -> 24.9 us
  other arithmetic: 6.55 us -> 0 us
  local copies, waits for them, and re-layouts: 8.5 us -> 10.4 us
    dot_general x13 -> x0, matrix products: 28.9 us -> none  [the longest x3 14.7 us: single_rotation(): jnp.einsum('kt,kc->tc', placing, product.reshape(-1, coeff_width), precis...]
    pallas_call x0 -> x3, Pallas kernels: none -> 28.8 us  [the longest x1 24.6 us: run_main(): pl.pallas_call(main_kernel, out_shape=tuple([shape((96, R), BF)] * 4), in...]
    all_gather x3 -> x0, blocking collectives: 17.8 us -> none  [the longest x1 7.29 us: local(): owned_rows = lax.all_gather(multipoles, 'sub', axis=0, tiled=True)]
    reduce_scatter x1 -> x0, waiting for transfers between devices: 17.3 us -> none  [local(): lax.psum_scatter(partial_six.astype(jnp.bfloat16), 'sub', scatter_dimensi...]
    unnamed x1 -> x0, blocking collectives: 12.2 us -> none
    all_to_all x0 -> x1, starting transfers between devices: none -> 9.78 us  [local(): coarse = lax.all_to_all(spread, ('z',) + SUB, 0, 0)]
    unnamed x12 -> x23, local copies, waits for them, and re-layouts: 4.48 us -> 10.4 us
    unnamed x2 -> x0, other arithmetic: 2.96 us -> none
  transfers between devices with their start and end apart: 6 -> 9, of which waited for: 3 -> 2; matrix products, arithmetic and copies ran while one was open for 18% -> 13% of each run, Pallas kernels for 0% -> 3%
where the time goes in v1:
time: 68 us; the launch traced here: 67.4 us
  Pallas kernels  28.8 us (42%)
  starting transfers between devices  24.9 us (37%)
  local copies, waits for them, and re-layouts  10.4 us (15%)
  waiting for transfers between devices  3.27 us (5%)
    pallas_call x1, Pallas kernels, run_main(): pl.pallas_call(main_kernel, out_shape=tuple([shape((96, R), BF)] * 4), in...  24.6 us
    unnamed x23, local copies, waits for them, and re-layouts  10.4 us
    all_to_all x1, starting transfers between devices, local(): coarse = lax.all_to_all(spread, ('z',) + SUB, 0, 0)  9.78 us
    ppermute x1, starting transfers between devices, local(): after = lax.ppermute(own, MORTON, [(i + 1, i) for i in range(n - 1)])  6.53 us
    ppermute x6, starting transfers between devices, crossed(): return lax.ppermute(value, SUB, [(i, i ^ k) for i in range(4)])  5.29 us
    ppermute x6, waiting for transfers between devices, crossed(): return lax.ppermute(value, SUB, [(i, i ^ k) for i in range(4)])  3.27 us
    ppermute x1, starting transfers between devices, local(): before = lax.ppermute(own, MORTON, [(i, i + 1) for i in range(n - 1)])  3.26 us
    pallas_call x1, Pallas kernels, run_prep(): pl.pallas_call(prep_kernel, out_shape=(shape((32, 16, R), BF), shape((R,...  2.19 us
  transfers between devices with their start and end apart: 9, of which 2 were waited for; matrix products, arithmetic and copies ran while one was open for 13% of the time, Pallas kernels for 3%

profile of v1, /device:TPU:9, one launch (start us, length us, event | category | flops | bytes accessed | tf_op | source)
XLA Modules:
  0.0 67.4 jit_solution(8672821350940153115)
XLA Ops:
  0.0 0.7 %collective-permute-start = (bf16[64,128]{1,0:T(8,128)(2,1)}, bf16[64,128]{1,0:T(8,128)(2,1)S(1)}, u32[]{:S(2)}, u32[]{:S(2)}) collective-permute-start(bf16[64,128]{1,0:T(8,128)(2,1)} %m_ref.1), channel_id=1, source_target_pairs={{0,1},{1,0},{2,3},{3,2},{4,5},{5,4},{6,7},{7,6},{8,9},{9,8},{10,11... | collective-permute-start | bytes 49160 | tf_op jit(solution)/shard_map/ppermute | solution.py:210
  0.7 1.2 %collective-permute-start.1 = (bf16[64,128]{1,0:T(8,128)(2,1)}, bf16[64,128]{1,0:T(8,128)(2,1)S(1)}, u32[]{:S(2)}, u32[]{:S(2)}) collective-permute-start(bf16[64,128]{1,0:T(8,128)(2,1)} %m_ref.1), channel_id=1, source_target_pairs={{0,2},{1,3},{2,0},{3,1},{4,6},{5,7},{6,4},{7,5},{8,10},{9,11},{10,... | collective-permute-start | bytes 49160 | tf_op jit(solution)/shard_map/ppermute | solution.py:210
  1.9 0.4 collective-permute-start.2
  2.3 1.4 %copy.14 = s32[1,79,16]{2,1,0:T(8,128)} copy(s32[1,79,16]{1,2,0:T(8,128)} %param.21) | data formatting | bytes 10112 | tf_op args[8]
  3.7 1.4 %copy.23 = s32[1,79,128]{2,1,0:T(8,128)} copy(s32[1,79,128]{2,0,1:T(1,128)} %param.18) | data formatting | bytes 80896
  5.1 1.4 %copy.15 = s32[1,79,2]{2,1,0:T(8,128)} copy(s32[1,79,2]{1,2,0:T(2,128)} %param.24) | data formatting | bytes 1264 | tf_op args[11]
  6.5 1.4 %copy.16 = s32[1,79,16]{2,1,0:T(8,128)} copy(s32[1,79,16]{1,2,0:T(8,128)} %param.20) | data formatting | bytes 10112 | tf_op args[7]
  7.9 1.4 %copy.17 = s32[1,79,2]{2,1,0:T(8,128)} copy(s32[1,79,2]{1,2,0:T(2,128)} %param.23) | data formatting | bytes 1264 | tf_op args[10]
  9.3 2.2 %prep.1 = (bf16[32,16,128]{2,1,0:T(8,128)(2,1)}, f32[128,128]{1,0:T(8,128)}, f32[128,128]{1,0:T(8,128)}, f32[32,128]{1,0:T(8,128)}, f32[32,128]{1,0:T(8,128)}, /*index=5*/f32[24,128]{1,0:T(8,128)}) custom-call(s32[1]{0:T(128)} %bitcast.q_ref, bf16[64,128]{1,0:T(8,128)(2,1)} %m_ref.1, bf16[8,128,128]{2,1,0:T(8,128)(2,1)} %up_ref.1, s32[79,128]{1,0:T(8,128)} %bitcast.12, ...), custom_call_target="tpu_custom_call" | custom-call | tf_op jit(solution)/shard_map/prep/pallas_call | solution.py:167
  11.5 9.8 %all-to-all-start = ((bf16[32,16,128]{2,1,0:T(8,128)(2,1)}), bf16[32,16,128]{2,1,0:T(8,128)(2,1)S(1)}, u32[]{:S(2)}, u32[]{:S(2)}) async-start(bf16[32,16,128]{2,1,0:T(8,128)(2,1)} %get-tuple-element.15), calls=%async_computation | async-start | bytes 262144 | tf_op jit(solution)/shard_map/all_to_all | solution.py:224
  21.2 0.7 %constant_dynamic-update-slice_fusion.3 = bf16[256,128]{1,0:T(8,128)(2,1)S(1)} fusion(bf16[64,128]{1,0:T(8,128)(2,1)} %m_ref.1), kind=kLoop, calls=%fused_computation.5 | loop fusion | bytes 32768
  22.0 0.0 collective-permute-done
  22.0 0.0 collective-permute-done.1
  22.0 0.0 collective-permute-done.2
  22.0 3.3 %collective-permute-start.3 = (bf16[256,128]{1,0:T(8,128)(2,1)S(1)}, bf16[256,128]{1,0:T(8,128)(2,1)S(1)}, u32[]{:S(2)}, u32[]{:S(2)}) collective-permute-start(bf16[256,128]{1,0:T(8,128)(2,1)S(1)} %constant_dynamic-update-slice_fusion.own_ref), channel_id=1, source_target_pairs={{0,4},{4,8},{8,12},{12,16},{16,20},{20,24},{24,28},{28,32},{32,36}... | collective-permute-start | bytes 196616 | tf_op jit(solution)/shard_map/ppermute | solution.py:222
  25.3 6.5 %collective-permute-start.4 = (bf16[256,128]{1,0:T(8,128)(2,1)S(1)}, bf16[256,128]{1,0:T(8,128)(2,1)S(1)}, u32[]{:S(2)}, u32[]{:S(2)}) collective-permute-start(bf16[256,128]{1,0:T(8,128)(2,1)S(1)} %constant_dynamic-update-slice_fusion.own_ref), channel_id=1, source_target_pairs={{4,0},{8,4},{12,8},{16,12},{20,16},{24,20},{28,24},{32,28},{36,32}... | collective-permute-start | bytes 196616 | tf_op jit(solution)/shard_map/ppermute | solution.py:223
  31.8 1.4 %copy.22 = s32[1,79,128]{2,1,0:T(8,128)} copy(s32[1,79,128]{2,0,1:T(1,128)} %param.17) | data formatting | bytes 80896
  33.2 0.0 collective-permute-done.3.prev_ref
  33.2 0.0 collective-permute-done.4.next_ref
  33.3 0.0 all-to-all-done.grp_ref
  33.3 0.6 copy-done.2
  33.9 0.0 copy-done.3
  33.9 0.1 copy-done
  34.0 24.6 %translate.1 = (bf16[96,128]{1,0:T(8,128)(2,1)}, bf16[96,128]{1,0:T(8,128)(2,1)}, bf16[96,128]{1,0:T(8,128)(2,1)}, bf16[96,128]{1,0:T(8,128)(2,1)}) custom-call(s32[1]{0:T(128)} %bitcast.q_ref, bf16[256,128]{1,0:T(8,128)(2,1)} %copy-done.1, bf16[256,128]{1,0:T(8,128)(2,1)} %copy-done.2, bf16[256,128]{1,0:T(8,128)(2,1)} %copy-done.3, ...), custom_call_target="tpu_custom_call" | custom-call | tf_op jit(solution)/shard_map/translate/pallas_call | solution.py:178
  58.6 1.3 %collective-permute-start.5 = (bf16[96,128]{1,0:T(8,128)(2,1)}, bf16[96,128]{1,0:T(8,128)(2,1)S(1)}, u32[]{:S(2)}, u32[]{:S(2)}) collective-permute-start(bf16[96,128]{1,0:T(8,128)(2,1)} %get-tuple-element.22), channel_id=1, source_target_pairs={{0,1},{1,0},{2,3},{3,2},{4,5},{5,4},{6,7},{7,6},{8,9},{9,8},{10,11... | collective-permute-start | bytes 73736 | tf_op jit(solution)/shard_map/ppermute | solution.py:210
  59.8 1.5 %collective-permute-start.6 = (bf16[96,128]{1,0:T(8,128)(2,1)}, bf16[96,128]{1,0:T(8,128)(2,1)S(1)}, u32[]{:S(2)}, u32[]{:S(2)}) collective-permute-start(bf16[96,128]{1,0:T(8,128)(2,1)} %get-tuple-element.23), channel_id=1, source_target_pairs={{0,2},{1,3},{2,0},{3,1},{4,6},{5,7},{6,4},{7,5},{8,10},{9,11},{10,... | collective-permute-start | bytes 73736 | tf_op jit(solution)/shard_map/ppermute | solution.py:210
  61.3 0.2 collective-permute-start.7
  61.5 0.0 collective-permute-done.5.b_ref
  61.5 1.2 %collective-permute-done.6.c_ref = bf16[96,128]{1,0:T(8,128)(2,1)S(1)} collective-permute-done((bf16[96,128]{1,0:T(8,128)(2,1)}, bf16[96,128]{1,0:T(8,128)(2,1)S(1)}, u32[]{:S(2)}, u32[]{:S(2)}) %collective-permute-start.6) | collective-permute-done | bytes 24608 | tf_op jit(solution)/shard_map/ppermute | solution.py:210
  62.8 2.0 %collective-permute-done.7.d_ref = bf16[96,128]{1,0:T(8,128)(2,1)S(1)} collective-permute-done((bf16[96,128]{1,0:T(8,128)(2,1)}, bf16[96,128]{1,0:T(8,128)(2,1)S(1)}, u32[]{:S(2)}, u32[]{:S(2)}) %collective-permute-start.7) | collective-permute-done | bytes 24608 | tf_op jit(solution)/shard_map/ppermute | solution.py:210
  64.8 0.6 copy-done.6
  65.4 2.0 %downward.1 = bf16[64,128]{1,0:T(8,128)(2,1)} custom-call(bf16[96,128]{1,0:T(8,128)(2,1)} %get-tuple-element.21.a_ref, bf16[96,128]{1,0:T(8,128)(2,1)} %copy-done.4, bf16[96,128]{1,0:T(8,128)(2,1)} %copy-done.5, bf16[96,128]{1,0:T(8,128)(2,1)} %copy-done.6, bf16[8,128,128]{2,1,0:T(8,128)(2,1)} %dn_ref.1), custom_call_target="tpu_custom_call" | custom-call | tf_op jit(solution)/shard_map/downward/pallas_call | solution.py:195
  (13 shorter events, 0.0 us)
Async XLA Ops:
  0.0 22.0 %collective-permute-start = (bf16[64,128]{1,0:T(8,128)(2,1)}, bf16[64,128]{1,0:T(8,128)(2,1)S(1)}, u32[]{:S(2)}, u32[]{:S(2)}) collective-permute-start(bf16[64,128]{1,0:T(8,128)(2,1)} %m_ref.1), channel_id=1, source_target_pairs={{0,1},{1,0},{2,3},{3,2},{4,5},{5,4},{6,7},{7,6},{8,9},{9,8},{10,11... | collective-permute-start | bytes 49160 | tf_op jit(solution)/shard_map/ppermute | solution.py:210
  0.7 21.3 %collective-permute-start.1 = (bf16[64,128]{1,0:T(8,128)(2,1)}, bf16[64,128]{1,0:T(8,128)(2,1)S(1)}, u32[]{:S(2)}, u32[]{:S(2)}) collective-permute-start(bf16[64,128]{1,0:T(8,128)(2,1)} %m_ref.1), channel_id=1, source_target_pairs={{0,2},{1,3},{2,0},{3,1},{4,6},{5,7},{6,4},{7,5},{8,10},{9,11},{10,... | collective-permute-start | bytes 49160 | tf_op jit(solution)/shard_map/ppermute | solution.py:210
  1.9 20.1 %collective-permute-start.2 = (bf16[64,128]{1,0:T(8,128)(2,1)}, bf16[64,128]{1,0:T(8,128)(2,1)S(1)}, u32[]{:S(2)}, u32[]{:S(2)}) collective-permute-start(bf16[64,128]{1,0:T(8,128)(2,1)} %m_ref.1), channel_id=1, source_target_pairs={{0,3},{1,2},{2,1},{3,0},{4,7},{5,6},{6,5},{7,4},{8,11},{9,10},{10,... | collective-permute-start | bytes 49160 | tf_op jit(solution)/shard_map/ppermute | solution.py:210
  11.5 21.8 %all-to-all-start = ((bf16[32,16,128]{2,1,0:T(8,128)(2,1)}), bf16[32,16,128]{2,1,0:T(8,128)(2,1)S(1)}, u32[]{:S(2)}, u32[]{:S(2)}) async-start(bf16[32,16,128]{2,1,0:T(8,128)(2,1)} %get-tuple-element.15), calls=%async_computation | async-start | bytes 262144 | tf_op jit(solution)/shard_map/all_to_all | solution.py:224
  22.0 11.3 %copy-start.1 = (bf16[256,128]{1,0:T(8,128)(2,1)}, bf16[256,128]{1,0:T(8,128)(2,1)S(1)}, u32[]{:S(2)}) copy-start(bf16[256,128]{1,0:T(8,128)(2,1)S(1)} %constant_dynamic-update-slice_fusion.own_ref) | copy-start | bytes 196612
  22.0 11.2 %collective-permute-start.3 = (bf16[256,128]{1,0:T(8,128)(2,1)S(1)}, bf16[256,128]{1,0:T(8,128)(2,1)S(1)}, u32[]{:S(2)}, u32[]{:S(2)}) collective-permute-start(bf16[256,128]{1,0:T(8,128)(2,1)S(1)} %constant_dynamic-update-slice_fusion.own_ref), channel_id=1, source_target_pairs={{0,4},{4,8},{8,12},{12,16},{16,20},{20,24},{24,28},{28,32},{32,36}... | collective-permute-start | bytes 196616 | tf_op jit(solution)/shard_map/ppermute | solution.py:222
  25.3 7.9 %collective-permute-start.4 = (bf16[256,128]{1,0:T(8,128)(2,1)S(1)}, bf16[256,128]{1,0:T(8,128)(2,1)S(1)}, u32[]{:S(2)}, u32[]{:S(2)}) collective-permute-start(bf16[256,128]{1,0:T(8,128)(2,1)S(1)} %constant_dynamic-update-slice_fusion.own_ref), channel_id=1, source_target_pairs={{4,0},{8,4},{12,8},{16,12},{20,16},{24,20},{28,24},{32,28},{36,32}... | collective-permute-start | bytes 196616 | tf_op jit(solution)/shard_map/ppermute | solution.py:223
  33.2 0.6 copy-start.2
  33.2 0.6 copy-start.3
  33.3 0.7 %copy-start = (bf16[32,16,128]{2,1,0:T(8,128)(2,1)}, bf16[32,16,128]{2,1,0:T(8,128)(2,1)S(1)}, u32[]{:S(2)}) copy-start(bf16[32,16,128]{2,1,0:T(8,128)(2,1)S(1)} %all-to-all-done.grp_ref) | copy-start | bytes 393220
  58.6 3.0 %collective-permute-start.5 = (bf16[96,128]{1,0:T(8,128)(2,1)}, bf16[96,128]{1,0:T(8,128)(2,1)S(1)}, u32[]{:S(2)}, u32[]{:S(2)}) collective-permute-start(bf16[96,128]{1,0:T(8,128)(2,1)} %get-tuple-element.22), channel_id=1, source_target_pairs={{0,1},{1,0},{2,3},{3,2},{4,5},{5,4},{6,7},{7,6},{8,9},{9,8},{10,11... | collective-permute-start | bytes 73736 | tf_op jit(solution)/shard_map/ppermute | solution.py:210
  59.8 2.9 %collective-permute-start.6 = (bf16[96,128]{1,0:T(8,128)(2,1)}, bf16[96,128]{1,0:T(8,128)(2,1)S(1)}, u32[]{:S(2)}, u32[]{:S(2)}) collective-permute-start(bf16[96,128]{1,0:T(8,128)(2,1)} %get-tuple-element.23), channel_id=1, source_target_pairs={{0,2},{1,3},{2,0},{3,1},{4,6},{5,7},{6,4},{7,5},{8,10},{9,11},{10,... | collective-permute-start | bytes 73736 | tf_op jit(solution)/shard_map/ppermute | solution.py:210
  61.3 3.5 %collective-permute-start.7 = (bf16[96,128]{1,0:T(8,128)(2,1)}, bf16[96,128]{1,0:T(8,128)(2,1)S(1)}, u32[]{:S(2)}, u32[]{:S(2)}) collective-permute-start(bf16[96,128]{1,0:T(8,128)(2,1)} %get-tuple-element.24), channel_id=1, source_target_pairs={{0,3},{1,2},{2,1},{3,0},{4,7},{5,6},{6,5},{7,4},{8,11},{9,10},{10,... | collective-permute-start | bytes 73736 | tf_op jit(solution)/shard_map/ppermute | solution.py:210
  61.5 3.3 %copy-start.4 = (bf16[96,128]{1,0:T(8,128)(2,1)}, bf16[96,128]{1,0:T(8,128)(2,1)S(1)}, u32[]{:S(2)}) copy-start(bf16[96,128]{1,0:T(8,128)(2,1)S(1)} %collective-permute-done.5.b_ref) | copy-start | bytes 73732
  62.8 2.0 %copy-start.5 = (bf16[96,128]{1,0:T(8,128)(2,1)}, bf16[96,128]{1,0:T(8,128)(2,1)S(1)}, u32[]{:S(2)}) copy-start(bf16[96,128]{1,0:T(8,128)(2,1)S(1)} %collective-permute-done.6.c_ref) | copy-start | bytes 73732
  64.8 0.6 copy-start.6

commit v2 on v1

--- a/solution.py
+++ b/solution.py
@@ -8,7 +8,7 @@
 
 R = 128
 NO = 79
-G = 4
+G = 40
 BF = jnp.bfloat16
 F32 = jnp.float32
 
@@ -33,10 +33,9 @@
     both = jnp.concatenate([c5, c4], axis=0).astype(BF)
     grp_ref[...] = jnp.broadcast_to(both[None], (32, 16, R))
 
-    def flipped(x):
-        sq_ref[...] = jnp.zeros((R, R), F32)
-        sq_ref[0:NO, 0 : x.shape[1]] = x.astype(F32)
-        return sq_ref[...].T
+    sq_ref[...] = jnp.zeros((R, R), F32)
+    sq_ref[0:NO, :] = src_ref[...].reshape(NO, R).astype(F32)
+    src = sq_ref[...].T.astype(jnp.int32)
 
     def live(c_ref, rows):
         sq_ref[0:1, :] = jnp.zeros((1, R), F32)
@@ -44,26 +43,27 @@
         counts = jnp.broadcast_to(sq_ref[0:1, :], (rows, R))
         return iota((rows, R), 0).astype(F32) < counts
 
-    src = src_ref[...]
-    low = flipped(jnp.bitwise_xor(jnp.bitwise_and(src, 255), q * 64))
-    hi = flipped(jnp.right_shift(src, 8))
-    low6_ref[...] = jnp.where(live(c6_ref, R), low, -1.0)
-    hi6_ref[...] = hi
+    low = jnp.bitwise_xor(jnp.bitwise_and(src, 255), q * 64)
+    low6_ref[...] = jnp.where(live(c6_ref, R), low.astype(F32), -1.0)
+    hi6_ref[...] = jnp.right_shift(src, 8).astype(F32)
     a5 = a5_ref[...]
-    code5 = flipped(16 * jnp.right_shift(a5, 3) + jnp.bitwise_and(a5, 7))[0:16]
+    sq_ref[0:16, 0:NO] = (16 * jnp.right_shift(a5, 3) + jnp.bitwise_and(a5, 7)).astype(F32)
+    code5 = sq_ref[0:16, :]
     code5 = jnp.where(live(c5_ref, 16), code5, -1.0)
-    code4 = flipped(16 * a4_ref[...] + 8)[0:16]
+    sq_ref[0:2, 0:NO] = (16 * a4_ref[...] + 8).astype(F32)
+    code4 = sq_ref[0:16, :]
     code4 = jnp.where(live(c4_ref, 16), code4, -1.0)
     code = jnp.concatenate([code5, code4], axis=0)
     upper = code >= 256.0
     low54_ref[...] = jnp.where(upper, code - 256.0, code)
     hi54_ref[...] = upper.astype(F32)
     sq_ref[...] = jnp.full((R, R), -1.0, F32)
-    sq_ref[0:NO, 0:16] = t5_ref[...].astype(F32)
-    sq_ref[0:NO, 16:18] = t4_ref[...].astype(F32) + 32.0
+    sq_ref[0:16, 0:NO] = t5_ref[...].astype(F32)
+    sq_ref[16:18, 0:NO] = t4_ref[...].astype(F32) + 32.0
+    sq_ref[...] = sq_ref[...].T
     packed = sq_ref[pl.ds(0, 24, stride=4), :]
     lane = iota((24, R), 1)
-    for i in range(1, G):
+    for i in range(1, 4):
         part = pltpu.roll(sq_ref[pl.ds(i, 24, stride=4), :], 32 * i, 1)
         packed = jnp.where(lane >= 32 * i, part, packed)
     t54_ref[...] = packed
@@ -78,7 +78,7 @@
     x54_ref[:, R : 2 * R] = grp_ref[16:32].reshape(256, R)
     acc_ref[...] = jnp.zeros_like(acc_ref)
     acc54_ref[...] = jnp.zeros_like(acc54_ref)
-    tf_ref[0:NO, :] = tgt_ref[...].astype(F32)
+    tf_ref[0:NO, :] = tgt_ref[...].reshape(NO, R).astype(F32)
 
     def hot(column, rows):
         wide = jnp.broadcast_to(column, (rows, R)).astype(BF)
@@ -101,23 +101,29 @@
         hi6 = pltpu.roll(hi6_ref[...], shift, 1)
         low54 = pltpu.roll(low54_ref[...], shift, 1)
         hi54 = pltpu.roll(hi54_ref[...], shift, 1)
+        hots = jnp.concatenate([hot(low6[:, i : i + 1], R) for i in range(count)], axis=0)
+        picked = jnp.dot(hots, x_ref[...], preferred_element_type=F32)
+        hots = jnp.concatenate([hot(low54[:, i : i + 1], 32) for i in range(count)], axis=0)
+        few = jnp.dot(hots, x54_ref[...], preferred_element_type=F32)
         ys, y54s, places = [], [], []
         for i in range(count):
-            picked = jnp.dot(hot(low6[:, i : i + 1], R), x_ref[...], preferred_element_type=F32)
             seg = jnp.broadcast_to(hi6[:, i : i + 1], (R, R))
-            picked = jnp.where(seg == 0.0, picked[:, 0:R], jnp.where(seg == 1.0, picked[:, R : 2 * R], picked[:, 2 * R :]))
-            few = jnp.dot(hot(low54[:, i : i + 1], 32), x54_ref[...], preferred_element_type=F32)
+            p = picked[i * R : (i + 1) * R]
+            p = jnp.where(seg == 0.0, p[:, 0:R], jnp.where(seg == 1.0, p[:, R : 2 * R], p[:, 2 * R :]))
             seg = jnp.broadcast_to(hi54[:, i : i + 1], (32, R))
-            few = jnp.where(seg == 0.0, few[:, 0:R], few[:, R:])
-            rows = jnp.concatenate([picked.astype(BF), few.astype(BF)], axis=0)
+            w = few[i * 32 : (i + 1) * 32]
+            w = jnp.where(seg == 0.0, w[:, 0:R], w[:, R:])
+            rows = jnp.concatenate([p.astype(BF), w.astype(BF)], axis=0)
             y = jnp.dot(rows, t_ref[first + i], preferred_element_type=F32).astype(BF)
             ys.append(y[0:R])
             y54s.append(y[R:])
             places.append(placing(tf_ref[pl.ds(first + i, 1), :], 256, 0))
         acc_ref[...] += jnp.dot(jnp.concatenate(places, axis=1), jnp.concatenate(ys, axis=0), preferred_element_type=F32)
-        if count < G:
-            y54s.append(jnp.zeros((32 * (G - count), R), BF))
-        acc54_ref[...] += jnp.dot(placing(t54_ref[pl.ds(g, 1), :], 48, 0), jnp.concatenate(y54s, axis=0), preferred_element_type=F32)
+        if count % 4:
+            y54s.append(jnp.zeros((32 * (4 - count % 4), R), BF))
+        n = (count + 3) // 4
+        p54 = jnp.concatenate([placing(t54_ref[pl.ds(g * (G // 4) + j, 1), :], 48, 0) for j in range(n)], axis=1)
+        acc54_ref[...] += jnp.dot(p54, jnp.concatenate(y54s, axis=0), preferred_element_type=F32)
 
     def body(g, carry):
         group(g, G)
@@ -206,6 +212,10 @@
 MORTON = ("g", "z")
 
 
+def rows_of(table):
+    return table.transpose(1, 0, 2)
+
+
 def crossed(value, k):
     return lax.ppermute(value, SUB, [(i, i ^ k) for i in range(4)])
 
@@ -215,14 +225,14 @@
     q = lax.axis_index(SUB).astype(jnp.int32).reshape(1)
     peers = [crossed(multipoles, k) for k in (1, 2, 3)]
     spread, low6, hi6, low54, hi54, t54 = run_prep(
-        q, multipoles, upward_ops, source_boxes_level6[0], counts_l6, anchors_l5[0], counts_l5, anchors_l4[0], counts_l4,
-        target_boxes_level5[0], targets_l4[0])
+        q, multipoles, upward_ops, rows_of(source_boxes_level6), counts_l6, anchors_l5[0].T, counts_l5, anchors_l4[0].T, counts_l4,
+        target_boxes_level5[0].T, targets_l4[0].T)
     own = jnp.concatenate([multipoles] + peers, axis=0)
     n = lax.axis_size(MORTON)
     before = lax.ppermute(own, MORTON, [(i, i + 1) for i in range(n - 1)])
     after = lax.ppermute(own, MORTON, [(i + 1, i) for i in range(n - 1)])
     coarse = lax.all_to_all(spread, ("z",) + SUB, 0, 0)
-    parts = run_main(q, own, before, after, coarse, translations, low6, hi6, low54, hi54, targets_l6[0], t54)
+    parts = run_main(q, own, before, after, coarse, translations, low6, hi6, low54, hi54, rows_of(targets_l6), t54)
     received = [crossed(parts[k], k) for k in (1, 2, 3)]
     return run_final(parts[0], *received, downward_ops)
 

time: 68 us -> 44.6 us (0.66)
  Pallas kernels: 28.8 us -> 12.6 us
  local copies, waits for them, and re-layouts: 10.4 us -> 2.04 us
  waiting for transfers between devices: 3.27 us -> 4.57 us
    pallas_call x1, Pallas kernels: 24.6 us -> 8.45 us  [run_main(): pl.pallas_call(main_kernel, out_shape=tuple([shape((96, R), BF)] * 4), in...]
    unnamed x23 -> x17, local copies, waits for them, and re-layouts: 10.4 us -> 2.03 us
    ppermute x1, waiting for transfers between devices: 0.01 us -> 1.12 us  [local(): after = lax.ppermute(own, MORTON, [(i + 1, i) for i in range(n - 1)])]
  transfers between devices with their start and end apart: 9 -> 9, of which waited for: 2 -> 4; matrix products, arithmetic and copies ran while one was open for 13% -> 2% of each run, Pallas kernels for 3% -> 5%
where the time goes in v2:
time: 44.6 us; the launch traced here: 44.2 us
  starting transfers between devices  25 us (56%)
  Pallas kernels  12.6 us (28%)
  waiting for transfers between devices  4.57 us (10%)
  local copies, waits for them, and re-layouts  2.04 us (5%)
    all_to_all x1, starting transfers between devices, local(): coarse = lax.all_to_all(spread, ('z',) + SUB, 0, 0)  9.78 us
    pallas_call x1, Pallas kernels, run_main(): pl.pallas_call(main_kernel, out_shape=tuple([shape((96, R), BF)] * 4), in...  8.45 us
    ppermute x1, starting transfers between devices, local(): after = lax.ppermute(own, MORTON, [(i + 1, i) for i in range(n - 1)])  6.53 us
    ppermute x6, starting transfers between devices, crossed(): return lax.ppermute(value, SUB, [(i, i ^ k) for i in range(4)])  5.4 us
    ppermute x1, starting transfers between devices, local(): before = lax.ppermute(own, MORTON, [(i, i + 1) for i in range(n - 1)])  3.26 us
    ppermute x6, waiting for transfers between devices, crossed(): return lax.ppermute(value, SUB, [(i, i ^ k) for i in range(4)])  3.26 us
    pallas_call x1, Pallas kernels, run_prep(): pl.pallas_call(prep_kernel, out_shape=(shape((32, 16, R), BF), shape((R,...  2.14 us
    unnamed x17, local copies, waits for them, and re-layouts  2.03 us
  transfers between devices with their start and end apart: 9, of which 4 were waited for; matrix products, arithmetic and copies ran while one was open for 2% of the time, Pallas kernels for 5%

profile of v2, /device:TPU:9, one launch (start us, length us, event | category | flops | bytes accessed | tf_op | source)
XLA Modules:
  0.0 44.2 jit_solution(17455311214666854086)
XLA Ops:
  0.0 0.7 %collective-permute-start = (bf16[64,128]{1,0:T(8,128)(2,1)}, bf16[64,128]{1,0:T(8,128)(2,1)S(1)}, u32[]{:S(2)}, u32[]{:S(2)}) collective-permute-start(bf16[64,128]{1,0:T(8,128)(2,1)} %m_ref.1), channel_id=1, source_target_pairs={{0,1},{1,0},{2,3},{3,2},{4,5},{5,4},{6,7},{7,6},{8,9},{9,8},{10,11... | collective-permute-start | bytes 49160 | tf_op jit(solution)/shard_map/ppermute | solution.py:220
  0.7 1.2 %collective-permute-start.1 = (bf16[64,128]{1,0:T(8,128)(2,1)}, bf16[64,128]{1,0:T(8,128)(2,1)S(1)}, u32[]{:S(2)}, u32[]{:S(2)}) collective-permute-start(bf16[64,128]{1,0:T(8,128)(2,1)} %m_ref.1), channel_id=1, source_target_pairs={{0,2},{1,3},{2,0},{3,1},{4,6},{5,7},{6,4},{7,5},{8,10},{9,11},{10,... | collective-permute-start | bytes 49160 | tf_op jit(solution)/shard_map/ppermute | solution.py:220
  1.9 0.4 collective-permute-start.2
  2.3 2.1 %prep.1 = (bf16[32,16,128]{2,1,0:T(8,128)(2,1)}, f32[128,128]{1,0:T(8,128)}, f32[128,128]{1,0:T(8,128)}, f32[32,128]{1,0:T(8,128)}, f32[32,128]{1,0:T(8,128)}, /*index=5*/f32[24,128]{1,0:T(8,128)}) custom-call(s32[1]{0:T(128)} %bitcast.q_ref, bf16[64,128]{1,0:T(8,128)(2,1)} %m_ref.1, bf16[8,128,128]{2,1,0:T(8,128)(2,1)} %up_ref.1, s32[79,1,128]{2,1,0:T(1,128)} %bitcast.15, ...), custom_call_target="tpu_custom_call" | custom-call | tf_op jit(solution)/shard_map/prep/pallas_call | solution.py:173
  4.5 9.8 %all-to-all-start = ((bf16[32,16,128]{2,1,0:T(8,128)(2,1)}), bf16[32,16,128]{2,1,0:T(8,128)(2,1)S(1)}, u32[]{:S(2)}, u32[]{:S(2)}) async-start(bf16[32,16,128]{2,1,0:T(8,128)(2,1)} %get-tuple-element.15), calls=%async_computation | async-start | bytes 262144 | tf_op jit(solution)/shard_map/all_to_all | solution.py:234
  14.2 0.7 %constant_dynamic-update-slice_fusion.3 = bf16[256,128]{1,0:T(8,128)(2,1)S(1)} fusion(bf16[64,128]{1,0:T(8,128)(2,1)} %m_ref.1), kind=kLoop, calls=%fused_computation.3 | loop fusion | bytes 32768
  15.0 0.0 collective-permute-done
  15.0 0.0 collective-permute-done.1
  15.0 0.0 collective-permute-done.2
  15.0 0.0 copy-start.1
  15.0 3.3 %collective-permute-start.3 = (bf16[256,128]{1,0:T(8,128)(2,1)S(1)}, bf16[256,128]{1,0:T(8,128)(2,1)S(1)}, u32[]{:S(2)}, u32[]{:S(2)}) collective-permute-start(bf16[256,128]{1,0:T(8,128)(2,1)S(1)} %constant_dynamic-update-slice_fusion.own_ref), channel_id=1, source_target_pairs={{0,4},{4,8},{8,12},{12,16},{16,20},{20,24},{24,28},{28,32},{32,36}... | collective-permute-start | bytes 196616 | tf_op jit(solution)/shard_map/ppermute | solution.py:232
  18.3 6.5 %collective-permute-start.4 = (bf16[256,128]{1,0:T(8,128)(2,1)S(1)}, bf16[256,128]{1,0:T(8,128)(2,1)S(1)}, u32[]{:S(2)}, u32[]{:S(2)}) collective-permute-start(bf16[256,128]{1,0:T(8,128)(2,1)S(1)} %constant_dynamic-update-slice_fusion.own_ref), channel_id=1, source_target_pairs={{4,0},{8,4},{12,8},{16,12},{20,16},{24,20},{28,24},{32,28},{36,32}... | collective-permute-start | bytes 196616 | tf_op jit(solution)/shard_map/ppermute | solution.py:233
  24.8 0.2 collective-permute-done.3.prev_ref
  25.0 1.1 %collective-permute-done.4.next_ref = bf16[256,128]{1,0:T(8,128)(2,1)S(1)} collective-permute-done((bf16[256,128]{1,0:T(8,128)(2,1)S(1)}, bf16[256,128]{1,0:T(8,128)(2,1)S(1)}, u32[]{:S(2)}, u32[]{:S(2)}) %collective-permute-start.4) | collective-permute-done | bytes 65568 | tf_op jit(solution)/shard_map/ppermute | solution.py:233
  26.2 0.0 copy-start.3
  26.2 0.0 all-to-all-done.grp_ref
  26.2 0.0 copy-start
  26.2 0.0 copy-done.1
  26.2 0.0 copy-done.2
  26.2 0.6 %copy-done.3 = bf16[256,128]{1,0:T(8,128)(2,1)} copy-done((bf16[256,128]{1,0:T(8,128)(2,1)}, bf16[256,128]{1,0:T(8,128)(2,1)S(1)}, u32[]{:S(2)}) %copy-start.3) | copy-done | bytes 65560
  26.8 0.1 copy-done
  26.9 8.4 %translate.1 = (bf16[96,128]{1,0:T(8,128)(2,1)}, bf16[96,128]{1,0:T(8,128)(2,1)}, bf16[96,128]{1,0:T(8,128)(2,1)}, bf16[96,128]{1,0:T(8,128)(2,1)}) custom-call(s32[1]{0:T(128)} %bitcast.q_ref, bf16[256,128]{1,0:T(8,128)(2,1)} %copy-done.1, bf16[256,128]{1,0:T(8,128)(2,1)} %copy-done.2, bf16[256,128]{1,0:T(8,128)(2,1)} %copy-done.3, ...), custom_call_target="tpu_custom_call" | custom-call | tf_op jit(solution)/shard_map/translate/pallas_call | solution.py:184
  35.3 1.4 %collective-permute-start.5 = (bf16[96,128]{1,0:T(8,128)(2,1)}, bf16[96,128]{1,0:T(8,128)(2,1)S(1)}, u32[]{:S(2)}, u32[]{:S(2)}) collective-permute-start(bf16[96,128]{1,0:T(8,128)(2,1)} %get-tuple-element.22), channel_id=1, source_target_pairs={{0,1},{1,0},{2,3},{3,2},{4,5},{5,4},{6,7},{7,6},{8,9},{9,8},{10,11... | collective-permute-start | bytes 73736 | tf_op jit(solution)/shard_map/ppermute | solution.py:220
  36.7 1.5 %collective-permute-start.6 = (bf16[96,128]{1,0:T(8,128)(2,1)}, bf16[96,128]{1,0:T(8,128)(2,1)S(1)}, u32[]{:S(2)}, u32[]{:S(2)}) collective-permute-start(bf16[96,128]{1,0:T(8,128)(2,1)} %get-tuple-element.23), channel_id=1, source_target_pairs={{0,2},{1,3},{2,0},{3,1},{4,6},{5,7},{6,4},{7,5},{8,10},{9,11},{10,... | collective-permute-start | bytes 73736 | tf_op jit(solution)/shard_map/ppermute | solution.py:220
  38.2 0.2 collective-permute-start.7
  38.4 0.0 collective-permute-done.5.b_ref
  38.4 1.2 %collective-permute-done.6.c_ref = bf16[96,128]{1,0:T(8,128)(2,1)S(1)} collective-permute-done((bf16[96,128]{1,0:T(8,128)(2,1)}, bf16[96,128]{1,0:T(8,128)(2,1)S(1)}, u32[]{:S(2)}, u32[]{:S(2)}) %collective-permute-start.6) | collective-permute-done | bytes 24608 | tf_op jit(solution)/shard_map/ppermute | solution.py:220
  39.6 2.0 %collective-permute-done.7.d_ref = bf16[96,128]{1,0:T(8,128)(2,1)S(1)} collective-permute-done((bf16[96,128]{1,0:T(8,128)(2,1)}, bf16[96,128]{1,0:T(8,128)(2,1)S(1)}, u32[]{:S(2)}, u32[]{:S(2)}) %collective-permute-start.7) | collective-permute-done | bytes 24608 | tf_op jit(solution)/shard_map/ppermute | solution.py:220
  41.7 0.0 copy-done.4
  41.7 0.0 copy-done.5
  41.7 0.6 %copy-done.6 = bf16[96,128]{1,0:T(8,128)(2,1)} copy-done((bf16[96,128]{1,0:T(8,128)(2,1)}, bf16[96,128]{1,0:T(8,128)(2,1)S(1)}, u32[]{:S(2)}) %copy-start.6) | copy-done | bytes 24600
  42.3 2.0 %downward.1 = bf16[64,128]{1,0:T(8,128)(2,1)} custom-call(bf16[96,128]{1,0:T(8,128)(2,1)} %get-tuple-element.21.a_ref, bf16[96,128]{1,0:T(8,128)(2,1)} %copy-done.4, bf16[96,128]{1,0:T(8,128)(2,1)} %copy-done.5, bf16[96,128]{1,0:T(8,128)(2,1)} %copy-done.6, bf16[8,128,128]{2,1,0:T(8,128)(2,1)} %dn_ref.1), custom_call_target="tpu_custom_call" | custom-call | tf_op jit(solution)/shard_map/downward/pallas_call | solution.py:201
  (7 shorter events, 0.0 us)
Async XLA Ops:
  0.0 15.0 %collective-permute-start = (bf16[64,128]{1,0:T(8,128)(2,1)}, bf16[64,128]{1,0:T(8,128)(2,1)S(1)}, u32[]{:S(2)}, u32[]{:S(2)}) collective-permute-start(bf16[64,128]{1,0:T(8,128)(2,1)} %m_ref.1), channel_id=1, source_target_pairs={{0,1},{1,0},{2,3},{3,2},{4,5},{5,4},{6,7},{7,6},{8,9},{9,8},{10,11... | collective-permute-start | bytes 49160 | tf_op jit(solution)/shard_map/ppermute | solution.py:220
  0.7 14.3 %collective-permute-start.1 = (bf16[64,128]{1,0:T(8,128)(2,1)}, bf16[64,128]{1,0:T(8,128)(2,1)S(1)}, u32[]{:S(2)}, u32[]{:S(2)}) collective-permute-start(bf16[64,128]{1,0:T(8,128)(2,1)} %m_ref.1), channel_id=1, source_target_pairs={{0,2},{1,3},{2,0},{3,1},{4,6},{5,7},{6,4},{7,5},{8,10},{9,11},{10,... | collective-permute-start | bytes 49160 | tf_op jit(solution)/shard_map/ppermute | solution.py:220
  1.9 13.1 %collective-permute-start.2 = (bf16[64,128]{1,0:T(8,128)(2,1)}, bf16[64,128]{1,0:T(8,128)(2,1)S(1)}, u32[]{:S(2)}, u32[]{:S(2)}) collective-permute-start(bf16[64,128]{1,0:T(8,128)(2,1)} %m_ref.1), channel_id=1, source_target_pairs={{0,3},{1,2},{2,1},{3,0},{4,7},{5,6},{6,5},{7,4},{8,11},{9,10},{10,... | collective-permute-start | bytes 49160 | tf_op jit(solution)/shard_map/ppermute | solution.py:220
  4.5 21.7 %all-to-all-start = ((bf16[32,16,128]{2,1,0:T(8,128)(2,1)}), bf16[32,16,128]{2,1,0:T(8,128)(2,1)S(1)}, u32[]{:S(2)}, u32[]{:S(2)}) async-start(bf16[32,16,128]{2,1,0:T(8,128)(2,1)} %get-tuple-element.15), calls=%async_computation | async-start | bytes 262144 | tf_op jit(solution)/shard_map/all_to_all | solution.py:234
  15.0 11.1 %copy-start.1 = (bf16[256,128]{1,0:T(8,128)(2,1)}, bf16[256,128]{1,0:T(8,128)(2,1)S(1)}, u32[]{:S(2)}) copy-start(bf16[256,128]{1,0:T(8,128)(2,1)S(1)} %constant_dynamic-update-slice_fusion.own_ref) | copy-start | bytes 196612
  15.0 10.0 %collective-permute-start.3 = (bf16[256,128]{1,0:T(8,128)(2,1)S(1)}, bf16[256,128]{1,0:T(8,128)(2,1)S(1)}, u32[]{:S(2)}, u32[]{:S(2)}) collective-permute-start(bf16[256,128]{1,0:T(8,128)(2,1)S(1)} %constant_dynamic-update-slice_fusion.own_ref), channel_id=1, source_target_pairs={{0,4},{4,8},{8,12},{12,16},{16,20},{20,24},{24,28},{28,32},{32,36}... | collective-permute-start | bytes 196616 | tf_op jit(solution)/shard_map/ppermute | solution.py:232
  18.3 7.9 %collective-permute-start.4 = (bf16[256,128]{1,0:T(8,128)(2,1)S(1)}, bf16[256,128]{1,0:T(8,128)(2,1)S(1)}, u32[]{:S(2)}, u32[]{:S(2)}) collective-permute-start(bf16[256,128]{1,0:T(8,128)(2,1)S(1)} %constant_dynamic-update-slice_fusion.own_ref), channel_id=1, source_target_pairs={{4,0},{8,4},{12,8},{16,12},{20,16},{24,20},{28,24},{32,28},{36,32}... | collective-permute-start | bytes 196616 | tf_op jit(solution)/shard_map/ppermute | solution.py:233
  25.0 1.1 %copy-start.2 = (bf16[256,128]{1,0:T(8,128)(2,1)}, bf16[256,128]{1,0:T(8,128)(2,1)S(1)}, u32[]{:S(2)}) copy-start(bf16[256,128]{1,0:T(8,128)(2,1)S(1)} %collective-permute-done.3.prev_ref) | copy-start | bytes 196612
  26.2 0.6 %copy-start.3 = (bf16[256,128]{1,0:T(8,128)(2,1)}, bf16[256,128]{1,0:T(8,128)(2,1)S(1)}, u32[]{:S(2)}) copy-start(bf16[256,128]{1,0:T(8,128)(2,1)S(1)} %collective-permute-done.4.next_ref) | copy-start | bytes 196612
  26.2 0.7 %copy-start = (bf16[32,16,128]{2,1,0:T(8,128)(2,1)}, bf16[32,16,128]{2,1,0:T(8,128)(2,1)S(1)}, u32[]{:S(2)}) copy-start(bf16[32,16,128]{2,1,0:T(8,128)(2,1)S(1)} %all-to-all-done.grp_ref) | copy-start | bytes 393220
  35.3 3.1 %collective-permute-start.5 = (bf16[96,128]{1,0:T(8,128)(2,1)}, bf16[96,128]{1,0:T(8,128)(2,1)S(1)}, u32[]{:S(2)}, u32[]{:S(2)}) collective-permute-start(bf16[96,128]{1,0:T(8,128)(2,1)} %get-tuple-element.22), channel_id=1, source_target_pairs={{0,1},{1,0},{2,3},{3,2},{4,5},{5,4},{6,7},{7,6},{8,9},{9,8},{10,11... | collective-permute-start | bytes 73736 | tf_op jit(solution)/shard_map/ppermute | solution.py:220
  36.7 2.9 %collective-permute-start.6 = (bf16[96,128]{1,0:T(8,128)(2,1)}, bf16[96,128]{1,0:T(8,128)(2,1)S(1)}, u32[]{:S(2)}, u32[]{:S(2)}) collective-permute-start(bf16[96,128]{1,0:T(8,128)(2,1)} %get-tuple-element.23), channel_id=1, source_target_pairs={{0,2},{1,3},{2,0},{3,1},{4,6},{5,7},{6,4},{7,5},{8,10},{9,11},{10,... | collective-permute-start | bytes 73736 | tf_op jit(solution)/shard_map/ppermute | solution.py:220
  38.2 3.5 %collective-permute-start.7 = (bf16[96,128]{1,0:T(8,128)(2,1)}, bf16[96,128]{1,0:T(8,128)(2,1)S(1)}, u32[]{:S(2)}, u32[]{:S(2)}) collective-permute-start(bf16[96,128]{1,0:T(8,128)(2,1)} %get-tuple-element.24), channel_id=1, source_target_pairs={{0,3},{1,2},{2,1},{3,0},{4,7},{5,6},{6,5},{7,4},{8,11},{9,10},{10,... | collective-permute-start | bytes 73736 | tf_op jit(solution)/shard_map/ppermute | solution.py:220
  38.4 3.3 %copy-start.4 = (bf16[96,128]{1,0:T(8,128)(2,1)}, bf16[96,128]{1,0:T(8,128)(2,1)S(1)}, u32[]{:S(2)}) copy-start(bf16[96,128]{1,0:T(8,128)(2,1)S(1)} %collective-permute-done.5.b_ref) | copy-start | bytes 73732
  39.6 2.0 %copy-start.5 = (bf16[96,128]{1,0:T(8,128)(2,1)}, bf16[96,128]{1,0:T(8,128)(2,1)S(1)}, u32[]{:S(2)}) copy-start(bf16[96,128]{1,0:T(8,128)(2,1)S(1)} %collective-permute-done.6.c_ref) | copy-start | bytes 73732
  41.7 0.6 %copy-start.6 = (bf16[96,128]{1,0:T(8,128)(2,1)}, bf16[96,128]{1,0:T(8,128)(2,1)S(1)}, u32[]{:S(2)}) copy-start(bf16[96,128]{1,0:T(8,128)(2,1)S(1)} %collective-permute-done.7.d_ref) | copy-start | bytes 73732

commit v3 on v2

v3 whole, which is shorter than its diff:
```python
import jax
import jax.numpy as jnp
from jax import lax
from jax.experimental import pallas as pl
from jax.experimental.pallas import tpu as pltpu
from jax.sharding import Mesh
from jax.sharding import PartitionSpec as P


R = 128
NO = 79
G = 20
HELD = 20
BF = jnp.bfloat16
F32 = jnp.float32


def iota(shape, dim):
    return lax.broadcasted_iota(jnp.int32, shape, dim)


def prep_kernel(q_ref, m_ref, up_ref, src_ref, c6_ref, a5_ref, c5_ref, a4_ref, c4_ref, t5_ref, t4_ref, t6_ref, t_hbm,
                grp_ref, low6_ref, hi6_ref, low54_ref, hi54_ref, t54_ref, tgt_ref, own_ref, t_ref, sq_ref, st_ref, sem):
    fetch = pltpu.make_async_copy(t_hbm.at[pl.ds(0, HELD)], t_ref, sem)
    fetch.start()
    own_ref[0:64] = m_ref[...]
    own_ref[64:256] = jnp.zeros((192, R), BF)
    tgt_ref[0:NO, :] = t6_ref[...].reshape(NO, R).astype(F32)
    tgt_ref[NO:80, :] = jnp.zeros((80 - NO, R), F32)
    q = q_ref[0]
    st_ref[pl.ds(0, 64), :] = m_ref[...].astype(F32)
    c5 = jnp.zeros((8, R), F32)
    for c in range(8):
        rows = st_ref[pl.ds(c, 8, stride=8), :].astype(BF)
        c5 = c5 + jnp.dot(rows, up_ref[c], preferred_element_type=F32)
    c5r = c5.astype(BF).astype(F32)
    c4 = jnp.zeros((8, R), F32)
    for c in range(8):
        rows = jnp.broadcast_to(c5r[c : c + 1, :], (8, R)).astype(BF)
        c4 = c4 + jnp.dot(rows, up_ref[c], preferred_element_type=F32)
    both = jnp.concatenate([c5, c4], axis=0).astype(BF)
    grp_ref[...] = jnp.broadcast_to(both[None], (32, 16, R))

    sq_ref[...] = jnp.zeros((R, R), F32)
    sq_ref[0:NO, :] = src_ref[...].reshape(NO, R).astype(F32)
    src = sq_ref[...].T.astype(jnp.int32)

    def live(c_ref, rows):
        sq_ref[0:1, :] = jnp.zeros((1, R), F32)
        sq_ref[0:1, 0:NO] = c_ref[...].astype(F32)
        counts = jnp.broadcast_to(sq_ref[0:1, :], (rows, R))
        return iota((rows, R), 0).astype(F32) < counts

    low = jnp.bitwise_xor(jnp.bitwise_and(src, 255), q * 64)
    low6_ref[...] = jnp.where(live(c6_ref, R), low.astype(F32), -1.0).astype(BF)
    hi6_ref[...] = jnp.right_shift(src, 8).astype(F32).astype(BF)
    a5 = a5_ref[...]
    sq_ref[0:16, 0:NO] = (16 * jnp.right_shift(a5, 3) + jnp.bitwise_and(a5, 7)).astype(F32)
    code5 = sq_ref[0:16, :]
    code5 = jnp.where(live(c5_ref, 16), code5, -1.0)
    sq_ref[0:2, 0:NO] = (16 * a4_ref[...] + 8).astype(F32)
    code4 = sq_ref[0:16, :]
    code4 = jnp.where(live(c4_ref, 16), code4, -1.0)
    code = jnp.concatenate([code5, code4], axis=0)
    upper = code >= 256.0
    low54_ref[...] = jnp.where(upper, code - 256.0, code).astype(BF)
    hi54_ref[...] = upper.astype(F32).astype(BF)
    sq_ref[...] = jnp.full((R, R), -1.0, F32)
    sq_ref[0:16, 0:NO] = t5_ref[...].astype(F32)
    sq_ref[16:18, 0:NO] = t4_ref[...].astype(F32) + 32.0
    sq_ref[...] = sq_ref[...].T
    packed = sq_ref[pl.ds(0, 24, stride=4), :]
    lane = iota((24, R), 1)
    for i in range(1, 4):
        part = pltpu.roll(sq_ref[pl.ds(i, 24, stride=4), :], 32 * i, 1)
        packed = jnp.where(lane >= 32 * i, part, packed)
    t54_ref[...] = packed
    fetch.wait()


def hot(column, rows):
    wide = jnp.broadcast_to(column, (rows, R))
    lane = iota((rows, R), 1)
    one = jnp.ones((rows, R), BF)
    zero = jnp.zeros((rows, R), BF)
    left = jnp.where(wide == lane.astype(BF), one, zero)
    right = jnp.where(wide == (lane + R).astype(BF), one, zero)
    return jnp.concatenate([left, right], axis=1)


def placing(row, rows):
    wide = jnp.broadcast_to(row, (rows, R)).astype(BF)
    down = iota((rows, R), 0).astype(BF)
    return jnp.where(wide == down, jnp.ones((rows, R), BF), jnp.zeros((rows, R), BF))


def fine_kernel(z_ref, g_ref, own_ref, prev_ref, next_ref, far_ref, h_ref, low_ref, hi_ref, tgt_ref, t_hbm, acc_ref, t_ref, x_ref, sem):
    fetch = pltpu.make_async_copy(t_hbm.at[pl.ds(HELD, NO - HELD)], t_ref, sem)
    fetch.start()
    z = z_ref[0]
    x_ref[:, R : 2 * R] = own_ref[...]

    g = g_ref[0]
    nothing = jnp.zeros((256, R), BF)

    @pl.when(z == 0)
    def _():
        x_ref[:, 0:R] = jnp.where(g > 0, far_ref[...], nothing)

    @pl.when(z > 0)
    def _():
        x_ref[:, 0:R] = prev_ref[...]

    @pl.when(z == 7)
    def _():
        x_ref[:, 2 * R : 3 * R] = jnp.where(g < 7, far_ref[...], nothing)

    @pl.when(z < 7)
    def _():
        x_ref[:, 2 * R : 3 * R] = next_ref[...]

    low = low_ref[...]
    hi = hi_ref[...]
    for first in range(0, NO, G):
        ops = range(first, min(first + G, NO))
        hots = jnp.concatenate([hot(low[:, o : o + 1], R) for o in ops], axis=0)
        found = jnp.dot(hots, x_ref[...], preferred_element_type=F32).astype(BF)
        if first == HELD:
            fetch.wait()
        ys, places = [], []
        for n, o in enumerate(ops):
            seg = jnp.broadcast_to(hi[:, o : o + 1], (R, R))
            p = found[n * R : (n + 1) * R]
            p = jnp.where(seg == jnp.asarray(0, BF), p[:, 0:R], jnp.where(seg == jnp.asarray(1, BF), p[:, R : 2 * R], p[:, 2 * R :]))
            operator = h_ref[o] if o < HELD else t_ref[o - HELD]
            ys.append(jnp.dot(p, operator, preferred_element_type=F32).astype(BF))
            places.append(placing(tgt_ref[o : o + 1, :], 256))
        added = jnp.dot(jnp.concatenate(places, axis=1), jnp.concatenate(ys, axis=0), preferred_element_type=F32)
        if first == 0:
            acc_ref[...] = added
        else:
            acc_ref[...] += added


def coarse_kernel(q_ref, acc_ref, grp_ref, h_ref, t_ref, low_ref, hi_ref, t54_ref, o0_ref, o1_ref, o2_ref, o3_ref, x_ref, far_ref):
    x_ref[:, 0:R] = grp_ref[0:16].reshape(256, R)
    x_ref[:, R : 2 * R] = grp_ref[16:32].reshape(256, R)
    low = low_ref[...]
    hi = hi_ref[...]
    for first in range(0, NO, G):
        ops = range(first, min(first + G, NO))
        hots = jnp.concatenate([hot(low[:, o : o + 1], 32) for o in ops], axis=0)
        found = jnp.dot(hots, x_ref[...], preferred_element_type=F32).astype(BF)
        ys = []
        for n, o in enumerate(ops):
            seg = jnp.broadcast_to(hi[:, o : o + 1], (32, R))
            p = found[n * 32 : (n + 1) * 32]
            p = jnp.where(seg == jnp.asarray(0, BF), p[:, 0:R], p[:, R:])
            operator = h_ref[o] if o < HELD else t_ref[o - HELD]
            ys.append(jnp.dot(p, operator, preferred_element_type=F32).astype(BF))
        short = -len(ops) % 4
        if short:
            ys.append(jnp.zeros((32 * short, R), BF))
        rows = range(first // 4, (first + len(ops) + 3) // 4)
        places = jnp.concatenate([placing(t54_ref[j : j + 1, :], 48) for j in rows], axis=1)
        added = jnp.dot(places, jnp.concatenate(ys, axis=0), preferred_element_type=F32)
        if first == 0:
            far_ref[...] = added
        else:
            far_ref[...] += added
    q = q_ref[0]
    far_ref[0:32] = far_ref[0:32] * 0.5
    far_ref[32:48] = far_ref[32:48] * 0.25
    for k, out in enumerate((o0_ref, o1_ref, o2_ref, o3_ref)):
        d = jnp.bitwise_xor(q, k)
        out[0:64] = acc_ref[pl.ds(64 * d, 64), :].astype(BF)
        five = far_ref[pl.ds(8 * d, 8), :]
        four = jnp.broadcast_to(far_ref[pl.ds(32 + d, 1), :], (8, R))
        small = jnp.concatenate([five, four], axis=0)
        top = small.astype(BF)
        out[64:80] = top
        out[80:96] = (small - top.astype(F32)).astype(BF)


def final_kernel(a_ref, b_ref, c_ref, d_ref, dn_ref, out_ref, s_ref):
    total = (a_ref[...].astype(F32) + b_ref[...].astype(F32)) + (c_ref[...].astype(F32) + d_ref[...].astype(F32))
    small = total[64:80] + total[80:96]
    far5 = small[0:8]
    local4 = small[8:16].astype(BF)
    row = iota((8, R), 0)
    local5 = far5
    for c in range(8):
        spread = jnp.dot(local4, dn_ref[c], preferred_element_type=F32)
        local5 = local5 + jnp.where(row == c, spread, 0.0)
    local5 = local5.astype(BF)
    for c in range(8):
        s_ref[pl.ds(c, 8, stride=8), :] = jnp.dot(local5, dn_ref[c], preferred_element_type=F32)
    out_ref[...] = (total[0:64] + s_ref[...]).astype(BF)


VM = pl.BlockSpec(memory_space=pltpu.VMEM)
SM = pl.BlockSpec(memory_space=pltpu.SMEM)
FAR = pl.BlockSpec(memory_space=pl.ANY)
LIMIT = pltpu.CompilerParams(vmem_limit_bytes=24 * 1024 * 1024)


def near_core(value):
    return pltpu.with_memory_space_constraint(value, pltpu.VMEM)


def in_hbm(value):
    return pltpu.with_memory_space_constraint(value, pltpu.HBM)


def call(kernel, outs, scratch, vectors, scalars=(), far=0):
    return pl.pallas_call(
        kernel,
        out_shape=tuple(pltpu.VMEM(dims, kind) for dims, kind in outs),
        in_specs=[SM] * len(scalars) + [VM] * (len(vectors) - far) + [FAR] * far,
        out_specs=tuple([VM] * len(outs)),
        scratch_shapes=scratch,
        compiler_params=LIMIT,
    )(*scalars, *vectors)


SUB = ("x", "c")
MORTON = ("g", "z")


def rows_of(table):
    return table.transpose(1, 0, 2)


def crossed(value, k):
    return lax.ppermute(value, SUB, [(i, i ^ k) for i in range(4)])


def local(multipoles, translations, upward_ops, downward_ops, targets_l6, source_boxes_level6, counts_l6,
          target_boxes_level5, anchors_l5, counts_l5, targets_l4, anchors_l4, counts_l4):
    q = lax.axis_index(SUB).astype(jnp.int32).reshape(1)
    z = lax.axis_index("z").astype(jnp.int32).reshape(1)
    g = lax.axis_index("g").astype(jnp.int32).reshape(1)
    groups, ring = lax.axis_size("g"), lax.axis_size("z")
    peers = [crossed(multipoles, k) for k in (1, 2, 3)]
    spread, low6, hi6, low54, hi54, t54, tgt, own, held = call(
        prep_kernel,
        [((32, 16, R), BF), ((R, R), BF), ((R, R), BF), ((32, R), BF), ((32, R), BF), ((24, R), F32), ((80, R), F32),
         ((256, R), BF), ((HELD, R, R), BF)],
        [pltpu.VMEM((R, R), F32), pltpu.VMEM((64, R), F32), pltpu.SemaphoreType.DMA],
        [*map(in_hbm, (multipoles, upward_ops, rows_of(source_boxes_level6), counts_l6, anchors_l5[0].T, counts_l5,
                       anchors_l4[0].T, counts_l4, target_boxes_level5[0].T, targets_l4[0].T, rows_of(targets_l6), translations))],
        [q], far=1)
    for k, peer in enumerate(peers):
        own = lax.dynamic_update_slice(own, peer, (64 * k + 64, 0))
    before = lax.ppermute(own, "z", [(i, (i + 1) % ring) for i in range(ring)])
    after = lax.ppermute(own, "z", [((i + 1) % ring, i) for i in range(ring)])
    ends = [(i * ring + ring - 1, i * ring + ring) for i in range(groups - 1)]
    ends = dict(ends + [(j, i) for i, j in ends])
    far = lax.ppermute(own, MORTON, [(i, ends.get(i, i)) for i in range(groups * ring)])
    coarse = lax.all_to_all(spread, ("z",) + SUB, 0, 0)
    fine, rest = call(fine_kernel, [((256, R), F32), ((NO - HELD, R, R), BF)],
                   [pltpu.VMEM((256, 3 * R), BF), pltpu.SemaphoreType.DMA],
                   [*map(near_core, (own, before, after, far, held, low6, hi6, tgt)), in_hbm(translations)], [z, g], far=1)
    parts = call(coarse_kernel, [((96, R), BF)] * 4, [pltpu.VMEM((256, 2 * R), BF), pltpu.VMEM((48, R), F32)],
                 [*map(near_core, (fine, coarse, held, rest, low54, hi54, t54))], [q])
    received = [crossed(parts[k], k) for k in (1, 2, 3)]
    return pl.pallas_call(
        final_kernel,
        out_shape=jax.ShapeDtypeStruct((64, R), BF),
        in_specs=[VM] * 5,
        out_specs=VM,
        scratch_shapes=[pltpu.VMEM((64, R), F32)],
        compiler_params=LIMIT,
        name="downward",
    )(*[near_core(v) for v in (parts[0], *received, downward_ops)])


def solution(mesh):
    cut = Mesh(mesh.devices.reshape(8, 8, 2, 2), ("g", "z", "x", "c"))
    both = MORTON + SUB
    placed = (
        P(both, None),
        P(SUB, None, None),
        P(),
        P(),
        P(MORTON, SUB, None),
        P(MORTON, SUB, None),
        P(MORTON, SUB),
        P(MORTON, SUB, None),
        P(MORTON, SUB, None),
        P(MORTON, SUB),
        P(MORTON, SUB, None),
        P(MORTON, SUB, None),
        P(MORTON, SUB),
    )
    return jax.shard_map(local, mesh=cut, in_specs=placed, out_specs=P(both, None), check_vma=False)
```

time: 44.6 us -> 42.6 us (0.955)
  the two profiles are of different devices: /device:TPU:9 before, /device:TPU:1 now
where the time goes in v3:
time: 42.6 us; the launch traced here: 42.3 us
  starting transfers between devices  23.8 us (56%)
  Pallas kernels  11.7 us (27%)
  waiting for transfers between devices  6.75 us (16%)
    pallas_call x3, Pallas kernels, call(): pl.pallas_call(kernel, out_shape=tuple((pltpu.VMEM(dims, kind) for dims,...  10.7 us
    all_to_all x1, starting transfers between devices, local(): coarse = lax.all_to_all(spread, ('z',) + SUB, 0, 0)  8.64 us
    ppermute x6, starting transfers between devices, crossed(): return lax.ppermute(value, SUB, [(i, i ^ k) for i in range(4)])  8.32 us
    ppermute x1, starting transfers between devices, local(): after = lax.ppermute(own, 'z', [((i + 1) % ring, i) for i in range(ring)])  6.16 us
    ppermute x1, waiting for transfers between devices, local(): before = lax.ppermute(own, 'z', [(i, (i + 1) % ring) for i in range(ring)])  2.99 us
    ppermute x6, waiting for transfers between devices, crossed(): return lax.ppermute(value, SUB, [(i, i ^ k) for i in range(4)])  2.42 us
    ppermute x1, waiting for transfers between devices, local(): after = lax.ppermute(own, 'z', [((i + 1) % ring, i) for i in range(ring)])  1.33 us
    pallas_call x1, Pallas kernels, local(): pl.pallas_call(final_kernel, out_shape=jax.ShapeDtypeStruct((64, R), BF),...  0.96 us
  transfers between devices with their start and end apart: 10, of which 4 were waited for; matrix products, arithmetic and copies ran while one was open for 0% of the time, Pallas kernels for 20%

profile of v3, /device:TPU:1, one launch (start us, length us, event | category | flops | bytes accessed | tf_op | source)
XLA Modules:
  0.0 42.3 jit_solution(1194081052171262800)
XLA Ops:
  0.0 3.2 %collective-permute-start = (bf16[64,128]{1,0:T(8,128)(2,1)}, bf16[64,128]{1,0:T(8,128)(2,1)S(1)}, u32[]{:S(2)}, u32[]{:S(2)}) collective-permute-start(bf16[64,128]{1,0:T(8,128)(2,1)} %m_ref.1), channel_id=1, source_target_pairs={{0,1},{1,0},{2,3},{3,2},{4,5},{5,4},{6,7},{7,6},{8,9},{9,8},{10,11... | collective-permute-start | bytes 49160 | tf_op jit(solution)/shard_map/ppermute | solution.py:235
  3.2 0.0 collective-permute-start.2
  3.2 1.4 %collective-permute-start.1 = (bf16[64,128]{1,0:T(8,128)(2,1)}, bf16[64,128]{1,0:T(8,128)(2,1)S(1)}, u32[]{:S(2)}, u32[]{:S(2)}) collective-permute-start(bf16[64,128]{1,0:T(8,128)(2,1)} %m_ref.1), channel_id=1, source_target_pairs={{0,2},{1,3},{2,0},{3,1},{4,6},{5,7},{6,4},{7,5},{8,10},{9,11},{10,... | collective-permute-start | bytes 49160 | tf_op jit(solution)/shard_map/ppermute | solution.py:235
  4.6 3.0 %shard_map.127 = (bf16[32,16,128]{2,1,0:T(8,128)(2,1)}, bf16[128,128]{1,0:T(8,128)(2,1)S(1)}, bf16[128,128]{1,0:T(8,128)(2,1)S(1)}, bf16[32,128]{1,0:T(8,128)(2,...) custom-call(s32[1]{0:T(128)} %bitcast.q_ref, ...), custom_call_target="tpu_custom_call" | custom-call | tf_op jit(solution)/shard_map/pallas_call | solution.py:216
  7.5 8.6 %all-to-all-start = ((bf16[32,16,128]{2,1,0:T(8,128)(2,1)}), bf16[32,16,128]{2,1,0:T(8,128)(2,1)S(1)}, u32[]{:S(2)}, u32[]{:S(2)}) async-start(bf16[32,16,128]{2,1,0:T(8,128)(2,1)} %get-tuple-element.26), calls=%async_computation | async-start | bytes 262144 | tf_op jit(solution)/shard_map/all_to_all | solution.py:260
  16.2 0.0 collective-permute-done
  16.2 0.0 collective-permute-done.1
  16.2 0.0 collective-permute-done.2
  16.3 0.7 %collective-permute-start.5 = (bf16[256,128]{1,0:T(8,128)(2,1)S(1)}, bf16[256,128]{1,0:T(8,128)(2,1)S(1)}, u32[]{:S(2)}, u32[]{:S(2)}) collective-permute-start(bf16[256,128]{1,0:T(8,128)(2,1)S(1)} %constant_dynamic-update-slice_fusion.own_ref), channel_id=1, source_target_pairs={{0,0},{4,4},{8,8},{12,12},{16,16},{20,20},{24,24},{28,32},{32,28},... | collective-permute-start | bytes 196616 | tf_op jit(solution)/shard_map/ppermute | solution.py:259
  16.9 6.2 %collective-permute-start.4 = (bf16[256,128]{1,0:T(8,128)(2,1)S(1)}, bf16[256,128]{1,0:T(8,128)(2,1)S(1)}, u32[]{:S(2)}, u32[]{:S(2)}) collective-permute-start(bf16[256,128]{1,0:T(8,128)(2,1)S(1)} %constant_dynamic-update-slice_fusion.own_ref), channel_id=1, source_target_pairs={{4,0},{8,4},{12,8},{16,12},{20,16},{24,20},{28,24},{0,28},{5,1},{9... | collective-permute-start | bytes 196616 | tf_op jit(solution)/shard_map/ppermute | solution.py:256
  23.1 0.0 collective-permute-start.3
  23.1 0.0 collective-permute-done.5.far_ref
  23.1 1.3 %collective-permute-done.4.next_ref = bf16[256,128]{1,0:T(8,128)(2,1)S(1)} collective-permute-done((bf16[256,128]{1,0:T(8,128)(2,1)S(1)}, bf16[256,128]{1,0:T(8,128)(2,1)S(1)}, u32[]{:S(2)}, u32[]{:S(2)}) %collective-permute-start.4) | collective-permute-done | bytes 65568 | tf_op jit(solution)/shard_map/ppermute | solution.py:256
  24.4 3.0 %collective-permute-done.3.prev_ref = bf16[256,128]{1,0:T(8,128)(2,1)S(1)} collective-permute-done((bf16[256,128]{1,0:T(8,128)(2,1)S(1)}, bf16[256,128]{1,0:T(8,128)(2,1)S(1)}, u32[]{:S(2)}, u32[]{:S(2)}) %collective-permute-start.3) | collective-permute-done | bytes 65568 | tf_op jit(solution)/shard_map/ppermute | solution.py:255
  27.4 0.0 copy-start
  27.4 5.6 %shard_map.128 = (f32[256,128]{1,0:T(8,128)S(1)}, bf16[59,128,128]{2,1,0:T(8,128)(2,1)S(1)}) custom-call(s32[1]{0:T(128)} %bitcast.1.z_ref, s32[1]{0:T(128)} %bitcast.2.g_ref, bf16[256,128]{1,0:T(8,128)(2,1)S(1)} %constant_dynamic-update-slice_fusion.own_ref, bf16[256,128]{1,0:T(8,128)(2,1)S(1)} %collective-permute-done.3.prev_ref, ...), custom_call_target="tpu_custom_call" | custom-call | tf_op jit(solution)/shard_map/pallas_call | solution.py:216
  33.0 0.0 all-to-all-done.grp_ref
  33.0 2.2 %shard_map.129 = (bf16[96,128]{1,0:T(8,128)(2,1)S(1)}, bf16[96,128]{1,0:T(8,128)(2,1)S(1)}, bf16[96,128]{1,0:T(8,128)(2,1)S(1)}, bf16[96,128]{1,0:T(8,128)(2,1)S(1)}) custom-call(s32[1]{0:T(128)} %bitcast.q_ref, f32[256,128]{1,0:T(8,128)S(1)} %get-tuple-element.25.acc_ref, bf16[32,16,128]{2,1,0:T(8,128)(2,1)S(1)} %all-to-all-done.grp_ref, ...), custom_call_target="tpu_custom_call" | custom-call | tf_op jit(solution)/shard_map/pallas_call | solution.py:216
  35.2 2.0 %collective-permute-start.6 = (bf16[96,128]{1,0:T(8,128)(2,1)S(1)}, bf16[96,128]{1,0:T(8,128)(2,1)S(1)}, u32[]{:S(2)}, u32[]{:S(2)}) collective-permute-start(bf16[96,128]{1,0:T(8,128)(2,1)S(1)} %get-tuple-element.32), channel_id=1, source_target_pairs={{0,1},{1,0},{2,3},{3,2},{4,5},{5,4},{6,7},{7,6},{8,9},{9,8},{10,11... | collective-permute-start | bytes 73736 | tf_op jit(solution)/shard_map/ppermute | solution.py:235
  37.2 0.9 %collective-permute-start.7 = (bf16[96,128]{1,0:T(8,128)(2,1)S(1)}, bf16[96,128]{1,0:T(8,128)(2,1)S(1)}, u32[]{:S(2)}, u32[]{:S(2)}) collective-permute-start(bf16[96,128]{1,0:T(8,128)(2,1)S(1)} %get-tuple-element.33), channel_id=1, source_target_pairs={{0,2},{1,3},{2,0},{3,1},{4,6},{5,7},{6,4},{7,5},{8,10},{9,11},{10,... | collective-permute-start | bytes 73736 | tf_op jit(solution)/shard_map/ppermute | solution.py:235
  38.1 0.8 %collective-permute-start.8 = (bf16[96,128]{1,0:T(8,128)(2,1)S(1)}, bf16[96,128]{1,0:T(8,128)(2,1)S(1)}, u32[]{:S(2)}, u32[]{:S(2)}) collective-permute-start(bf16[96,128]{1,0:T(8,128)(2,1)S(1)} %get-tuple-element.34), channel_id=1, source_target_pairs={{0,3},{1,2},{2,1},{3,0},{4,7},{5,6},{6,5},{7,4},{8,11},{9,10},{10,... | collective-permute-start | bytes 73736 | tf_op jit(solution)/shard_map/ppermute | solution.py:235
  39.0 0.0 collective-permute-done.6.b_ref
  39.0 0.9 %collective-permute-done.7.c_ref = bf16[96,128]{1,0:T(8,128)(2,1)S(1)} collective-permute-done((bf16[96,128]{1,0:T(8,128)(2,1)S(1)}, bf16[96,128]{1,0:T(8,128)(2,1)S(1)}, u32[]{:S(2)}, u32[]{:S(2)}) %collective-permute-start.7) | collective-permute-done | bytes 24608 | tf_op jit(solution)/shard_map/ppermute | solution.py:235
  39.9 1.5 %collective-permute-done.8.d_ref = bf16[96,128]{1,0:T(8,128)(2,1)S(1)} collective-permute-done((bf16[96,128]{1,0:T(8,128)(2,1)S(1)}, bf16[96,128]{1,0:T(8,128)(2,1)S(1)}, u32[]{:S(2)}, u32[]{:S(2)}) %collective-permute-start.8) | collective-permute-done | bytes 24608 | tf_op jit(solution)/shard_map/ppermute | solution.py:235
  41.4 0.0 copy-done
  41.4 1.0 %downward.1 = bf16[64,128]{1,0:T(8,128)(2,1)} custom-call(bf16[96,128]{1,0:T(8,128)(2,1)S(1)} %get-tuple-element.31.a_ref, bf16[96,128]{1,0:T(8,128)(2,1)S(1)} %collective-permute-done.6.b_ref, bf16[96,128]{1,0:T(8,128)(2,1)S(1)} %collective-permute-done.7.c_ref, bf16[96,128]{1,0:T(8,128)(2,1)S(1)} %collective-permute-done.8.d_ref, ...), custom_call_target="tpu_custom_call" | custom-call | tf_op jit(solution)/shard_map/downward/pallas_call | solution.py:267
  (3 shorter events, 0.0 us)
Async XLA Ops:
  0.0 16.2 %collective-permute-start = (bf16[64,128]{1,0:T(8,128)(2,1)}, bf16[64,128]{1,0:T(8,128)(2,1)S(1)}, u32[]{:S(2)}, u32[]{:S(2)}) collective-permute-start(bf16[64,128]{1,0:T(8,128)(2,1)} %m_ref.1), channel_id=1, source_target_pairs={{0,1},{1,0},{2,3},{3,2},{4,5},{5,4},{6,7},{7,6},{8,9},{9,8},{10,11... | collective-permute-start | bytes 49160 | tf_op jit(solution)/shard_map/ppermute | solution.py:235
  3.2 13.0 %collective-permute-start.2 = (bf16[64,128]{1,0:T(8,128)(2,1)}, bf16[64,128]{1,0:T(8,128)(2,1)S(1)}, u32[]{:S(2)}, u32[]{:S(2)}) collective-permute-start(bf16[64,128]{1,0:T(8,128)(2,1)} %m_ref.1), channel_id=1, source_target_pairs={{0,3},{1,2},{2,1},{3,0},{4,7},{5,6},{6,5},{7,4},{8,11},{9,10},{10,... | collective-permute-start | bytes 49160 | tf_op jit(solution)/shard_map/ppermute | solution.py:235
  3.2 13.0 %collective-permute-start.1 = (bf16[64,128]{1,0:T(8,128)(2,1)}, bf16[64,128]{1,0:T(8,128)(2,1)S(1)}, u32[]{:S(2)}, u32[]{:S(2)}) collective-permute-start(bf16[64,128]{1,0:T(8,128)(2,1)} %m_ref.1), channel_id=1, source_target_pairs={{0,2},{1,3},{2,0},{3,1},{4,6},{5,7},{6,4},{7,5},{8,10},{9,11},{10,... | collective-permute-start | bytes 49160 | tf_op jit(solution)/shard_map/ppermute | solution.py:235
  7.5 25.5 %all-to-all-start = ((bf16[32,16,128]{2,1,0:T(8,128)(2,1)}), bf16[32,16,128]{2,1,0:T(8,128)(2,1)S(1)}, u32[]{:S(2)}, u32[]{:S(2)}) async-start(bf16[32,16,128]{2,1,0:T(8,128)(2,1)} %get-tuple-element.26), calls=%async_computation | async-start | bytes 262144 | tf_op jit(solution)/shard_map/all_to_all | solution.py:260
  16.3 6.8 %collective-permute-start.5 = (bf16[256,128]{1,0:T(8,128)(2,1)S(1)}, bf16[256,128]{1,0:T(8,128)(2,1)S(1)}, u32[]{:S(2)}, u32[]{:S(2)}) collective-permute-start(bf16[256,128]{1,0:T(8,128)(2,1)S(1)} %constant_dynamic-update-slice_fusion.own_ref), channel_id=1, source_target_pairs={{0,0},{4,4},{8,8},{12,12},{16,16},{20,20},{24,24},{28,32},{32,28},... | collective-permute-start | bytes 196616 | tf_op jit(solution)/shard_map/ppermute | solution.py:259
  16.9 7.5 %collective-permute-start.4 = (bf16[256,128]{1,0:T(8,128)(2,1)S(1)}, bf16[256,128]{1,0:T(8,128)(2,1)S(1)}, u32[]{:S(2)}, u32[]{:S(2)}) collective-permute-start(bf16[256,128]{1,0:T(8,128)(2,1)S(1)} %constant_dynamic-update-slice_fusion.own_ref), channel_id=1, source_target_pairs={{4,0},{8,4},{12,8},{16,12},{20,16},{24,20},{28,24},{0,28},{5,1},{9... | collective-permute-start | bytes 196616 | tf_op jit(solution)/shard_map/ppermute | solution.py:256
  23.1 4.3 %collective-permute-start.3 = (bf16[256,128]{1,0:T(8,128)(2,1)S(1)}, bf16[256,128]{1,0:T(8,128)(2,1)S(1)}, u32[]{:S(2)}, u32[]{:S(2)}) collective-permute-start(bf16[256,128]{1,0:T(8,128)(2,1)S(1)} %constant_dynamic-update-slice_fusion.own_ref), channel_id=1, source_target_pairs={{0,4},{4,8},{8,12},{12,16},{16,20},{20,24},{24,28},{28,0},{1,5},{5... | collective-permute-start | bytes 196616 | tf_op jit(solution)/shard_map/ppermute | solution.py:255
  27.4 14.0 %copy-start = (bf16[8,128,128]{2,1,0:T(8,128)(2,1)S(1)}, bf16[8,128,128]{2,1,0:T(8,128)(2,1)}, u32[]{:S(2)}) copy-start(bf16[8,128,128]{2,1,0:T(8,128)(2,1)} %dn_ref.1) | copy-start | bytes 786436
  35.2 3.8 %collective-permute-start.6 = (bf16[96,128]{1,0:T(8,128)(2,1)S(1)}, bf16[96,128]{1,0:T(8,128)(2,1)S(1)}, u32[]{:S(2)}, u32[]{:S(2)}) collective-permute-start(bf16[96,128]{1,0:T(8,128)(2,1)S(1)} %get-tuple-element.32), channel_id=1, source_target_pairs={{0,1},{1,0},{2,3},{3,2},{4,5},{5,4},{6,7},{7,6},{8,9},{9,8},{10,11... | collective-permute-start | bytes 73736 | tf_op jit(solution)/shard_map/ppermute | solution.py:235
  37.2 2.7 %collective-permute-start.7 = (bf16[96,128]{1,0:T(8,128)(2,1)S(1)}, bf16[96,128]{1,0:T(8,128)(2,1)S(1)}, u32[]{:S(2)}, u32[]{:S(2)}) collective-permute-start(bf16[96,128]{1,0:T(8,128)(2,1)S(1)} %get-tuple-element.33), channel_id=1, source_target_pairs={{0,2},{1,3},{2,0},{3,1},{4,6},{5,7},{6,4},{7,5},{8,10},{9,11},{10,... | collective-permute-start | bytes 73736 | tf_op jit(solution)/shard_map/ppermute | solution.py:235
  38.1 3.3 %collective-permute-start.8 = (bf16[96,128]{1,0:T(8,128)(2,1)S(1)}, bf16[96,128]{1,0:T(8,128)(2,1)S(1)}, u32[]{:S(2)}, u32[]{:S(2)}) collective-permute-start(bf16[96,128]{1,0:T(8,128)(2,1)S(1)} %get-tuple-element.34), channel_id=1, source_target_pairs={{0,3},{1,2},{2,1},{3,0},{4,7},{5,6},{6,5},{7,4},{8,11},{9,10},{10,... | collective-permute-start | bytes 73736 | tf_op jit(solution)/shard_map/ppermute | solution.py:235

commit v4 on v3

--- a/solution.py
+++ b/solution.py
@@ -10,7 +10,6 @@
 R = 128
 NO = 79
 G = 20
-HELD = 20
 BF = jnp.bfloat16
 F32 = jnp.float32
 
@@ -19,16 +18,8 @@
     return lax.broadcasted_iota(jnp.int32, shape, dim)
 
 
-def prep_kernel(q_ref, m_ref, up_ref, src_ref, c6_ref, a5_ref, c5_ref, a4_ref, c4_ref, t5_ref, t4_ref, t6_ref, t_hbm,
-                grp_ref, low6_ref, hi6_ref, low54_ref, hi54_ref, t54_ref, tgt_ref, own_ref, t_ref, sq_ref, st_ref, sem):
-    fetch = pltpu.make_async_copy(t_hbm.at[pl.ds(0, HELD)], t_ref, sem)
-    fetch.start()
-    own_ref[0:64] = m_ref[...]
-    own_ref[64:256] = jnp.zeros((192, R), BF)
-    tgt_ref[0:NO, :] = t6_ref[...].reshape(NO, R).astype(F32)
-    tgt_ref[NO:80, :] = jnp.zeros((80 - NO, R), F32)
-    q = q_ref[0]
-    st_ref[pl.ds(0, 64), :] = m_ref[...].astype(F32)
+def upward_kernel(m_ref, up_ref, pack_ref, st_ref):
+    st_ref[...] = m_ref[...].astype(F32)
     c5 = jnp.zeros((8, R), F32)
     for c in range(8):
         rows = st_ref[pl.ds(c, 8, stride=8), :].astype(BF)
@@ -38,8 +29,28 @@
     for c in range(8):
         rows = jnp.broadcast_to(c5r[c : c + 1, :], (8, R)).astype(BF)
         c4 = c4 + jnp.dot(rows, up_ref[c], preferred_element_type=F32)
-    both = jnp.concatenate([c5, c4], axis=0).astype(BF)
-    grp_ref[...] = jnp.broadcast_to(both[None], (32, 16, R))
+    pack_ref[0:64] = m_ref[...]
+    pack_ref[64:80] = jnp.concatenate([c5, c4], axis=0).astype(BF)
+
+
+def prep_kernel(i_ref, pack_ref, src_hbm, c6_hbm, a5_hbm, c5_hbm, a4_hbm, c4_hbm, t5_hbm, t4_hbm, t6_hbm, t_hbm,
+                low6_ref, hi6_ref, low54_ref, hi54_ref, t54_ref, tgt_ref, own_ref, r0_ref, t_ref, sq_ref,
+                src_ref, c6_ref, a5_ref, c5_ref, a4_ref, c4_ref, t5_ref, t4_ref, t6_ref, sems):
+    pairs = ((src_hbm, src_ref), (c6_hbm, c6_ref), (a5_hbm, a5_ref), (c5_hbm, c5_ref),
+             (a4_hbm, a4_ref), (c4_hbm, c4_ref), (t5_hbm, t5_ref), (t4_hbm, t4_ref), (t6_hbm, t6_ref), (t_hbm, t_ref))
+    fetches = [pltpu.make_async_copy(source, place, sems.at[i]) for i, (source, place) in enumerate(pairs)]
+    for fetch in fetches:
+        fetch.start()
+    own_ref[0:64] = pack_ref[0:64]
+    own_ref[64:256] = jnp.zeros((192, R), BF)
+    r0_ref[0:16] = pack_ref[64:80]
+    r0_ref[16:64] = jnp.zeros((48, R), BF)
+    for fetch in fetches[:-1]:
+        fetch.wait()
+    i = i_ref[0]
+    q = jnp.bitwise_and(i, 3)
+    tgt_ref[0:NO, :] = t6_ref[...].reshape(NO, R).astype(F32)
+    tgt_ref[NO:80, :] = jnp.zeros((80 - NO, R), F32)
 
     sq_ref[...] = jnp.zeros((R, R), F32)
     sq_ref[0:NO, :] = src_ref[...].reshape(NO, R).astype(F32)
@@ -55,10 +66,10 @@
     low6_ref[...] = jnp.where(live(c6_ref, R), low.astype(F32), -1.0).astype(BF)
     hi6_ref[...] = jnp.right_shift(src, 8).astype(F32).astype(BF)
     a5 = a5_ref[...]
-    sq_ref[0:16, 0:NO] = (16 * jnp.right_shift(a5, 3) + jnp.bitwise_and(a5, 7)).astype(F32)
+    sq_ref[0:16, 0:NO] = (16 * jnp.bitwise_xor(jnp.right_shift(a5, 3), i) + jnp.bitwise_and(a5, 7)).astype(F32)
     code5 = sq_ref[0:16, :]
     code5 = jnp.where(live(c5_ref, 16), code5, -1.0)
-    sq_ref[0:2, 0:NO] = (16 * a4_ref[...] + 8).astype(F32)
+    sq_ref[0:2, 0:NO] = (16 * jnp.bitwise_xor(a4_ref[...], i) + 8).astype(F32)
     code4 = sq_ref[0:16, :]
     code4 = jnp.where(live(c4_ref, 16), code4, -1.0)
     code = jnp.concatenate([code5, code4], axis=0)
@@ -75,7 +86,7 @@
         part = pltpu.roll(sq_ref[pl.ds(i, 24, stride=4), :], 32 * i, 1)
         packed = jnp.where(lane >= 32 * i, part, packed)
     t54_ref[...] = packed
-    fetch.wait()
+    fetches[-1].wait()
 
 
 def hot(column, rows):
@@ -94,9 +105,7 @@
     return jnp.where(wide == down, jnp.ones((rows, R), BF), jnp.zeros((rows, R), BF))
 
 
-def fine_kernel(z_ref, g_ref, own_ref, prev_ref, next_ref, far_ref, h_ref, low_ref, hi_ref, tgt_ref, t_hbm, acc_ref, t_ref, x_ref, sem):
-    fetch = pltpu.make_async_copy(t_hbm.at[pl.ds(HELD, NO - HELD)], t_ref, sem)
-    fetch.start()
+def fine_kernel(z_ref, g_ref, own_ref, prev_ref, next_ref, far_ref, t_ref, low_ref, hi_ref, tgt_ref, acc_ref, x_ref):
     z = z_ref[0]
     x_ref[:, R : 2 * R] = own_ref[...]
 
@@ -125,15 +134,12 @@
         ops = range(first, min(first + G, NO))
         hots = jnp.concatenate([hot(low[:, o : o + 1], R) for o in ops], axis=0)
         found = jnp.dot(hots, x_ref[...], preferred_element_type=F32).astype(BF)
-        if first == HELD:
-            fetch.wait()
         ys, places = [], []
         for n, o in enumerate(ops):
             seg = jnp.broadcast_to(hi[:, o : o + 1], (R, R))
             p = found[n * R : (n + 1) * R]
             p = jnp.where(seg == jnp.asarray(0, BF), p[:, 0:R], jnp.where(seg == jnp.asarray(1, BF), p[:, R : 2 * R], p[:, 2 * R :]))
-            operator = h_ref[o] if o < HELD else t_ref[o - HELD]
-            ys.append(jnp.dot(p, operator, preferred_element_type=F32).astype(BF))
+            ys.append(jnp.dot(p, t_ref[o], preferred_element_type=F32).astype(BF))
             places.append(placing(tgt_ref[o : o + 1, :], 256))
         added = jnp.dot(jnp.concatenate(places, axis=1), jnp.concatenate(ys, axis=0), preferred_element_type=F32)
         if first == 0:
@@ -142,9 +148,12 @@
             acc_ref[...] += added
 
 
-def coarse_kernel(q_ref, acc_ref, grp_ref, h_ref, t_ref, low_ref, hi_ref, t54_ref, o0_ref, o1_ref, o2_ref, o3_ref, x_ref, far_ref):
-    x_ref[:, 0:R] = grp_ref[0:16].reshape(256, R)
-    x_ref[:, R : 2 * R] = grp_ref[16:32].reshape(256, R)
+def coarse_kernel(q_ref, acc_ref, r0_ref, r1_ref, r2_ref, r3_ref, t_ref, low_ref, hi_ref, t54_ref,
+                  o0_ref, o1_ref, o2_ref, o3_ref, x_ref, far_ref):
+    x_ref[0:64, 0:R] = r0_ref[...]
+    x_ref[64:128, 0:R] = r1_ref[...]
+    x_ref[128:256, 0:R] = r2_ref[...]
+    x_ref[:, R : 2 * R] = r3_ref[...]
     low = low_ref[...]
     hi = hi_ref[...]
     for first in range(0, NO, G):
@@ -156,8 +165,7 @@
             seg = jnp.broadcast_to(hi[:, o : o + 1], (32, R))
             p = found[n * 32 : (n + 1) * 32]
             p = jnp.where(seg == jnp.asarray(0, BF), p[:, 0:R], p[:, R:])
-            operator = h_ref[o] if o < HELD else t_ref[o - HELD]
-            ys.append(jnp.dot(p, operator, preferred_element_type=F32).astype(BF))
+            ys.append(jnp.dot(p, t_ref[o], preferred_element_type=F32).astype(BF))
         short = -len(ops) % 4
         if short:
             ys.append(jnp.zeros((32 * short, R), BF))
@@ -241,28 +249,41 @@
     z = lax.axis_index("z").astype(jnp.int32).reshape(1)
     g = lax.axis_index("g").astype(jnp.int32).reshape(1)
     groups, ring = lax.axis_size("g"), lax.axis_size("z")
-    peers = [crossed(multipoles, k) for k in (1, 2, 3)]
-    spread, low6, hi6, low54, hi54, t54, tgt, own, held = call(
+    ends = [(i * ring + ring - 1, i * ring + ring) for i in range(groups - 1)]
+    ends = dict(ends + [(j, i) for i, j in ends])
+
+    def doubled(value, bit):
+        return lax.ppermute(value, "z", [(i, i ^ bit) for i in range(ring)])
+
+    (pack,) = call(upward_kernel, [((80, R), BF)], [pltpu.VMEM((64, R), F32)], [in_hbm(multipoles), in_hbm(upward_ops)])
+    peers = [crossed(pack, k) for k in (1, 2, 3)]
+    low6, hi6, low54, hi54, t54, tgt, own, r0, held = call(
         prep_kernel,
-        [((32, 16, R), BF), ((R, R), BF), ((R, R), BF), ((32, R), BF), ((32, R), BF), ((24, R), F32), ((80, R), F32),
-         ((256, R), BF), ((HELD, R, R), BF)],
-        [pltpu.VMEM((R, R), F32), pltpu.VMEM((64, R), F32), pltpu.SemaphoreType.DMA],
-        [*map(in_hbm, (multipoles, upward_ops, rows_of(source_boxes_level6), counts_l6, anchors_l5[0].T, counts_l5,
+        [((R, R), BF), ((R, R), BF), ((32, R), BF), ((32, R), BF), ((24, R), F32), ((80, R), F32),
+         ((256, R), BF), ((64, R), BF), ((NO, R, R), BF)],
+        [pltpu.VMEM((R, R), F32),
+         pltpu.VMEM((NO, 1, R), jnp.int32), pltpu.VMEM((1, NO), jnp.int32), pltpu.VMEM((16, NO), jnp.int32),
+         pltpu.VMEM((1, NO), jnp.int32), pltpu.VMEM((2, NO), jnp.int32), pltpu.VMEM((1, NO), jnp.int32),
+         pltpu.VMEM((16, NO), jnp.int32), pltpu.VMEM((2, NO), jnp.int32), pltpu.VMEM((NO, 1, R), jnp.int32),
+         pltpu.SemaphoreType.DMA((10,))],
+        [near_core(pack), *map(in_hbm, (rows_of(source_boxes_level6), counts_l6, anchors_l5[0].T, counts_l5,
                        anchors_l4[0].T, counts_l4, target_boxes_level5[0].T, targets_l4[0].T, rows_of(targets_l6), translations))],
-        [q], far=1)
+        [4 * z + q], far=10)
     for k, peer in enumerate(peers):
-        own = lax.dynamic_update_slice(own, peer, (64 * k + 64, 0))
+        own = lax.dynamic_update_slice(own, peer[0:64], (64 * k + 64, 0))
+        r0 = lax.dynamic_update_slice(r0, peer[64:80], (16 * k + 16, 0))
+    r1 = doubled(r0, 1)
+    far = lax.ppermute(own, MORTON, [(i, ends.get(i, i)) for i in range(groups * ring)])
+    r01 = jnp.concatenate([r0, r1], axis=0)
+    r2 = doubled(r01, 2)
     before = lax.ppermute(own, "z", [(i, (i + 1) % ring) for i in range(ring)])
     after = lax.ppermute(own, "z", [((i + 1) % ring, i) for i in range(ring)])
-    ends = [(i * ring + ring - 1, i * ring + ring) for i in range(groups - 1)]
-    ends = dict(ends + [(j, i) for i, j in ends])
-    far = lax.ppermute(own, MORTON, [(i, ends.get(i, i)) for i in range(groups * ring)])
-    coarse = lax.all_to_all(spread, ("z",) + SUB, 0, 0)
-    fine, rest = call(fine_kernel, [((256, R), F32), ((NO - HELD, R, R), BF)],
-                   [pltpu.VMEM((256, 3 * R), BF), pltpu.SemaphoreType.DMA],
-                   [*map(near_core, (own, before, after, far, held, low6, hi6, tgt)), in_hbm(translations)], [z, g], far=1)
+    r02 = jnp.concatenate([r01, r2], axis=0)
+    r3 = doubled(r02, 4)
+    (fine,) = call(fine_kernel, [((256, R), F32)], [pltpu.VMEM((256, 3 * R), BF)],
+                   [*map(near_core, (own, before, after, far, held, low6, hi6, tgt))], [z, g])
     parts = call(coarse_kernel, [((96, R), BF)] * 4, [pltpu.VMEM((256, 2 * R), BF), pltpu.VMEM((48, R), F32)],
-                 [*map(near_core, (fine, coarse, held, rest, low54, hi54, t54))], [q])
+                 [*map(near_core, (fine, r0, r1, r2, r3, held, low54, hi54, t54))], [q])
     received = [crossed(parts[k], k) for k in (1, 2, 3)]
     return pl.pallas_call(
         final_kernel,

time: 42.6 us -> 41.3 us (0.969)
  the two profiles are of different devices: /device:TPU:1 before, /device:TPU:9 now
where the time goes in v4:
time: 41.3 us; the launch traced here: 41.1 us
  starting transfers between devices  21.1 us (51%)
  Pallas kernels  12 us (29%)
  waiting for transfers between devices  7.83 us (19%)
    pallas_call x4, Pallas kernels, call(): pl.pallas_call(kernel, out_shape=tuple((pltpu.VMEM(dims, kind) for dims,...  11 us
    ppermute x6, starting transfers between devices, crossed(): return lax.ppermute(value, SUB, [(i, i ^ k) for i in range(4)])  7.42 us
    ppermute x1, starting transfers between devices, local(): lax.ppermute(own, MORTON, [(i, ends.get(i, i)) for i in range(groups * ri...  5.41 us
    ppermute x3, starting transfers between devices, doubled(): return lax.ppermute(value, 'z', [(i, i ^ bit) for i in range(ring)])  4.72 us
    ppermute x1, waiting for transfers between devices, local(): lax.ppermute(own, MORTON, [(i, ends.get(i, i)) for i in range(groups * ri...  3.94 us
    ppermute x6, waiting for transfers between devices, crossed(): return lax.ppermute(value, SUB, [(i, i ^ k) for i in range(4)])  2.77 us
    ppermute x1, starting transfers between devices, local(): after = lax.ppermute(own, 'z', [((i + 1) % ring, i) for i in range(ring)])  2.12 us
    ppermute x1, starting transfers between devices, local(): before = lax.ppermute(own, 'z', [(i, (i + 1) % ring) for i in range(ring)])  1.46 us
  transfers between devices with their start and end apart: 12, of which 5 were waited for; matrix products, arithmetic and copies ran while one was open for 0% of the time, Pallas kernels for 18%

profile of v4, /device:TPU:9, one launch (start us, length us, event | category | flops | bytes accessed | tf_op | source)
XLA Modules:
  0.0 41.1 jit_solution(17192357720784610489)
XLA Ops:
  0.0 1.4 %shard_map.127.pack_ref = bf16[80,128]{1,0:T(8,128)(2,1)S(1)} custom-call(bf16[64,128]{1,0:T(8,128)(2,1)} %m_ref.1, bf16[8,128,128]{2,1,0:T(8,128)(2,1)} %up_ref.1), custom_call_target="tpu_custom_call" | custom-call | tf_op jit(solution)/shard_map/pallas_call | solution.py:224
  1.4 0.7 %collective-permute-start = (bf16[80,128]{1,0:T(8,128)(2,1)S(1)}, bf16[80,128]{1,0:T(8,128)(2,1)S(1)}, u32[]{:S(2)}, u32[]{:S(2)}) collective-permute-start(bf16[80,128]{1,0:T(8,128)(2,1)S(1)} %shard_map.127.pack_ref), channel_id=1, source_target_pairs={{0,1},{1,0},{2,3},{3,2},{4,5},{5,4},{6,7},{7,6},{8,9},{9,8},{10,11... | collective-permute-start | bytes 61448 | tf_op jit(solution)/shard_map/ppermute | solution.py:243
  2.1 1.2 %collective-permute-start.1 = (bf16[80,128]{1,0:T(8,128)(2,1)S(1)}, bf16[80,128]{1,0:T(8,128)(2,1)S(1)}, u32[]{:S(2)}, u32[]{:S(2)}) collective-permute-start(bf16[80,128]{1,0:T(8,128)(2,1)S(1)} %shard_map.127.pack_ref), channel_id=1, source_target_pairs={{0,2},{1,3},{2,0},{3,1},{4,6},{5,7},{6,4},{7,5},{8,10},{9,11},{10,... | collective-permute-start | bytes 61448 | tf_op jit(solution)/shard_map/ppermute | solution.py:243
  3.3 0.5 %collective-permute-start.2 = (bf16[80,128]{1,0:T(8,128)(2,1)S(1)}, bf16[80,128]{1,0:T(8,128)(2,1)S(1)}, u32[]{:S(2)}, u32[]{:S(2)}) collective-permute-start(bf16[80,128]{1,0:T(8,128)(2,1)S(1)} %shard_map.127.pack_ref), channel_id=1, source_target_pairs={{0,3},{1,2},{2,1},{3,0},{4,7},{5,6},{6,5},{7,4},{8,11},{9,10},{10,... | collective-permute-start | bytes 61448 | tf_op jit(solution)/shard_map/ppermute | solution.py:243
  3.8 2.0 %shard_map.128 = (bf16[128,128]{1,0:T(8,128)(2,1)S(1)}, bf16[128,128]{1,0:T(8,128)(2,1)S(1)}, bf16[32,128]{1,0:T(8,128)(2,1)S(1)}, bf16[32,128]{1,0:T(8,128)(2,1...) custom-call(s32[1]{0:T(128)S(6)} %add.7.i_ref, ...), custom_call_target="tpu_custom_call" | custom-call | tf_op jit(solution)/shard_map/pallas_call | solution.py:224
  5.8 0.0 collective-permute-done
  5.8 0.0 collective-permute-done.1
  5.9 0.7 %collective-permute-done.2 = bf16[80,128]{1,0:T(8,128)(2,1)S(1)} collective-permute-done((bf16[80,128]{1,0:T(8,128)(2,1)S(1)}, bf16[80,128]{1,0:T(8,128)(2,1)S(1)}, u32[]{:S(2)}, u32[]{:S(2)}) %collective-permute-start.2) | collective-permute-done | bytes 20512 | tf_op jit(solution)/shard_map/ppermute | solution.py:243
  6.6 1.6 %collective-permute-start.6 = (bf16[64,128]{1,0:T(8,128)(2,1)S(1)}, bf16[64,128]{1,0:T(8,128)(2,1)S(1)}, u32[]{:S(2)}, u32[]{:S(2)}) collective-permute-start(bf16[64,128]{1,0:T(8,128)(2,1)S(1)} %slice_dynamic-update-slice_fusion.3.r0_ref), channel_id=1, source_target_pairs={{0,4},{4,0},{8,12},{12,8},{16,20},{20,16},{24,28},{28,24},{1,5},{5... | collective-permute-start | bytes 49160 | tf_op jit(solution)/shard_map/ppermute | solution.py:256
  8.2 1.1 %collective-permute-done.6.r1_ref = bf16[64,128]{1,0:T(8,128)(2,1)S(1)} collective-permute-done((bf16[64,128]{1,0:T(8,128)(2,1)S(1)}, bf16[64,128]{1,0:T(8,128)(2,1)S(1)}, u32[]{:S(2)}, u32[]{:S(2)}) %collective-permute-start.6) | collective-permute-done | bytes 16416 | tf_op jit(solution)/shard_map/ppermute | solution.py:256
  9.3 3.0 %collective-permute-start.7 = (bf16[128,128]{1,0:T(8,128)(2,1)S(1)}, bf16[128,128]{1,0:T(8,128)(2,1)S(1)}, u32[]{:S(2)}, u32[]{:S(2)}) collective-permute-start(bf16[128,128]{1,0:T(8,128)(2,1)S(1)} %pad_maximum_fusion.1), channel_id=1, source_target_pairs={{0,8},{4,12},{8,0},{12,4},{16,24},{20,28},{24,16},{28,20},{1,9},{5... | collective-permute-start | bytes 98312 | tf_op jit(solution)/shard_map/ppermute | solution.py:256
  12.3 1.5 %collective-permute-start.3 = (bf16[256,128]{1,0:T(8,128)(2,1)S(1)}, bf16[256,128]{1,0:T(8,128)(2,1)S(1)}, u32[]{:S(2)}, u32[]{:S(2)}) collective-permute-start(bf16[256,128]{1,0:T(8,128)(2,1)S(1)} %slice_dynamic-update-slice_fusion.own_ref), channel_id=1, source_target_pairs={{0,4},{4,8},{8,12},{12,16},{16,20},{20,24},{24,28},{28,0},{1,5},{5... | collective-permute-start | bytes 196616 | tf_op jit(solution)/shard_map/ppermute | solution.py:279
  13.8 2.1 %collective-permute-start.4 = (bf16[256,128]{1,0:T(8,128)(2,1)S(1)}, bf16[256,128]{1,0:T(8,128)(2,1)S(1)}, u32[]{:S(2)}, u32[]{:S(2)}) collective-permute-start(bf16[256,128]{1,0:T(8,128)(2,1)S(1)} %slice_dynamic-update-slice_fusion.own_ref), channel_id=1, source_target_pairs={{4,0},{8,4},{12,8},{16,12},{20,16},{24,20},{28,24},{0,28},{5,1},{9... | collective-permute-start | bytes 196616 | tf_op jit(solution)/shard_map/ppermute | solution.py:280
  15.9 5.4 %collective-permute-start.5 = (bf16[256,128]{1,0:T(8,128)(2,1)S(1)}, bf16[256,128]{1,0:T(8,128)(2,1)S(1)}, u32[]{:S(2)}, u32[]{:S(2)}) collective-permute-start(bf16[256,128]{1,0:T(8,128)(2,1)S(1)} %slice_dynamic-update-slice_fusion.own_ref), channel_id=1, source_target_pairs={{0,0},{4,4},{8,8},{12,12},{16,16},{20,20},{24,24},{28,32},{32,28},... | collective-permute-start | bytes 196616 | tf_op jit(solution)/shard_map/ppermute | solution.py:276
  21.3 0.0 collective-permute-done.7.r2_ref
  21.4 0.1 collective-permute-start.8
  21.5 0.0 collective-permute-done.3.prev_ref
  21.5 0.0 collective-permute-done.4.next_ref
  21.5 3.9 %collective-permute-done.5.far_ref = bf16[256,128]{1,0:T(8,128)(2,1)S(1)} collective-permute-done((bf16[256,128]{1,0:T(8,128)(2,1)S(1)}, bf16[256,128]{1,0:T(8,128)(2,1)S(1)}, u32[]{:S(2)}, u32[]{:S(2)}) %collective-permute-start.5) | collective-permute-done | bytes 65568 | tf_op jit(solution)/shard_map/ppermute | solution.py:276
  25.4 0.0 copy-start
  25.4 5.4 %shard_map.129.acc_ref = f32[256,128]{1,0:T(8,128)S(1)} custom-call(s32[1]{0:T(128)} %bitcast.1.z_ref, s32[1]{0:T(128)} %bitcast.2.g_ref, bf16[256,128]{1,0:T(8,128)(2,1)S(1)} %slice_dynamic-update-slice_fusion.own_ref, bf16[256,128]{1,0:T(8,128)(2,1)S(1)} %collective-permute-done.3.prev_ref, bf16[256,128]{1,0:T(8,128)(2,1)S(1)} %collective-permute-done.4.next_ref, ...), custom_call_target="tpu_custom_call" | custom-call | tf_op jit(solution)/shard_map/pallas_call | solution.py:224
  30.8 0.0 collective-permute-done.8.r3_ref
  30.8 2.2 %shard_map.130 = (bf16[96,128]{1,0:T(8,128)(2,1)S(1)}, bf16[96,128]{1,0:T(8,128)(2,1)S(1)}, bf16[96,128]{1,0:T(8,128)(2,1)S(1)}, bf16[96,128]{1,0:T(8,128)(2,1)S(1)}) custom-call(s32[1]{0:T(128)} %bitcast.q_ref, f32[256,128]{1,0:T(8,128)S(1)} %shard_map.129.acc_ref, bf16[64,128]{1,0:T(8,128)(2,1)S(1)} %slice_dynamic-update-slice_fusion.3.r0_ref, ...), custom_call_target="tpu_custom_call" | custom-call | tf_op jit(solution)/shard_map/pallas_call | solution.py:224
  33.0 3.3 %collective-permute-start.9 = (bf16[96,128]{1,0:T(8,128)(2,1)S(1)}, bf16[96,128]{1,0:T(8,128)(2,1)S(1)}, u32[]{:S(2)}, u32[]{:S(2)}) collective-permute-start(bf16[96,128]{1,0:T(8,128)(2,1)S(1)} %get-tuple-element.28), channel_id=1, source_target_pairs={{0,1},{1,0},{2,3},{3,2},{4,5},{5,4},{6,7},{7,6},{8,9},{9,8},{10,11... | collective-permute-start | bytes 73736 | tf_op jit(solution)/shard_map/ppermute | solution.py:243
  36.3 0.6 %collective-permute-start.10 = (bf16[96,128]{1,0:T(8,128)(2,1)S(1)}, bf16[96,128]{1,0:T(8,128)(2,1)S(1)}, u32[]{:S(2)}, u32[]{:S(2)}) collective-permute-start(bf16[96,128]{1,0:T(8,128)(2,1)S(1)} %get-tuple-element.29), channel_id=1, source_target_pairs={{0,2},{1,3},{2,0},{3,1},{4,6},{5,7},{6,4},{7,5},{8,10},{9,11},{10,... | collective-permute-start | bytes 73736 | tf_op jit(solution)/shard_map/ppermute | solution.py:243
  36.9 1.2 %collective-permute-start.11 = (bf16[96,128]{1,0:T(8,128)(2,1)S(1)}, bf16[96,128]{1,0:T(8,128)(2,1)S(1)}, u32[]{:S(2)}, u32[]{:S(2)}) collective-permute-start(bf16[96,128]{1,0:T(8,128)(2,1)S(1)} %get-tuple-element.30), channel_id=1, source_target_pairs={{0,3},{1,2},{2,1},{3,0},{4,7},{5,6},{6,5},{7,4},{8,11},{9,10},{10,... | collective-permute-start | bytes 73736 | tf_op jit(solution)/shard_map/ppermute | solution.py:243
  38.0 0.0 collective-permute-done.9.b_ref
  38.1 0.9 %collective-permute-done.10.c_ref = bf16[96,128]{1,0:T(8,128)(2,1)S(1)} collective-permute-done((bf16[96,128]{1,0:T(8,128)(2,1)S(1)}, bf16[96,128]{1,0:T(8,128)(2,1)S(1)}, u32[]{:S(2)}, u32[]{:S(2)}) %collective-permute-start.10) | collective-permute-done | bytes 24608 | tf_op jit(solution)/shard_map/ppermute | solution.py:243
  39.0 1.1 %collective-permute-done.11.d_ref = bf16[96,128]{1,0:T(8,128)(2,1)S(1)} collective-permute-done((bf16[96,128]{1,0:T(8,128)(2,1)S(1)}, bf16[96,128]{1,0:T(8,128)(2,1)S(1)}, u32[]{:S(2)}, u32[]{:S(2)}) %collective-permute-start.11) | collective-permute-done | bytes 24608 | tf_op jit(solution)/shard_map/ppermute | solution.py:243
  40.1 0.0 copy-done
  40.1 1.0 %downward.1 = bf16[64,128]{1,0:T(8,128)(2,1)} custom-call(bf16[96,128]{1,0:T(8,128)(2,1)S(1)} %get-tuple-element.27.a_ref, bf16[96,128]{1,0:T(8,128)(2,1)S(1)} %collective-permute-done.9.b_ref, bf16[96,128]{1,0:T(8,128)(2,1)S(1)} %collective-permute-done.10.c_ref, bf16[96,128]{1,0:T(8,128)(2,1)S(1)} %collective-permute-done.11.d_ref, ...), custom_call_target="tpu_custom_call" | custom-call | tf_op jit(solution)/shard_map/downward/pallas_call | solution.py:288
  (8 shorter events, 0.1 us)
Async XLA Ops:
  1.4 4.4 %collective-permute-start = (bf16[80,128]{1,0:T(8,128)(2,1)S(1)}, bf16[80,128]{1,0:T(8,128)(2,1)S(1)}, u32[]{:S(2)}, u32[]{:S(2)}) collective-permute-start(bf16[80,128]{1,0:T(8,128)(2,1)S(1)} %shard_map.127.pack_ref), channel_id=1, source_target_pairs={{0,1},{1,0},{2,3},{3,2},{4,5},{5,4},{6,7},{7,6},{8,9},{9,8},{10,11... | collective-permute-start | bytes 61448 | tf_op jit(solution)/shard_map/ppermute | solution.py:243
  2.1 3.7 %collective-permute-start.1 = (bf16[80,128]{1,0:T(8,128)(2,1)S(1)}, bf16[80,128]{1,0:T(8,128)(2,1)S(1)}, u32[]{:S(2)}, u32[]{:S(2)}) collective-permute-start(bf16[80,128]{1,0:T(8,128)(2,1)S(1)} %shard_map.127.pack_ref), channel_id=1, source_target_pairs={{0,2},{1,3},{2,0},{3,1},{4,6},{5,7},{6,4},{7,5},{8,10},{9,11},{10,... | collective-permute-start | bytes 61448 | tf_op jit(solution)/shard_map/ppermute | solution.py:243
  3.3 3.2 %collective-permute-start.2 = (bf16[80,128]{1,0:T(8,128)(2,1)S(1)}, bf16[80,128]{1,0:T(8,128)(2,1)S(1)}, u32[]{:S(2)}, u32[]{:S(2)}) collective-permute-start(bf16[80,128]{1,0:T(8,128)(2,1)S(1)} %shard_map.127.pack_ref), channel_id=1, source_target_pairs={{0,3},{1,2},{2,1},{3,0},{4,7},{5,6},{6,5},{7,4},{8,11},{9,10},{10,... | collective-permute-start | bytes 61448 | tf_op jit(solution)/shard_map/ppermute | solution.py:243
  6.6 2.8 %collective-permute-start.6 = (bf16[64,128]{1,0:T(8,128)(2,1)S(1)}, bf16[64,128]{1,0:T(8,128)(2,1)S(1)}, u32[]{:S(2)}, u32[]{:S(2)}) collective-permute-start(bf16[64,128]{1,0:T(8,128)(2,1)S(1)} %slice_dynamic-update-slice_fusion.3.r0_ref), channel_id=1, source_target_pairs={{0,4},{4,0},{8,12},{12,8},{16,20},{20,16},{24,28},{28,24},{1,5},{5... | collective-permute-start | bytes 49160 | tf_op jit(solution)/shard_map/ppermute | solution.py:256
  9.3 12.0 %collective-permute-start.7 = (bf16[128,128]{1,0:T(8,128)(2,1)S(1)}, bf16[128,128]{1,0:T(8,128)(2,1)S(1)}, u32[]{:S(2)}, u32[]{:S(2)}) collective-permute-start(bf16[128,128]{1,0:T(8,128)(2,1)S(1)} %pad_maximum_fusion.1), channel_id=1, source_target_pairs={{0,8},{4,12},{8,0},{12,4},{16,24},{20,28},{24,16},{28,20},{1,9},{5... | collective-permute-start | bytes 98312 | tf_op jit(solution)/shard_map/ppermute | solution.py:256
  12.3 9.1 %collective-permute-start.3 = (bf16[256,128]{1,0:T(8,128)(2,1)S(1)}, bf16[256,128]{1,0:T(8,128)(2,1)S(1)}, u32[]{:S(2)}, u32[]{:S(2)}) collective-permute-start(bf16[256,128]{1,0:T(8,128)(2,1)S(1)} %slice_dynamic-update-slice_fusion.own_ref), channel_id=1, source_target_pairs={{0,4},{4,8},{8,12},{12,16},{16,20},{20,24},{24,28},{28,0},{1,5},{5... | collective-permute-start | bytes 196616 | tf_op jit(solution)/shard_map/ppermute | solution.py:279
  13.8 7.7 %collective-permute-start.4 = (bf16[256,128]{1,0:T(8,128)(2,1)S(1)}, bf16[256,128]{1,0:T(8,128)(2,1)S(1)}, u32[]{:S(2)}, u32[]{:S(2)}) collective-permute-start(bf16[256,128]{1,0:T(8,128)(2,1)S(1)} %slice_dynamic-update-slice_fusion.own_ref), channel_id=1, source_target_pairs={{4,0},{8,4},{12,8},{16,12},{20,16},{24,20},{28,24},{0,28},{5,1},{9... | collective-permute-start | bytes 196616 | tf_op jit(solution)/shard_map/ppermute | solution.py:280
  15.9 9.5 %collective-permute-start.5 = (bf16[256,128]{1,0:T(8,128)(2,1)S(1)}, bf16[256,128]{1,0:T(8,128)(2,1)S(1)}, u32[]{:S(2)}, u32[]{:S(2)}) collective-permute-start(bf16[256,128]{1,0:T(8,128)(2,1)S(1)} %slice_dynamic-update-slice_fusion.own_ref), channel_id=1, source_target_pairs={{0,0},{4,4},{8,8},{12,12},{16,16},{20,20},{24,24},{28,32},{32,28},... | collective-permute-start | bytes 196616 | tf_op jit(solution)/shard_map/ppermute | solution.py:276
  21.4 9.5 %collective-permute-start.8 = (bf16[256,128]{1,0:T(8,128)(2,1)S(1)}, bf16[256,128]{1,0:T(8,128)(2,1)S(1)}, u32[]{:S(2)}, u32[]{:S(2)}) collective-permute-start(bf16[256,128]{1,0:T(8,128)(2,1)S(1)} %pad_maximum_fusion), channel_id=1, source_target_pairs={{0,16},{4,20},{8,24},{12,28},{16,0},{20,4},{24,8},{28,12},{1,17},{... | collective-permute-start | bytes 196616 | tf_op jit(solution)/shard_map/ppermute | solution.py:256
  25.4 14.7 %copy-start = (bf16[8,128,128]{2,1,0:T(8,128)(2,1)S(1)}, bf16[8,128,128]{2,1,0:T(8,128)(2,1)}, u32[]{:S(2)}) copy-start(bf16[8,128,128]{2,1,0:T(8,128)(2,1)} %dn_ref.1) | copy-start | bytes 786436
  33.0 5.0 %collective-permute-start.9 = (bf16[96,128]{1,0:T(8,128)(2,1)S(1)}, bf16[96,128]{1,0:T(8,128)(2,1)S(1)}, u32[]{:S(2)}, u32[]{:S(2)}) collective-permute-start(bf16[96,128]{1,0:T(8,128)(2,1)S(1)} %get-tuple-element.28), channel_id=1, source_target_pairs={{0,1},{1,0},{2,3},{3,2},{4,5},{5,4},{6,7},{7,6},{8,9},{9,8},{10,11... | collective-permute-start | bytes 73736 | tf_op jit(solution)/shard_map/ppermute | solution.py:243
  36.3 2.7 %collective-permute-start.10 = (bf16[96,128]{1,0:T(8,128)(2,1)S(1)}, bf16[96,128]{1,0:T(8,128)(2,1)S(1)}, u32[]{:S(2)}, u32[]{:S(2)}) collective-permute-start(bf16[96,128]{1,0:T(8,128)(2,1)S(1)} %get-tuple-element.29), channel_id=1, source_target_pairs={{0,2},{1,3},{2,0},{3,1},{4,6},{5,7},{6,4},{7,5},{8,10},{9,11},{10,... | collective-permute-start | bytes 73736 | tf_op jit(solution)/shard_map/ppermute | solution.py:243
  36.9 3.3 %collective-permute-start.11 = (bf16[96,128]{1,0:T(8,128)(2,1)S(1)}, bf16[96,128]{1,0:T(8,128)(2,1)S(1)}, u32[]{:S(2)}, u32[]{:S(2)}) collective-permute-start(bf16[96,128]{1,0:T(8,128)(2,1)S(1)} %get-tuple-element.30), channel_id=1, source_target_pairs={{0,3},{1,2},{2,1},{3,0},{4,7},{5,6},{6,5},{7,4},{8,11},{9,10},{10,... | collective-permute-start | bytes 73736 | tf_op jit(solution)/shard_map/ppermute | solution.py:243

commit v5 on v4

--- a/solution.py
+++ b/solution.py
@@ -34,7 +34,7 @@
 
 
 def prep_kernel(i_ref, pack_ref, src_hbm, c6_hbm, a5_hbm, c5_hbm, a4_hbm, c4_hbm, t5_hbm, t4_hbm, t6_hbm, t_hbm,
-                low6_ref, hi6_ref, low54_ref, hi54_ref, t54_ref, tgt_ref, own_ref, r0_ref, t_ref, sq_ref,
+                low6_ref, hi6_ref, low54_ref, hi54_ref, t54_ref, tgt_ref, own_ref, t_ref, sq_ref,
                 src_ref, c6_ref, a5_ref, c5_ref, a4_ref, c4_ref, t5_ref, t4_ref, t6_ref, sems):
     pairs = ((src_hbm, src_ref), (c6_hbm, c6_ref), (a5_hbm, a5_ref), (c5_hbm, c5_ref),
              (a4_hbm, a4_ref), (c4_hbm, c4_ref), (t5_hbm, t5_ref), (t4_hbm, t4_ref), (t6_hbm, t6_ref), (t_hbm, t_ref))
@@ -43,12 +43,18 @@
         fetch.start()
     own_ref[0:64] = pack_ref[0:64]
     own_ref[64:256] = jnp.zeros((192, R), BF)
-    r0_ref[0:16] = pack_ref[64:80]
-    r0_ref[16:64] = jnp.zeros((48, R), BF)
+    own_ref[256:272] = pack_ref[64:80]
+    own_ref[272:320] = jnp.zeros((48, R), BF)
     for fetch in fetches[:-1]:
         fetch.wait()
     i = i_ref[0]
     q = jnp.bitwise_and(i, 3)
+    z = jnp.right_shift(i, 2)
+
+    def block(d):
+        ahead = jnp.bitwise_and(jnp.right_shift(d, 2) - z, 7)
+        return 64 * ahead + 16 * jnp.bitwise_xor(jnp.bitwise_and(d, 3), q)
+
     tgt_ref[0:NO, :] = t6_ref[...].reshape(NO, R).astype(F32)
     tgt_ref[NO:80, :] = jnp.zeros((80 - NO, R), F32)
 
@@ -66,10 +72,10 @@
     low6_ref[...] = jnp.where(live(c6_ref, R), low.astype(F32), -1.0).astype(BF)
     hi6_ref[...] = jnp.right_shift(src, 8).astype(F32).astype(BF)
     a5 = a5_ref[...]
-    sq_ref[0:16, 0:NO] = (16 * jnp.bitwise_xor(jnp.right_shift(a5, 3), i) + jnp.bitwise_and(a5, 7)).astype(F32)
+    sq_ref[0:16, 0:NO] = (block(jnp.right_shift(a5, 3)) + jnp.bitwise_and(a5, 7)).astype(F32)
     code5 = sq_ref[0:16, :]
     code5 = jnp.where(live(c5_ref, 16), code5, -1.0)
-    sq_ref[0:2, 0:NO] = (16 * jnp.bitwise_xor(a4_ref[...], i) + 8).astype(F32)
+    sq_ref[0:2, 0:NO] = (block(a4_ref[...]) + 8).astype(F32)
     code4 = sq_ref[0:16, :]
     code4 = jnp.where(live(c4_ref, 16), code4, -1.0)
     code = jnp.concatenate([code5, code4], axis=0)
@@ -107,7 +113,7 @@
 
 def fine_kernel(z_ref, g_ref, own_ref, prev_ref, next_ref, far_ref, t_ref, low_ref, hi_ref, tgt_ref, acc_ref, x_ref):
     z = z_ref[0]
-    x_ref[:, R : 2 * R] = own_ref[...]
+    x_ref[:, R : 2 * R] = own_ref[0:256]
 
     g = g_ref[0]
     nothing = jnp.zeros((256, R), BF)
@@ -118,7 +124,7 @@
 
     @pl.when(z > 0)
     def _():
-        x_ref[:, 0:R] = prev_ref[...]
+        x_ref[:, 0:R] = prev_ref[0:256]
 
     @pl.when(z == 7)
     def _():
@@ -126,7 +132,7 @@
 
     @pl.when(z < 7)
     def _():
-        x_ref[:, 2 * R : 3 * R] = next_ref[...]
+        x_ref[:, 2 * R : 3 * R] = next_ref[0:256]
 
     low = low_ref[...]
     hi = hi_ref[...]
@@ -148,16 +154,20 @@
             acc_ref[...] += added
 
 
-def coarse_kernel(q_ref, acc_ref, r0_ref, r1_ref, r2_ref, r3_ref, t_ref, low_ref, hi_ref, t54_ref,
+def coarse_kernel(q_ref, acc_ref, both_ref, prev_ref, next_ref, p_ref, m_ref, t_ref, low_ref, hi_ref, t54_ref,
                   o0_ref, o1_ref, o2_ref, o3_ref, x_ref, far_ref):
-    x_ref[0:64, 0:R] = r0_ref[...]
-    x_ref[64:128, 0:R] = r1_ref[...]
-    x_ref[128:256, 0:R] = r2_ref[...]
-    x_ref[:, R : 2 * R] = r3_ref[...]
+    x_ref[0:64, 0:R] = both_ref[256:320]
+    x_ref[64:128, 0:R] = next_ref[256:320]
+    x_ref[128:192, 0:R] = m_ref[64:128]
+    x_ref[192:256, 0:R] = m_ref[0:64]
+    x_ref[0:64, R : 2 * R] = m_ref[128:192]
+    x_ref[64:128, R : 2 * R] = p_ref[0:64]
+    x_ref[128:192, R : 2 * R] = p_ref[64:128]
+    x_ref[192:256, R : 2 * R] = prev_ref[256:320]
     low = low_ref[...]
     hi = hi_ref[...]
-    for first in range(0, NO, G):
-        ops = range(first, min(first + G, NO))
+    for first in range(0, NO, NO):
+        ops = range(first, min(first + NO, NO))
         hots = jnp.concatenate([hot(low[:, o : o + 1], 32) for o in ops], axis=0)
         found = jnp.dot(hots, x_ref[...], preferred_element_type=F32).astype(BF)
         ys = []
@@ -252,15 +262,12 @@
     ends = [(i * ring + ring - 1, i * ring + ring) for i in range(groups - 1)]
     ends = dict(ends + [(j, i) for i, j in ends])
 
-    def doubled(value, bit):
-        return lax.ppermute(value, "z", [(i, i ^ bit) for i in range(ring)])
-
     (pack,) = call(upward_kernel, [((80, R), BF)], [pltpu.VMEM((64, R), F32)], [in_hbm(multipoles), in_hbm(upward_ops)])
     peers = [crossed(pack, k) for k in (1, 2, 3)]
-    low6, hi6, low54, hi54, t54, tgt, own, r0, held = call(
+    low6, hi6, low54, hi54, t54, tgt, both, held = call(
         prep_kernel,
         [((R, R), BF), ((R, R), BF), ((32, R), BF), ((32, R), BF), ((24, R), F32), ((80, R), F32),
-         ((256, R), BF), ((64, R), BF), ((NO, R, R), BF)],
+         ((320, R), BF), ((NO, R, R), BF)],
         [pltpu.VMEM((R, R), F32),
          pltpu.VMEM((NO, 1, R), jnp.int32), pltpu.VMEM((1, NO), jnp.int32), pltpu.VMEM((16, NO), jnp.int32),
          pltpu.VMEM((1, NO), jnp.int32), pltpu.VMEM((2, NO), jnp.int32), pltpu.VMEM((1, NO), jnp.int32),
@@ -270,20 +277,23 @@
                        anchors_l4[0].T, counts_l4, target_boxes_level5[0].T, targets_l4[0].T, rows_of(targets_l6), translations))],
         [4 * z + q], far=10)
     for k, peer in enumerate(peers):
-        own = lax.dynamic_update_slice(own, peer[0:64], (64 * k + 64, 0))
-        r0 = lax.dynamic_update_slice(r0, peer[64:80], (16 * k + 16, 0))
-    r1 = doubled(r0, 1)
-    far = lax.ppermute(own, MORTON, [(i, ends.get(i, i)) for i in range(groups * ring)])
-    r01 = jnp.concatenate([r0, r1], axis=0)
-    r2 = doubled(r01, 2)
-    before = lax.ppermute(own, "z", [(i, (i + 1) % ring) for i in range(ring)])
-    after = lax.ppermute(own, "z", [((i + 1) % ring, i) for i in range(ring)])
-    r02 = jnp.concatenate([r01, r2], axis=0)
-    r3 = doubled(r02, 4)
+        both = lax.dynamic_update_slice(both, peer[0:64], (64 * k + 64, 0))
+        both = lax.dynamic_update_slice(both, peer[64:80], (16 * k + 272, 0))
+
+    def shifted(value, by):
+        return lax.ppermute(value, "z", [(i, (i + by) % ring) for i in range(ring)])
+
+    before = shifted(both, 1)
+    after = shifted(both, -1)
+    far = lax.ppermute(both[0:256], MORTON, [(i, ends.get(i, i)) for i in range(groups * ring)])
+    pair = jnp.concatenate([both[256:320], after[256:320]], axis=0)
+    three = jnp.concatenate([both[256:320], before[256:320], after[256:320]], axis=0)
+    minus = shifted(three, -3)
+    plus = shifted(pair, 3)
     (fine,) = call(fine_kernel, [((256, R), F32)], [pltpu.VMEM((256, 3 * R), BF)],
-                   [*map(near_core, (own, before, after, far, held, low6, hi6, tgt))], [z, g])
+                   [*map(near_core, (both, before, after, far, held, low6, hi6, tgt))], [z, g])
     parts = call(coarse_kernel, [((96, R), BF)] * 4, [pltpu.VMEM((256, 2 * R), BF), pltpu.VMEM((48, R), F32)],
-                 [*map(near_core, (fine, r0, r1, r2, r3, held, low54, hi54, t54))], [q])
+                 [*map(near_core, (fine, both, before, after, plus, minus, held, low54, hi54, t54))], [q])
     received = [crossed(parts[k], k) for k in (1, 2, 3)]
     return pl.pallas_call(
         final_kernel,

time: 41.3 us -> 35.8 us (0.87)
  waiting for transfers between devices: 7.83 us -> 2.47 us
  Pallas kernels: 12 us -> 11.1 us
  starting transfers between devices: 21.1 us -> 21.6 us
    ppermute x6 -> x5, waiting for transfers between devices: 5.06 us -> 0.01 us  [the longest x4 0.01 us: shifted(): return lax.ppermute(value, 'z', [(i, (i + by) % ring) for i in range(ring)])]
    ppermute x6 -> x5, starting transfers between devices: 13.7 us -> 15.6 us  [the longest x4 8.97 us: shifted(): return lax.ppermute(value, 'z', [(i, (i + by) % ring) for i in range(ring)])]
    ppermute x6, starting transfers between devices: 7.42 us -> 5.96 us  [crossed(): return lax.ppermute(value, SUB, [(i, i ^ k) for i in range(4)])]
    pallas_call x4, Pallas kernels: 11 us -> 10.1 us  [call(): pl.pallas_call(kernel, out_shape=tuple((pltpu.VMEM(dims, kind) for dims,...]
  transfers between devices with their start and end apart: 12 -> 11, of which waited for: 5 -> 3; matrix products, arithmetic and copies ran while one was open for 0% -> 0% of each run, Pallas kernels for 18% -> 20%
where the time goes in v5:
time: 35.8 us; the launch traced here: 35.3 us
  starting transfers between devices  21.6 us (60%)
  Pallas kernels  11.1 us (31%)
  waiting for transfers between devices  2.47 us (7%)
    pallas_call x4, Pallas kernels, call(): pl.pallas_call(kernel, out_shape=tuple((pltpu.VMEM(dims, kind) for dims,...  10.1 us
    ppermute x4, starting transfers between devices, shifted(): return lax.ppermute(value, 'z', [(i, (i + by) % ring) for i in range(ring)])  8.97 us
    ppermute x1, starting transfers between devices, local(): lax.ppermute(both[0:256], MORTON, [(i, ends.get(i, i)) for i in range(gro...  6.63 us
    ppermute x6, starting transfers between devices, crossed(): return lax.ppermute(value, SUB, [(i, i ^ k) for i in range(4)])  5.96 us
    ppermute x6, waiting for transfers between devices, crossed(): return lax.ppermute(value, SUB, [(i, i ^ k) for i in range(4)])  2.46 us
    pallas_call x1, Pallas kernels, local(): pl.pallas_call(final_kernel, out_shape=jax.ShapeDtypeStruct((64, R), BF),...  0.96 us
  transfers between devices with their start and end apart: 11, of which 3 were waited for; matrix products, arithmetic and copies ran while one was open for 0% of the time, Pallas kernels for 20%

profile of v5, /device:TPU:9, one launch (start us, length us, event | category | flops | bytes accessed | tf_op | source)
XLA Modules:
  0.0 35.3 jit_solution(11801393975298263513)
XLA Ops:
  0.0 1.4 %shard_map.127.pack_ref = bf16[80,128]{1,0:T(8,128)(2,1)S(1)} custom-call(bf16[64,128]{1,0:T(8,128)(2,1)} %m_ref.1, bf16[8,128,128]{2,1,0:T(8,128)(2,1)} %up_ref.1), custom_call_target="tpu_custom_call" | custom-call | tf_op jit(solution)/shard_map/pallas_call | solution.py:234
  1.4 0.7 %collective-permute-start = (bf16[80,128]{1,0:T(8,128)(2,1)S(1)}, bf16[80,128]{1,0:T(8,128)(2,1)S(1)}, u32[]{:S(2)}, u32[]{:S(2)}) collective-permute-start(bf16[80,128]{1,0:T(8,128)(2,1)S(1)} %shard_map.127.pack_ref), channel_id=1, source_target_pairs={{0,1},{1,0},{2,3},{3,2},{4,5},{5,4},{6,7},{7,6},{8,9},{9,8},{10,11... | collective-permute-start | bytes 61448 | tf_op jit(solution)/shard_map/ppermute | solution.py:253
  2.1 1.2 %collective-permute-start.1 = (bf16[80,128]{1,0:T(8,128)(2,1)S(1)}, bf16[80,128]{1,0:T(8,128)(2,1)S(1)}, u32[]{:S(2)}, u32[]{:S(2)}) collective-permute-start(bf16[80,128]{1,0:T(8,128)(2,1)S(1)} %shard_map.127.pack_ref), channel_id=1, source_target_pairs={{0,2},{1,3},{2,0},{3,1},{4,6},{5,7},{6,4},{7,5},{8,10},{9,11},{10,... | collective-permute-start | bytes 61448 | tf_op jit(solution)/shard_map/ppermute | solution.py:253
  3.3 0.5 %collective-permute-start.2 = (bf16[80,128]{1,0:T(8,128)(2,1)S(1)}, bf16[80,128]{1,0:T(8,128)(2,1)S(1)}, u32[]{:S(2)}, u32[]{:S(2)}) collective-permute-start(bf16[80,128]{1,0:T(8,128)(2,1)S(1)} %shard_map.127.pack_ref), channel_id=1, source_target_pairs={{0,3},{1,2},{2,1},{3,0},{4,7},{5,6},{6,5},{7,4},{8,11},{9,10},{10,... | collective-permute-start | bytes 61448 | tf_op jit(solution)/shard_map/ppermute | solution.py:253
  3.8 2.0 %shard_map.128 = (bf16[128,128]{1,0:T(8,128)(2,1)S(1)}, bf16[128,128]{1,0:T(8,128)(2,1)S(1)}, bf16[32,128]{1,0:T(8,128)(2,1)S(1)}, bf16[32,128]{1,0:T(8,128)(2,1...) custom-call(s32[1]{0:T(128)S(6)} %add.7.i_ref, ...), custom_call_target="tpu_custom_call" | custom-call | tf_op jit(solution)/shard_map/pallas_call | solution.py:234
  5.8 0.0 collective-permute-done
  5.9 0.0 collective-permute-done.1
  5.9 0.7 %collective-permute-done.2 = bf16[80,128]{1,0:T(8,128)(2,1)S(1)} collective-permute-done((bf16[80,128]{1,0:T(8,128)(2,1)S(1)}, bf16[80,128]{1,0:T(8,128)(2,1)S(1)}, u32[]{:S(2)}, u32[]{:S(2)}) %collective-permute-start.2) | collective-permute-done | bytes 20512 | tf_op jit(solution)/shard_map/ppermute | solution.py:253
  6.6 5.6 %collective-permute-start.4 = (bf16[320,128]{1,0:T(8,128)(2,1)S(1)}, bf16[320,128]{1,0:T(8,128)(2,1)S(1)}, u32[]{:S(2)}, u32[]{:S(2)}) collective-permute-start(bf16[320,128]{1,0:T(8,128)(2,1)S(1)} %slice_dynamic-update-slice_fusion.3.own_ref.both_ref), channel_id=1, source_target_pairs={{0,28},{4,0},{8,4},{12,8},{16,12},{20,16},{24,20},{28,24},{1,29},{... | collective-permute-start | bytes 245768 | tf_op jit(solution)/shard_map/ppermute | solution.py:284
  12.2 0.0 collective-permute-start.3
  12.2 6.6 %collective-permute-start.5 = (bf16[256,128]{1,0:T(8,128)(2,1)S(1)}, bf16[256,128]{1,0:T(8,128)(2,1)S(1)}, u32[]{:S(2)}, u32[]{:S(2)}) collective-permute-start(bf16[256,128]{1,0:T(8,128)(2,1)S(1)} %slice.48), channel_id=1, source_target_pairs={{0,0},{4,4},{8,8},{12,12},{16,16},{20,20},{24,24},{28,32},{32,28},... | collective-permute-start | bytes 196616 | tf_op jit(solution)/shard_map/ppermute | solution.py:288
  18.9 0.0 collective-permute-done.4.next_ref
  18.9 0.0 collective-permute-done.3.prev_ref
  18.9 0.1 collective-permute-start.7
  19.0 3.2 %collective-permute-start.6 = (bf16[128,128]{1,0:T(8,128)(2,1)S(1)}, bf16[128,128]{1,0:T(8,128)(2,1)S(1)}, u32[]{:S(2)}, u32[]{:S(2)}) collective-permute-start(bf16[128,128]{1,0:T(8,128)(2,1)S(1)} %pad_maximum_fusion.1), channel_id=1, source_target_pairs={{0,12},{4,16},{8,20},{12,24},{16,28},{20,0},{24,4},{28,8},{1,13},{... | collective-permute-start | bytes 98312 | tf_op jit(solution)/shard_map/ppermute | solution.py:284
  22.3 0.0 collective-permute-done.5.far_ref
  22.3 0.0 copy-start
  22.3 5.2 %shard_map.129.acc_ref = f32[256,128]{1,0:T(8,128)S(1)} custom-call(s32[1]{0:T(128)} %bitcast.1.z_ref, s32[1]{0:T(128)} %bitcast.2.g_ref, bf16[320,128]{1,0:T(8,128)(2,1)S(1)} %slice_dynamic-update-slice_fusion.3.own_ref.both_ref, bf16[320,128]{1,0:T(8,128)(2,1)S(1)} %collective-permute-done.3.prev_ref, ...), custom_call_target="tpu_custom_call" | custom-call | tf_op jit(solution)/shard_map/pallas_call | solution.py:234
  27.5 0.0 collective-permute-done.6.p_ref
  27.5 0.0 collective-permute-done.7.m_ref
  27.5 1.5 %shard_map.130 = (bf16[96,128]{1,0:T(8,128)(2,1)S(1)}, bf16[96,128]{1,0:T(8,128)(2,1)S(1)}, bf16[96,128]{1,0:T(8,128)(2,1)S(1)}, bf16[96,128]{1,0:T(8,128)(2,1)S(1)}) custom-call(s32[1]{0:T(128)} %bitcast.q_ref, f32[256,128]{1,0:T(8,128)S(1)} %shard_map.129.acc_ref, bf16[320,128]{1,0:T(8,128)(2,1)S(1)} %slice_dynamic-update-slice_fusion.3.own_ref.both_ref, ...), custom_call_target="tpu_custom_call" | custom-call | tf_op jit(solution)/shard_map/pallas_call | solution.py:234
  29.0 1.8 %collective-permute-start.8 = (bf16[96,128]{1,0:T(8,128)(2,1)S(1)}, bf16[96,128]{1,0:T(8,128)(2,1)S(1)}, u32[]{:S(2)}, u32[]{:S(2)}) collective-permute-start(bf16[96,128]{1,0:T(8,128)(2,1)S(1)} %get-tuple-element.26), channel_id=1, source_target_pairs={{0,1},{1,0},{2,3},{3,2},{4,5},{5,4},{6,7},{7,6},{8,9},{9,8},{10,11... | collective-permute-start | bytes 73736 | tf_op jit(solution)/shard_map/ppermute | solution.py:253
  30.8 0.0 collective-permute-start.9
  30.8 1.7 %collective-permute-start.10 = (bf16[96,128]{1,0:T(8,128)(2,1)S(1)}, bf16[96,128]{1,0:T(8,128)(2,1)S(1)}, u32[]{:S(2)}, u32[]{:S(2)}) collective-permute-start(bf16[96,128]{1,0:T(8,128)(2,1)S(1)} %get-tuple-element.28), channel_id=1, source_target_pairs={{0,3},{1,2},{2,1},{3,0},{4,7},{5,6},{6,5},{7,4},{8,11},{9,10},{10,... | collective-permute-start | bytes 73736 | tf_op jit(solution)/shard_map/ppermute | solution.py:253
  32.5 0.0 collective-permute-done.8.b_ref
  32.5 0.9 %collective-permute-done.9.c_ref = bf16[96,128]{1,0:T(8,128)(2,1)S(1)} collective-permute-done((bf16[96,128]{1,0:T(8,128)(2,1)S(1)}, bf16[96,128]{1,0:T(8,128)(2,1)S(1)}, u32[]{:S(2)}, u32[]{:S(2)}) %collective-permute-start.9) | collective-permute-done | bytes 24608 | tf_op jit(solution)/shard_map/ppermute | solution.py:253
  33.5 0.9 %collective-permute-done.10.d_ref = bf16[96,128]{1,0:T(8,128)(2,1)S(1)} collective-permute-done((bf16[96,128]{1,0:T(8,128)(2,1)S(1)}, bf16[96,128]{1,0:T(8,128)(2,1)S(1)}, u32[]{:S(2)}, u32[]{:S(2)}) %collective-permute-start.10) | collective-permute-done | bytes 24608 | tf_op jit(solution)/shard_map/ppermute | solution.py:253
  34.3 0.0 copy-done
  34.3 1.0 %downward.1 = bf16[64,128]{1,0:T(8,128)(2,1)} custom-call(bf16[96,128]{1,0:T(8,128)(2,1)S(1)} %get-tuple-element.25.a_ref, bf16[96,128]{1,0:T(8,128)(2,1)S(1)} %collective-permute-done.8.b_ref, bf16[96,128]{1,0:T(8,128)(2,1)S(1)} %collective-permute-done.9.c_ref, bf16[96,128]{1,0:T(8,128)(2,1)S(1)} %collective-permute-done.10.d_ref, ...), custom_call_target="tpu_custom_call" | custom-call | tf_op jit(solution)/shard_map/downward/pallas_call | solution.py:298
  (12 shorter events, 0.1 us)
Async XLA Ops:
  1.4 4.4 %collective-permute-start = (bf16[80,128]{1,0:T(8,128)(2,1)S(1)}, bf16[80,128]{1,0:T(8,128)(2,1)S(1)}, u32[]{:S(2)}, u32[]{:S(2)}) collective-permute-start(bf16[80,128]{1,0:T(8,128)(2,1)S(1)} %shard_map.127.pack_ref), channel_id=1, source_target_pairs={{0,1},{1,0},{2,3},{3,2},{4,5},{5,4},{6,7},{7,6},{8,9},{9,8},{10,11... | collective-permute-start | bytes 61448 | tf_op jit(solution)/shard_map/ppermute | solution.py:253
  2.1 3.7 %collective-permute-start.1 = (bf16[80,128]{1,0:T(8,128)(2,1)S(1)}, bf16[80,128]{1,0:T(8,128)(2,1)S(1)}, u32[]{:S(2)}, u32[]{:S(2)}) collective-permute-start(bf16[80,128]{1,0:T(8,128)(2,1)S(1)} %shard_map.127.pack_ref), channel_id=1, source_target_pairs={{0,2},{1,3},{2,0},{3,1},{4,6},{5,7},{6,4},{7,5},{8,10},{9,11},{10,... | collective-permute-start | bytes 61448 | tf_op jit(solution)/shard_map/ppermute | solution.py:253
  3.3 3.2 %collective-permute-start.2 = (bf16[80,128]{1,0:T(8,128)(2,1)S(1)}, bf16[80,128]{1,0:T(8,128)(2,1)S(1)}, u32[]{:S(2)}, u32[]{:S(2)}) collective-permute-start(bf16[80,128]{1,0:T(8,128)(2,1)S(1)} %shard_map.127.pack_ref), channel_id=1, source_target_pairs={{0,3},{1,2},{2,1},{3,0},{4,7},{5,6},{6,5},{7,4},{8,11},{9,10},{10,... | collective-permute-start | bytes 61448 | tf_op jit(solution)/shard_map/ppermute | solution.py:253
  6.6 12.3 %collective-permute-start.4 = (bf16[320,128]{1,0:T(8,128)(2,1)S(1)}, bf16[320,128]{1,0:T(8,128)(2,1)S(1)}, u32[]{:S(2)}, u32[]{:S(2)}) collective-permute-start(bf16[320,128]{1,0:T(8,128)(2,1)S(1)} %slice_dynamic-update-slice_fusion.3.own_ref.both_ref), channel_id=1, source_target_pairs={{0,28},{4,0},{8,4},{12,8},{16,12},{20,16},{24,20},{28,24},{1,29},{... | collective-permute-start | bytes 245768 | tf_op jit(solution)/shard_map/ppermute | solution.py:284
  12.2 6.7 %collective-permute-start.3 = (bf16[320,128]{1,0:T(8,128)(2,1)S(1)}, bf16[320,128]{1,0:T(8,128)(2,1)S(1)}, u32[]{:S(2)}, u32[]{:S(2)}) collective-permute-start(bf16[320,128]{1,0:T(8,128)(2,1)S(1)} %slice_dynamic-update-slice_fusion.3.own_ref.both_ref), channel_id=1, source_target_pairs={{0,4},{4,8},{8,12},{12,16},{16,20},{20,24},{24,28},{28,0},{1,5},{5... | collective-permute-start | bytes 245768 | tf_op jit(solution)/shard_map/ppermute | solution.py:284
  12.2 10.0 %collective-permute-start.5 = (bf16[256,128]{1,0:T(8,128)(2,1)S(1)}, bf16[256,128]{1,0:T(8,128)(2,1)S(1)}, u32[]{:S(2)}, u32[]{:S(2)}) collective-permute-start(bf16[256,128]{1,0:T(8,128)(2,1)S(1)} %slice.48), channel_id=1, source_target_pairs={{0,0},{4,4},{8,8},{12,12},{16,16},{20,20},{24,24},{28,32},{32,28},... | collective-permute-start | bytes 196616 | tf_op jit(solution)/shard_map/ppermute | solution.py:288
  18.9 8.6 %collective-permute-start.7 = (bf16[192,128]{1,0:T(8,128)(2,1)S(1)}, bf16[192,128]{1,0:T(8,128)(2,1)S(1)}, u32[]{:S(2)}, u32[]{:S(2)}) collective-permute-start(bf16[192,128]{1,0:T(8,128)(2,1)S(1)} %pad_maximum_fusion), channel_id=1, source_target_pairs={{0,20},{4,24},{8,28},{12,0},{16,4},{20,8},{24,12},{28,16},{1,21},{... | collective-permute-start | bytes 147464 | tf_op jit(solution)/shard_map/ppermute | solution.py:284
  19.0 8.5 %collective-permute-start.6 = (bf16[128,128]{1,0:T(8,128)(2,1)S(1)}, bf16[128,128]{1,0:T(8,128)(2,1)S(1)}, u32[]{:S(2)}, u32[]{:S(2)}) collective-permute-start(bf16[128,128]{1,0:T(8,128)(2,1)S(1)} %pad_maximum_fusion.1), channel_id=1, source_target_pairs={{0,12},{4,16},{8,20},{12,24},{16,28},{20,0},{24,4},{28,8},{1,13},{... | collective-permute-start | bytes 98312 | tf_op jit(solution)/shard_map/ppermute | solution.py:284
  22.3 12.1 %copy-start = (bf16[8,128,128]{2,1,0:T(8,128)(2,1)S(1)}, bf16[8,128,128]{2,1,0:T(8,128)(2,1)}, u32[]{:S(2)}) copy-start(bf16[8,128,128]{2,1,0:T(8,128)(2,1)} %dn_ref.1) | copy-start | bytes 786436
  29.0 3.6 %collective-permute-start.8 = (bf16[96,128]{1,0:T(8,128)(2,1)S(1)}, bf16[96,128]{1,0:T(8,128)(2,1)S(1)}, u32[]{:S(2)}, u32[]{:S(2)}) collective-permute-start(bf16[96,128]{1,0:T(8,128)(2,1)S(1)} %get-tuple-element.26), channel_id=1, source_target_pairs={{0,1},{1,0},{2,3},{3,2},{4,5},{5,4},{6,7},{7,6},{8,9},{9,8},{10,11... | collective-permute-start | bytes 73736 | tf_op jit(solution)/shard_map/ppermute | solution.py:253
  30.8 2.7 %collective-permute-start.9 = (bf16[96,128]{1,0:T(8,128)(2,1)S(1)}, bf16[96,128]{1,0:T(8,128)(2,1)S(1)}, u32[]{:S(2)}, u32[]{:S(2)}) collective-permute-start(bf16[96,128]{1,0:T(8,128)(2,1)S(1)} %get-tuple-element.27), channel_id=1, source_target_pairs={{0,2},{1,3},{2,0},{3,1},{4,6},{5,7},{6,4},{7,5},{8,10},{9,11},{10,... | collective-permute-start | bytes 73736 | tf_op jit(solution)/shard_map/ppermute | solution.py:253
  30.8 3.5 %collective-permute-start.10 = (bf16[96,128]{1,0:T(8,128)(2,1)S(1)}, bf16[96,128]{1,0:T(8,128)(2,1)S(1)}, u32[]{:S(2)}, u32[]{:S(2)}) collective-permute-start(bf16[96,128]{1,0:T(8,128)(2,1)S(1)} %get-tuple-element.28), channel_id=1, source_target_pairs={{0,3},{1,2},{2,1},{3,0},{4,7},{5,6},{6,5},{7,4},{8,11},{9,10},{10,... | collective-permute-start | bytes 73736 | tf_op jit(solution)/shard_map/ppermute | solution.py:253

commit v6 on v5

--- a/solution.py
+++ b/solution.py
@@ -18,42 +18,44 @@
     return lax.broadcasted_iota(jnp.int32, shape, dim)
 
 
-def upward_kernel(m_ref, up_ref, pack_ref, st_ref):
-    st_ref[...] = m_ref[...].astype(F32)
-    c5 = jnp.zeros((8, R), F32)
+def upward_kernel(m_ref, p1_ref, p2_ref, p3_ref, up_ref, both_ref, st_ref, five_ref):
+    for k, piece in enumerate((m_ref, p1_ref, p2_ref, p3_ref)):
+        both_ref[64 * k : 64 * k + 64] = piece[...]
+        st_ref[64 * k : 64 * k + 64] = piece[...].astype(F32)
+    c5 = jnp.zeros((32, R), F32)
     for c in range(8):
-        rows = st_ref[pl.ds(c, 8, stride=8), :].astype(BF)
+        rows = st_ref[pl.ds(c, 32, stride=8), :].astype(BF)
         c5 = c5 + jnp.dot(rows, up_ref[c], preferred_element_type=F32)
-    c5r = c5.astype(BF).astype(F32)
+    c5 = c5.astype(BF)
+    five_ref[...] = c5.astype(F32)
     c4 = jnp.zeros((8, R), F32)
     for c in range(8):
-        rows = jnp.broadcast_to(c5r[c : c + 1, :], (8, R)).astype(BF)
+        rows = five_ref[pl.ds(c, 4, stride=8), :]
+        rows = jnp.concatenate([rows, rows], axis=0).astype(BF)
         c4 = c4 + jnp.dot(rows, up_ref[c], preferred_element_type=F32)
-    pack_ref[0:64] = m_ref[...]
-    pack_ref[64:80] = jnp.concatenate([c5, c4], axis=0).astype(BF)
-
-
-def prep_kernel(i_ref, pack_ref, src_hbm, c6_hbm, a5_hbm, c5_hbm, a4_hbm, c4_hbm, t5_hbm, t4_hbm, t6_hbm, t_hbm,
-                low6_ref, hi6_ref, low54_ref, hi54_ref, t54_ref, tgt_ref, own_ref, t_ref, sq_ref,
+    both_ref[256:288] = c5
+    both_ref[288:304] = jnp.concatenate([c4, c4], axis=0).astype(BF)
+
+
+def prep_kernel(i_ref, m_hbm, up_hbm, src_hbm, c6_hbm, a5_hbm, c5_hbm, a4_hbm, c4_hbm, t5_hbm, t4_hbm, t6_hbm, t_hbm,
+                low6_ref, hi6_ref, low54_ref, hi54_ref, t54_ref, tgt_ref, m_ref, up_ref, t_ref, sq_ref,
                 src_ref, c6_ref, a5_ref, c5_ref, a4_ref, c4_ref, t5_ref, t4_ref, t6_ref, sems):
     pairs = ((src_hbm, src_ref), (c6_hbm, c6_ref), (a5_hbm, a5_ref), (c5_hbm, c5_ref),
-             (a4_hbm, a4_ref), (c4_hbm, c4_ref), (t5_hbm, t5_ref), (t4_hbm, t4_ref), (t6_hbm, t6_ref), (t_hbm, t_ref))
+             (a4_hbm, a4_ref), (c4_hbm, c4_ref), (t5_hbm, t5_ref), (t4_hbm, t4_ref), (t6_hbm, t6_ref),
+             (m_hbm, m_ref), (up_hbm, up_ref), (t_hbm, t_ref))
     fetches = [pltpu.make_async_copy(source, place, sems.at[i]) for i, (source, place) in enumerate(pairs)]
     for fetch in fetches:
         fetch.start()
-    own_ref[0:64] = pack_ref[0:64]
-    own_ref[64:256] = jnp.zeros((192, R), BF)
-    own_ref[256:272] = pack_ref[64:80]
-    own_ref[272:320] = jnp.zeros((48, R), BF)
-    for fetch in fetches[:-1]:
+    for fetch in fetches[:-3]:
         fetch.wait()
     i = i_ref[0]
     q = jnp.bitwise_and(i, 3)
     z = jnp.right_shift(i, 2)
 
-    def block(d):
+    def block(d, rows):
         ahead = jnp.bitwise_and(jnp.right_shift(d, 2) - z, 7)
-        return 64 * ahead + 16 * jnp.bitwise_xor(jnp.bitwise_and(d, 3), q)
+        place = 256 * jnp.right_shift(ahead, 2) + 48 * jnp.bitwise_and(ahead, 3)
+        return place + rows * jnp.bitwise_xor(jnp.bitwise_and(d, 3), q)
 
     tgt_ref[0:NO, :] = t6_ref[...].reshape(NO, R).astype(F32)
     tgt_ref[NO:80, :] = jnp.zeros((80 - NO, R), F32)
@@ -72,10 +74,10 @@
     low6_ref[...] = jnp.where(live(c6_ref, R), low.astype(F32), -1.0).astype(BF)
     hi6_ref[...] = jnp.right_shift(src, 8).astype(F32).astype(BF)
     a5 = a5_ref[...]
-    sq_ref[0:16, 0:NO] = (block(jnp.right_shift(a5, 3)) + jnp.bitwise_and(a5, 7)).astype(F32)
+    sq_ref[0:16, 0:NO] = (block(jnp.right_shift(a5, 3), 8) + jnp.bitwise_and(a5, 7)).astype(F32)
     code5 = sq_ref[0:16, :]
     code5 = jnp.where(live(c5_ref, 16), code5, -1.0)
-    sq_ref[0:2, 0:NO] = (block(a4_ref[...]) + 8).astype(F32)
+    sq_ref[0:2, 0:NO] = (block(a4_ref[...], 1) + 32).astype(F32)
     code4 = sq_ref[0:16, :]
     code4 = jnp.where(live(c4_ref, 16), code4, -1.0)
     code = jnp.concatenate([code5, code4], axis=0)
@@ -92,7 +94,8 @@
         part = pltpu.roll(sq_ref[pl.ds(i, 24, stride=4), :], 32 * i, 1)
         packed = jnp.where(lane >= 32 * i, part, packed)
     t54_ref[...] = packed
-    fetches[-1].wait()
+    for fetch in fetches[-3:]:
+        fetch.wait()
 
 
 def hot(column, rows):
@@ -156,14 +159,15 @@
 
 def coarse_kernel(q_ref, acc_ref, both_ref, prev_ref, next_ref, p_ref, m_ref, t_ref, low_ref, hi_ref, t54_ref,
                   o0_ref, o1_ref, o2_ref, o3_ref, x_ref, far_ref):
-    x_ref[0:64, 0:R] = both_ref[256:320]
-    x_ref[64:128, 0:R] = next_ref[256:320]
-    x_ref[128:192, 0:R] = m_ref[64:128]
-    x_ref[192:256, 0:R] = m_ref[0:64]
-    x_ref[0:64, R : 2 * R] = m_ref[128:192]
-    x_ref[64:128, R : 2 * R] = p_ref[0:64]
-    x_ref[128:192, R : 2 * R] = p_ref[64:128]
-    x_ref[192:256, R : 2 * R] = prev_ref[256:320]
+    x_ref[0:48, 0:R] = both_ref[256:304]
+    x_ref[48:96, 0:R] = next_ref[256:304]
+    x_ref[96:144, 0:R] = m_ref[48:96]
+    x_ref[144:192, 0:R] = m_ref[0:48]
+    x_ref[0:48, R : 2 * R] = m_ref[96:144]
+    x_ref[48:96, R : 2 * R] = p_ref[0:48]
+    x_ref[96:144, R : 2 * R] = p_ref[48:96]
+    x_ref[144:192, R : 2 * R] = prev_ref[256:304]
+    x_ref[192:256, :] = jnp.zeros((64, 2 * R), BF)
     low = low_ref[...]
     hi = hi_ref[...]
     for first in range(0, NO, NO):
@@ -262,23 +266,21 @@
     ends = [(i * ring + ring - 1, i * ring + ring) for i in range(groups - 1)]
     ends = dict(ends + [(j, i) for i, j in ends])
 
-    (pack,) = call(upward_kernel, [((80, R), BF)], [pltpu.VMEM((64, R), F32)], [in_hbm(multipoles), in_hbm(upward_ops)])
-    peers = [crossed(pack, k) for k in (1, 2, 3)]
-    low6, hi6, low54, hi54, t54, tgt, both, held = call(
+    peers = [crossed(multipoles, k) for k in (1, 2, 3)]
+    low6, hi6, low54, hi54, t54, tgt, mine, up, held = call(
         prep_kernel,
         [((R, R), BF), ((R, R), BF), ((32, R), BF), ((32, R), BF), ((24, R), F32), ((80, R), F32),
-         ((320, R), BF), ((NO, R, R), BF)],
+         ((64, R), BF), ((8, R, R), BF), ((NO, R, R), BF)],
         [pltpu.VMEM((R, R), F32),
          pltpu.VMEM((NO, 1, R), jnp.int32), pltpu.VMEM((1, NO), jnp.int32), pltpu.VMEM((16, NO), jnp.int32),
          pltpu.VMEM((1, NO), jnp.int32), pltpu.VMEM((2, NO), jnp.int32), pltpu.VMEM((1, NO), jnp.int32),
          pltpu.VMEM((16, NO), jnp.int32), pltpu.VMEM((2, NO), jnp.int32), pltpu.VMEM((NO, 1, R), jnp.int32),
-         pltpu.SemaphoreType.DMA((10,))],
-        [near_core(pack), *map(in_hbm, (rows_of(source_boxes_level6), counts_l6, anchors_l5[0].T, counts_l5,
+         pltpu.SemaphoreType.DMA((12,))],
+        [*map(in_hbm, (multipoles, upward_ops, rows_of(source_boxes_level6), counts_l6, anchors_l5[0].T, counts_l5,
                        anchors_l4[0].T, counts_l4, target_boxes_level5[0].T, targets_l4[0].T, rows_of(targets_l6), translations))],
-        [4 * z + q], far=10)
-    for k, peer in enumerate(peers):
-        both = lax.dynamic_update_slice(both, peer[0:64], (64 * k + 64, 0))
-        both = lax.dynamic_update_slice(both, peer[64:80], (16 * k + 272, 0))
+        [4 * z + q], far=12)
+    (both,) = call(upward_kernel, [((304, R), BF)], [pltpu.VMEM((256, R), F32), pltpu.VMEM((32, R), F32)],
+                   [*map(near_core, (mine, *peers, up))])
 
     def shifted(value, by):
         return lax.ppermute(value, "z", [(i, (i + by) % ring) for i in range(ring)])
@@ -286,8 +288,8 @@
     before = shifted(both, 1)
     after = shifted(both, -1)
     far = lax.ppermute(both[0:256], MORTON, [(i, ends.get(i, i)) for i in range(groups * ring)])
-    pair = jnp.concatenate([both[256:320], after[256:320]], axis=0)
-    three = jnp.concatenate([both[256:320], before[256:320], after[256:320]], axis=0)
+    pair = jnp.concatenate([both[256:304], after[256:304]], axis=0)
+    three = jnp.concatenate([both[256:304], before[256:304], after[256:304]], axis=0)
     minus = shifted(three, -3)
     plus = shifted(pair, 3)
     (fine,) = call(fine_kernel, [((256, R), F32)], [pltpu.VMEM((256, 3 * R), BF)],

time: 35.8 us -> 34.7 us (0.969)
  Pallas kernels: 11.1 us -> 10.1 us
    pallas_call x4, Pallas kernels: 10.1 us -> 9.18 us  [call(): pl.pallas_call(kernel, out_shape=tuple((pltpu.VMEM(dims, kind) for dims,...]
  transfers between devices with their start and end apart: 11 -> 11, of which waited for: 3 -> 3; matrix products, arithmetic and copies ran while one was open for 0% -> 0% of each run, Pallas kernels for 20% -> 21%
where the time goes in v6:
time: 34.7 us; the launch traced here: 34.3 us
  starting transfers between devices  21.4 us (62%)
  Pallas kernels  10.1 us (29%)
  waiting for transfers between devices  2.66 us (8%)
    pallas_call x4, Pallas kernels, call(): pl.pallas_call(kernel, out_shape=tuple((pltpu.VMEM(dims, kind) for dims,...  9.18 us
    ppermute x4, starting transfers between devices, shifted(): return lax.ppermute(value, 'z', [(i, (i + by) % ring) for i in range(ring)])  8.92 us
    ppermute x1, starting transfers between devices, local(): lax.ppermute(both[0:256], MORTON, [(i, ends.get(i, i)) for i in range(gro...  6.63 us
    ppermute x6, starting transfers between devices, crossed(): return lax.ppermute(value, SUB, [(i, i ^ k) for i in range(4)])  5.81 us
    ppermute x6, waiting for transfers between devices, crossed(): return lax.ppermute(value, SUB, [(i, i ^ k) for i in range(4)])  2.65 us
    pallas_call x1, Pallas kernels, local(): pl.pallas_call(final_kernel, out_shape=jax.ShapeDtypeStruct((64, R), BF),...  0.96 us
  transfers between devices with their start and end apart: 11, of which 3 were waited for; matrix products, arithmetic and copies ran while one was open for 0% of the time, Pallas kernels for 21%

profile of v6, /device:TPU:9, one launch (start us, length us, event | category | flops | bytes accessed | tf_op | source)
XLA Modules:
  0.0 34.3 jit_solution(16944740510598995344)
XLA Ops:
  0.0 0.7 %collective-permute-start = (bf16[64,128]{1,0:T(8,128)(2,1)}, bf16[64,128]{1,0:T(8,128)(2,1)S(1)}, u32[]{:S(2)}, u32[]{:S(2)}) collective-permute-start(bf16[64,128]{1,0:T(8,128)(2,1)} %m_hbm.1), channel_id=1, source_target_pairs={{0,1},{1,0},{2,3},{3,2},{4,5},{5,4},{6,7},{7,6},{8,9},{9,8},{10,11... | collective-permute-start | bytes 49160 | tf_op jit(solution)/shard_map/ppermute | solution.py:257
  0.7 1.2 %collective-permute-start.1 = (bf16[64,128]{1,0:T(8,128)(2,1)}, bf16[64,128]{1,0:T(8,128)(2,1)S(1)}, u32[]{:S(2)}, u32[]{:S(2)}) collective-permute-start(bf16[64,128]{1,0:T(8,128)(2,1)} %m_hbm.1), channel_id=1, source_target_pairs={{0,2},{1,3},{2,0},{3,1},{4,6},{5,7},{6,4},{7,5},{8,10},{9,11},{10,... | collective-permute-start | bytes 49160 | tf_op jit(solution)/shard_map/ppermute | solution.py:257
  1.9 0.4 %collective-permute-start.2 = (bf16[64,128]{1,0:T(8,128)(2,1)}, bf16[64,128]{1,0:T(8,128)(2,1)S(1)}, u32[]{:S(2)}, u32[]{:S(2)}) collective-permute-start(bf16[64,128]{1,0:T(8,128)(2,1)} %m_hbm.1), channel_id=1, source_target_pairs={{0,3},{1,2},{2,1},{3,0},{4,7},{5,6},{6,5},{7,4},{8,11},{9,10},{10,... | collective-permute-start | bytes 49160 | tf_op jit(solution)/shard_map/ppermute | solution.py:257
  2.3 2.1 %shard_map.127 = (bf16[128,128]{1,0:T(8,128)(2,1)S(1)}, bf16[128,128]{1,0:T(8,128)(2,1)S(1)}, bf16[32,128]{1,0:T(8,128)(2,1)S(1)}, bf16[32,128]{1,0:T(8,128)(2,1...) custom-call(s32[1]{0:T(128)S(6)} %add.7.i_ref, ...), custom_call_target="tpu_custom_call" | custom-call | tf_op jit(solution)/shard_map/pallas_call | solution.py:238
  4.4 0.0 collective-permute-done.p1_ref
  4.4 0.0 collective-permute-done.1.p2_ref
  4.4 0.8 %collective-permute-done.2.p3_ref = bf16[64,128]{1,0:T(8,128)(2,1)S(1)} collective-permute-done((bf16[64,128]{1,0:T(8,128)(2,1)}, bf16[64,128]{1,0:T(8,128)(2,1)S(1)}, u32[]{:S(2)}, u32[]{:S(2)}) %collective-permute-start.2) | collective-permute-done | bytes 16416 | tf_op jit(solution)/shard_map/ppermute | solution.py:257
  5.3 0.5 %shard_map.128.own_ref.both_ref = bf16[304,128]{1,0:T(8,128)(2,1)S(1)} custom-call(bf16[64,128]{1,0:T(8,128)(2,1)S(1)} %get-tuple-element.18.m_ref, bf16[64,128]{1,0:T(8,128)(2,1)S(1)} %collective-permute-done.p1_ref, bf16[64,128]{1,0:T(8,128)(2,1)S(1)} %collective-permute-done.1.p2_ref, bf16[64,128]{1,0:T(8,128)(2,1)S(1)} %collective-permute-done.2.p3_ref, ...), custom_call_target="tpu_custom_call" | custom-call | tf_op jit(solution)/shard_map/pallas_call | solution.py:238
  5.8 5.6 %collective-permute-start.4 = (bf16[304,128]{1,0:T(8,128)(2,1)S(1)}, bf16[304,128]{1,0:T(8,128)(2,1)S(1)}, u32[]{:S(2)}, u32[]{:S(2)}) collective-permute-start(bf16[304,128]{1,0:T(8,128)(2,1)S(1)} %shard_map.128.own_ref.both_ref), channel_id=1, source_target_pairs={{0,28},{4,0},{8,4},{12,8},{16,12},{20,16},{24,20},{28,24},{1,29},{... | collective-permute-start | bytes 233480 | tf_op jit(solution)/shard_map/ppermute | solution.py:286
  11.3 0.0 collective-permute-start.3
  11.4 6.6 %collective-permute-start.5 = (bf16[256,128]{1,0:T(8,128)(2,1)S(1)}, bf16[256,128]{1,0:T(8,128)(2,1)S(1)}, u32[]{:S(2)}, u32[]{:S(2)}) collective-permute-start(bf16[256,128]{1,0:T(8,128)(2,1)S(1)} %slice.18), channel_id=1, source_target_pairs={{0,0},{4,4},{8,8},{12,12},{16,16},{20,20},{24,24},{28,32},{32,28},... | collective-permute-start | bytes 196616 | tf_op jit(solution)/shard_map/ppermute | solution.py:290
  18.0 0.0 collective-permute-done.4.next_ref
  18.0 0.0 collective-permute-done.3.prev_ref
  18.1 0.1 collective-permute-start.7
  18.2 3.2 %collective-permute-start.6 = (bf16[96,128]{1,0:T(8,128)(2,1)S(1)}, bf16[96,128]{1,0:T(8,128)(2,1)S(1)}, u32[]{:S(2)}, u32[]{:S(2)}) collective-permute-start(bf16[96,128]{1,0:T(8,128)(2,1)S(1)} %pad_maximum_fusion.1), channel_id=1, source_target_pairs={{0,12},{4,16},{8,20},{12,24},{16,28},{20,0},{24,4},{28,8},{1,13},{... | collective-permute-start | bytes 73736 | tf_op jit(solution)/shard_map/ppermute | solution.py:286
  21.4 0.0 collective-permute-done.5.far_ref
  21.4 0.0 copy-start
  21.4 5.1 %shard_map.129.acc_ref = f32[256,128]{1,0:T(8,128)S(1)} custom-call(s32[1]{0:T(128)} %bitcast.1.z_ref, s32[1]{0:T(128)} %bitcast.2.g_ref, bf16[304,128]{1,0:T(8,128)(2,1)S(1)} %shard_map.128.own_ref.both_ref, bf16[304,128]{1,0:T(8,128)(2,1)S(1)} %collective-permute-done.3.prev_ref, bf16[304,128]{1,0:T(8,128)(2,1)S(1)} %collective-permute-done.4.next_ref, ...), custom_call_target="tpu_custom_call" | custom-call | tf_op jit(solution)/shard_map/pallas_call | solution.py:238
  26.6 0.0 collective-permute-done.6.p_ref
  26.6 0.0 collective-permute-done.7.m_ref
  26.6 1.5 %shard_map.130 = (bf16[96,128]{1,0:T(8,128)(2,1)S(1)}, bf16[96,128]{1,0:T(8,128)(2,1)S(1)}, bf16[96,128]{1,0:T(8,128)(2,1)S(1)}, bf16[96,128]{1,0:T(8,128)(2,1)S(1)}) custom-call(s32[1]{0:T(128)} %bitcast.q_ref, f32[256,128]{1,0:T(8,128)S(1)} %shard_map.129.acc_ref, bf16[304,128]{1,0:T(8,128)(2,1)S(1)} %shard_map.128.own_ref.both_ref, ...), custom_call_target="tpu_custom_call" | custom-call | tf_op jit(solution)/shard_map/pallas_call | solution.py:238
  28.1 1.8 %collective-permute-start.8 = (bf16[96,128]{1,0:T(8,128)(2,1)S(1)}, bf16[96,128]{1,0:T(8,128)(2,1)S(1)}, u32[]{:S(2)}, u32[]{:S(2)}) collective-permute-start(bf16[96,128]{1,0:T(8,128)(2,1)S(1)} %get-tuple-element.28), channel_id=1, source_target_pairs={{0,1},{1,0},{2,3},{3,2},{4,5},{5,4},{6,7},{7,6},{8,9},{9,8},{10,11... | collective-permute-start | bytes 73736 | tf_op jit(solution)/shard_map/ppermute | solution.py:257
  29.8 0.0 collective-permute-start.9
  29.8 1.7 %collective-permute-start.10 = (bf16[96,128]{1,0:T(8,128)(2,1)S(1)}, bf16[96,128]{1,0:T(8,128)(2,1)S(1)}, u32[]{:S(2)}, u32[]{:S(2)}) collective-permute-start(bf16[96,128]{1,0:T(8,128)(2,1)S(1)} %get-tuple-element.30), channel_id=1, source_target_pairs={{0,3},{1,2},{2,1},{3,0},{4,7},{5,6},{6,5},{7,4},{8,11},{9,10},{10,... | collective-permute-start | bytes 73736 | tf_op jit(solution)/shard_map/ppermute | solution.py:257
  31.6 0.0 collective-permute-done.8.b_ref
  31.6 0.9 %collective-permute-done.9.c_ref = bf16[96,128]{1,0:T(8,128)(2,1)S(1)} collective-permute-done((bf16[96,128]{1,0:T(8,128)(2,1)S(1)}, bf16[96,128]{1,0:T(8,128)(2,1)S(1)}, u32[]{:S(2)}, u32[]{:S(2)}) %collective-permute-start.9) | collective-permute-done | bytes 24608 | tf_op jit(solution)/shard_map/ppermute | solution.py:257
  32.5 0.9 %collective-permute-done.10.d_ref = bf16[96,128]{1,0:T(8,128)(2,1)S(1)} collective-permute-done((bf16[96,128]{1,0:T(8,128)(2,1)S(1)}, bf16[96,128]{1,0:T(8,128)(2,1)S(1)}, u32[]{:S(2)}, u32[]{:S(2)}) %collective-permute-start.10) | collective-permute-done | bytes 24608 | tf_op jit(solution)/shard_map/ppermute | solution.py:257
  33.4 0.0 copy-done
  33.4 1.0 %downward.1 = bf16[64,128]{1,0:T(8,128)(2,1)} custom-call(bf16[96,128]{1,0:T(8,128)(2,1)S(1)} %get-tuple-element.27.a_ref, bf16[96,128]{1,0:T(8,128)(2,1)S(1)} %collective-permute-done.8.b_ref, bf16[96,128]{1,0:T(8,128)(2,1)S(1)} %collective-permute-done.9.c_ref, bf16[96,128]{1,0:T(8,128)(2,1)S(1)} %collective-permute-done.10.d_ref, ...), custom_call_target="tpu_custom_call" | custom-call | tf_op jit(solution)/shard_map/downward/pallas_call | solution.py:300
  (6 shorter events, 0.0 us)
Async XLA Ops:
  0.0 4.4 %collective-permute-start = (bf16[64,128]{1,0:T(8,128)(2,1)}, bf16[64,128]{1,0:T(8,128)(2,1)S(1)}, u32[]{:S(2)}, u32[]{:S(2)}) collective-permute-start(bf16[64,128]{1,0:T(8,128)(2,1)} %m_hbm.1), channel_id=1, source_target_pairs={{0,1},{1,0},{2,3},{3,2},{4,5},{5,4},{6,7},{7,6},{8,9},{9,8},{10,11... | collective-permute-start | bytes 49160 | tf_op jit(solution)/shard_map/ppermute | solution.py:257
  0.7 3.7 %collective-permute-start.1 = (bf16[64,128]{1,0:T(8,128)(2,1)}, bf16[64,128]{1,0:T(8,128)(2,1)S(1)}, u32[]{:S(2)}, u32[]{:S(2)}) collective-permute-start(bf16[64,128]{1,0:T(8,128)(2,1)} %m_hbm.1), channel_id=1, source_target_pairs={{0,2},{1,3},{2,0},{3,1},{4,6},{5,7},{6,4},{7,5},{8,10},{9,11},{10,... | collective-permute-start | bytes 49160 | tf_op jit(solution)/shard_map/ppermute | solution.py:257
  1.9 3.4 %collective-permute-start.2 = (bf16[64,128]{1,0:T(8,128)(2,1)}, bf16[64,128]{1,0:T(8,128)(2,1)S(1)}, u32[]{:S(2)}, u32[]{:S(2)}) collective-permute-start(bf16[64,128]{1,0:T(8,128)(2,1)} %m_hbm.1), channel_id=1, source_target_pairs={{0,3},{1,2},{2,1},{3,0},{4,7},{5,6},{6,5},{7,4},{8,11},{9,10},{10,... | collective-permute-start | bytes 49160 | tf_op jit(solution)/shard_map/ppermute | solution.py:257
  5.8 12.3 %collective-permute-start.4 = (bf16[304,128]{1,0:T(8,128)(2,1)S(1)}, bf16[304,128]{1,0:T(8,128)(2,1)S(1)}, u32[]{:S(2)}, u32[]{:S(2)}) collective-permute-start(bf16[304,128]{1,0:T(8,128)(2,1)S(1)} %shard_map.128.own_ref.both_ref), channel_id=1, source_target_pairs={{0,28},{4,0},{8,4},{12,8},{16,12},{20,16},{24,20},{28,24},{1,29},{... | collective-permute-start | bytes 233480 | tf_op jit(solution)/shard_map/ppermute | solution.py:286
  11.3 6.7 %collective-permute-start.3 = (bf16[304,128]{1,0:T(8,128)(2,1)S(1)}, bf16[304,128]{1,0:T(8,128)(2,1)S(1)}, u32[]{:S(2)}, u32[]{:S(2)}) collective-permute-start(bf16[304,128]{1,0:T(8,128)(2,1)S(1)} %shard_map.128.own_ref.both_ref), channel_id=1, source_target_pairs={{0,4},{4,8},{8,12},{12,16},{16,20},{20,24},{24,28},{28,0},{1,5},{5... | collective-permute-start | bytes 233480 | tf_op jit(solution)/shard_map/ppermute | solution.py:286
  11.4 10.0 %collective-permute-start.5 = (bf16[256,128]{1,0:T(8,128)(2,1)S(1)}, bf16[256,128]{1,0:T(8,128)(2,1)S(1)}, u32[]{:S(2)}, u32[]{:S(2)}) collective-permute-start(bf16[256,128]{1,0:T(8,128)(2,1)S(1)} %slice.18), channel_id=1, source_target_pairs={{0,0},{4,4},{8,8},{12,12},{16,16},{20,20},{24,24},{28,32},{32,28},... | collective-permute-start | bytes 196616 | tf_op jit(solution)/shard_map/ppermute | solution.py:290
  18.1 8.5 %collective-permute-start.7 = (bf16[144,128]{1,0:T(8,128)(2,1)S(1)}, bf16[144,128]{1,0:T(8,128)(2,1)S(1)}, u32[]{:S(2)}, u32[]{:S(2)}) collective-permute-start(bf16[144,128]{1,0:T(8,128)(2,1)S(1)} %pad_maximum_fusion), channel_id=1, source_target_pairs={{0,20},{4,24},{8,28},{12,0},{16,4},{20,8},{24,12},{28,16},{1,21},{... | collective-permute-start | bytes 110600 | tf_op jit(solution)/shard_map/ppermute | solution.py:286
  18.2 8.4 %collective-permute-start.6 = (bf16[96,128]{1,0:T(8,128)(2,1)S(1)}, bf16[96,128]{1,0:T(8,128)(2,1)S(1)}, u32[]{:S(2)}, u32[]{:S(2)}) collective-permute-start(bf16[96,128]{1,0:T(8,128)(2,1)S(1)} %pad_maximum_fusion.1), channel_id=1, source_target_pairs={{0,12},{4,16},{8,20},{12,24},{16,28},{20,0},{24,4},{28,8},{1,13},{... | collective-permute-start | bytes 73736 | tf_op jit(solution)/shard_map/ppermute | solution.py:286
  21.4 11.9 %copy-start = (bf16[8,128,128]{2,1,0:T(8,128)(2,1)S(1)}, bf16[8,128,128]{2,1,0:T(8,128)(2,1)}, u32[]{:S(2)}) copy-start(bf16[8,128,128]{2,1,0:T(8,128)(2,1)} %dn_ref.1) | copy-start | bytes 786436
  28.1 3.5 %collective-permute-start.8 = (bf16[96,128]{1,0:T(8,128)(2,1)S(1)}, bf16[96,128]{1,0:T(8,128)(2,1)S(1)}, u32[]{:S(2)}, u32[]{:S(2)}) collective-permute-start(bf16[96,128]{1,0:T(8,128)(2,1)S(1)} %get-tuple-element.28), channel_id=1, source_target_pairs={{0,1},{1,0},{2,3},{3,2},{4,5},{5,4},{6,7},{7,6},{8,9},{9,8},{10,11... | collective-permute-start | bytes 73736 | tf_op jit(solution)/shard_map/ppermute | solution.py:257
  29.8 2.7 %collective-permute-start.9 = (bf16[96,128]{1,0:T(8,128)(2,1)S(1)}, bf16[96,128]{1,0:T(8,128)(2,1)S(1)}, u32[]{:S(2)}, u32[]{:S(2)}) collective-permute-start(bf16[96,128]{1,0:T(8,128)(2,1)S(1)} %get-tuple-element.29), channel_id=1, source_target_pairs={{0,2},{1,3},{2,0},{3,1},{4,6},{5,7},{6,4},{7,5},{8,10},{9,11},{10,... | collective-permute-start | bytes 73736 | tf_op jit(solution)/shard_map/ppermute | solution.py:257
  29.8 3.5 %collective-permute-start.10 = (bf16[96,128]{1,0:T(8,128)(2,1)S(1)}, bf16[96,128]{1,0:T(8,128)(2,1)S(1)}, u32[]{:S(2)}, u32[]{:S(2)}) collective-permute-start(bf16[96,128]{1,0:T(8,128)(2,1)S(1)} %get-tuple-element.30), channel_id=1, source_target_pairs={{0,3},{1,2},{2,1},{3,0},{4,7},{5,6},{6,5},{7,4},{8,11},{9,10},{10,... | collective-permute-start | bytes 73736 | tf_op jit(solution)/shard_map/ppermute | solution.py:257

commit v7 on v6

--- a/solution.py
+++ b/solution.py
@@ -266,7 +266,9 @@
     ends = [(i * ring + ring - 1, i * ring + ring) for i in range(groups - 1)]
     ends = dict(ends + [(j, i) for i, j in ends])
 
-    peers = [crossed(multipoles, k) for k in (1, 2, 3)]
+    peers = []
+    for k in (1, 2, 3):
+        peers.append(crossed(multipoles, k))
     low6, hi6, low54, hi54, t54, tgt, mine, up, held = call(
         prep_kernel,
         [((R, R), BF), ((R, R), BF), ((32, R), BF), ((32, R), BF), ((24, R), F32), ((80, R), F32),
@@ -296,7 +298,9 @@
                    [*map(near_core, (both, before, after, far, held, low6, hi6, tgt))], [z, g])
     parts = call(coarse_kernel, [((96, R), BF)] * 4, [pltpu.VMEM((256, 2 * R), BF), pltpu.VMEM((48, R), F32)],
                  [*map(near_core, (fine, both, before, after, plus, minus, held, low54, hi54, t54))], [q])
-    received = [crossed(parts[k], k) for k in (1, 2, 3)]
+    received = []
+    for k in (1, 2, 3):
+        received.append(crossed(parts[k], k))
     return pl.pallas_call(
         final_kernel,
         out_shape=jax.ShapeDtypeStruct((64, R), BF),

time: 34.7 us -> 34.7 us (level)
  no operation moved by 1% of the time
where the time goes in v7:
time: 34.7 us; the launch traced here: 34.3 us
  starting transfers between devices  21.4 us (62%)
  Pallas kernels  10.1 us (29%)
  waiting for transfers between devices  2.66 us (8%)
    pallas_call x4, Pallas kernels, call(): pl.pallas_call(kernel, out_shape=tuple((pltpu.VMEM(dims, kind) for dims,...  9.18 us
    ppermute x4, starting transfers between devices, shifted(): return lax.ppermute(value, 'z', [(i, (i + by) % ring) for i in range(ring)])  8.92 us
    ppermute x1, starting transfers between devices, local(): lax.ppermute(both[0:256], MORTON, [(i, ends.get(i, i)) for i in range(gro...  6.63 us
    ppermute x6, starting transfers between devices, crossed(): return lax.ppermute(value, SUB, [(i, i ^ k) for i in range(4)])  5.81 us
    ppermute x6, waiting for transfers between devices, crossed(): return lax.ppermute(value, SUB, [(i, i ^ k) for i in range(4)])  2.65 us
    pallas_call x1, Pallas kernels, local(): pl.pallas_call(final_kernel, out_shape=jax.ShapeDtypeStruct((64, R), BF),...  0.96 us
  transfers between devices with their start and end apart: 11, of which 3 were waited for; matrix products, arithmetic and copies ran while one was open for 0% of the time, Pallas kernels for 21%

profile of v7, /device:TPU:9, one launch (start us, length us, event | category | flops | bytes accessed | tf_op | source)
XLA Modules:
  0.0 34.3 jit_solution(16944740510598995344)
XLA Ops:
  0.0 0.7 %collective-permute-start = (bf16[64,128]{1,0:T(8,128)(2,1)}, bf16[64,128]{1,0:T(8,128)(2,1)S(1)}, u32[]{:S(2)}, u32[]{:S(2)}) collective-permute-start(bf16[64,128]{1,0:T(8,128)(2,1)} %m_hbm.1), channel_id=1, source_target_pairs={{0,1},{1,0},{2,3},{3,2},{4,5},{5,4},{6,7},{7,6},{8,9},{9,8},{10,11... | collective-permute-start | bytes 49160 | tf_op jit(solution)/shard_map/ppermute | solution.py:257
  0.7 1.2 %collective-permute-start.1 = (bf16[64,128]{1,0:T(8,128)(2,1)}, bf16[64,128]{1,0:T(8,128)(2,1)S(1)}, u32[]{:S(2)}, u32[]{:S(2)}) collective-permute-start(bf16[64,128]{1,0:T(8,128)(2,1)} %m_hbm.1), channel_id=1, source_target_pairs={{0,2},{1,3},{2,0},{3,1},{4,6},{5,7},{6,4},{7,5},{8,10},{9,11},{10,... | collective-permute-start | bytes 49160 | tf_op jit(solution)/shard_map/ppermute | solution.py:257
  1.9 0.4 %collective-permute-start.2 = (bf16[64,128]{1,0:T(8,128)(2,1)}, bf16[64,128]{1,0:T(8,128)(2,1)S(1)}, u32[]{:S(2)}, u32[]{:S(2)}) collective-permute-start(bf16[64,128]{1,0:T(8,128)(2,1)} %m_hbm.1), channel_id=1, source_target_pairs={{0,3},{1,2},{2,1},{3,0},{4,7},{5,6},{6,5},{7,4},{8,11},{9,10},{10,... | collective-permute-start | bytes 49160 | tf_op jit(solution)/shard_map/ppermute | solution.py:257
  2.3 2.1 %shard_map.127 = (bf16[128,128]{1,0:T(8,128)(2,1)S(1)}, bf16[128,128]{1,0:T(8,128)(2,1)S(1)}, bf16[32,128]{1,0:T(8,128)(2,1)S(1)}, bf16[32,128]{1,0:T(8,128)(2,1...) custom-call(s32[1]{0:T(128)S(6)} %add.7.i_ref, ...), custom_call_target="tpu_custom_call" | custom-call | tf_op jit(solution)/shard_map/pallas_call | solution.py:238
  4.4 0.0 collective-permute-done.p1_ref
  4.4 0.0 collective-permute-done.1.p2_ref
  4.4 0.8 %collective-permute-done.2.p3_ref = bf16[64,128]{1,0:T(8,128)(2,1)S(1)} collective-permute-done((bf16[64,128]{1,0:T(8,128)(2,1)}, bf16[64,128]{1,0:T(8,128)(2,1)S(1)}, u32[]{:S(2)}, u32[]{:S(2)}) %collective-permute-start.2) | collective-permute-done | bytes 16416 | tf_op jit(solution)/shard_map/ppermute | solution.py:257
  5.3 0.5 %shard_map.128.own_ref.both_ref = bf16[304,128]{1,0:T(8,128)(2,1)S(1)} custom-call(bf16[64,128]{1,0:T(8,128)(2,1)S(1)} %get-tuple-element.18.m_ref, bf16[64,128]{1,0:T(8,128)(2,1)S(1)} %collective-permute-done.p1_ref, bf16[64,128]{1,0:T(8,128)(2,1)S(1)} %collective-permute-done.1.p2_ref, bf16[64,128]{1,0:T(8,128)(2,1)S(1)} %collective-permute-done.2.p3_ref, ...), custom_call_target="tpu_custom_call" | custom-call | tf_op jit(solution)/shard_map/pallas_call | solution.py:238
  5.8 5.6 %collective-permute-start.4 = (bf16[304,128]{1,0:T(8,128)(2,1)S(1)}, bf16[304,128]{1,0:T(8,128)(2,1)S(1)}, u32[]{:S(2)}, u32[]{:S(2)}) collective-permute-start(bf16[304,128]{1,0:T(8,128)(2,1)S(1)} %shard_map.128.own_ref.both_ref), channel_id=1, source_target_pairs={{0,28},{4,0},{8,4},{12,8},{16,12},{20,16},{24,20},{28,24},{1,29},{... | collective-permute-start | bytes 233480 | tf_op jit(solution)/shard_map/ppermute | solution.py:288
  11.3 0.0 collective-permute-start.3
  11.4 6.6 %collective-permute-start.5 = (bf16[256,128]{1,0:T(8,128)(2,1)S(1)}, bf16[256,128]{1,0:T(8,128)(2,1)S(1)}, u32[]{:S(2)}, u32[]{:S(2)}) collective-permute-start(bf16[256,128]{1,0:T(8,128)(2,1)S(1)} %slice.18), channel_id=1, source_target_pairs={{0,0},{4,4},{8,8},{12,12},{16,16},{20,20},{24,24},{28,32},{32,28},... | collective-permute-start | bytes 196616 | tf_op jit(solution)/shard_map/ppermute | solution.py:292
  18.0 0.0 collective-permute-done.4.next_ref
  18.0 0.0 collective-permute-done.3.prev_ref
  18.1 0.1 collective-permute-start.7
  18.2 3.2 %collective-permute-start.6 = (bf16[96,128]{1,0:T(8,128)(2,1)S(1)}, bf16[96,128]{1,0:T(8,128)(2,1)S(1)}, u32[]{:S(2)}, u32[]{:S(2)}) collective-permute-start(bf16[96,128]{1,0:T(8,128)(2,1)S(1)} %pad_maximum_fusion.1), channel_id=1, source_target_pairs={{0,12},{4,16},{8,20},{12,24},{16,28},{20,0},{24,4},{28,8},{1,13},{... | collective-permute-start | bytes 73736 | tf_op jit(solution)/shard_map/ppermute | solution.py:288
  21.4 0.0 collective-permute-done.5.far_ref
  21.4 0.0 copy-start
  21.4 5.1 %shard_map.129.acc_ref = f32[256,128]{1,0:T(8,128)S(1)} custom-call(s32[1]{0:T(128)} %bitcast.1.z_ref, s32[1]{0:T(128)} %bitcast.2.g_ref, bf16[304,128]{1,0:T(8,128)(2,1)S(1)} %shard_map.128.own_ref.both_ref, bf16[304,128]{1,0:T(8,128)(2,1)S(1)} %collective-permute-done.3.prev_ref, bf16[304,128]{1,0:T(8,128)(2,1)S(1)} %collective-permute-done.4.next_ref, ...), custom_call_target="tpu_custom_call" | custom-call | tf_op jit(solution)/shard_map/pallas_call | solution.py:238
  26.6 0.0 collective-permute-done.6.p_ref
  26.6 0.0 collective-permute-done.7.m_ref
  26.6 1.5 %shard_map.130 = (bf16[96,128]{1,0:T(8,128)(2,1)S(1)}, bf16[96,128]{1,0:T(8,128)(2,1)S(1)}, bf16[96,128]{1,0:T(8,128)(2,1)S(1)}, bf16[96,128]{1,0:T(8,128)(2,1)S(1)}) custom-call(s32[1]{0:T(128)} %bitcast.q_ref, f32[256,128]{1,0:T(8,128)S(1)} %shard_map.129.acc_ref, bf16[304,128]{1,0:T(8,128)(2,1)S(1)} %shard_map.128.own_ref.both_ref, ...), custom_call_target="tpu_custom_call" | custom-call | tf_op jit(solution)/shard_map/pallas_call | solution.py:238
  28.1 1.8 %collective-permute-start.8 = (bf16[96,128]{1,0:T(8,128)(2,1)S(1)}, bf16[96,128]{1,0:T(8,128)(2,1)S(1)}, u32[]{:S(2)}, u32[]{:S(2)}) collective-permute-start(bf16[96,128]{1,0:T(8,128)(2,1)S(1)} %get-tuple-element.28), channel_id=1, source_target_pairs={{0,1},{1,0},{2,3},{3,2},{4,5},{5,4},{6,7},{7,6},{8,9},{9,8},{10,11... | collective-permute-start | bytes 73736 | tf_op jit(solution)/shard_map/ppermute | solution.py:257
  29.8 0.0 collective-permute-start.9
  29.8 1.7 %collective-permute-start.10 = (bf16[96,128]{1,0:T(8,128)(2,1)S(1)}, bf16[96,128]{1,0:T(8,128)(2,1)S(1)}, u32[]{:S(2)}, u32[]{:S(2)}) collective-permute-start(bf16[96,128]{1,0:T(8,128)(2,1)S(1)} %get-tuple-element.30), channel_id=1, source_target_pairs={{0,3},{1,2},{2,1},{3,0},{4,7},{5,6},{6,5},{7,4},{8,11},{9,10},{10,... | collective-permute-start | bytes 73736 | tf_op jit(solution)/shard_map/ppermute | solution.py:257
  31.6 0.0 collective-permute-done.8.b_ref
  31.6 0.9 %collective-permute-done.9.c_ref = bf16[96,128]{1,0:T(8,128)(2,1)S(1)} collective-permute-done((bf16[96,128]{1,0:T(8,128)(2,1)S(1)}, bf16[96,128]{1,0:T(8,128)(2,1)S(1)}, u32[]{:S(2)}, u32[]{:S(2)}) %collective-permute-start.9) | collective-permute-done | bytes 24608 | tf_op jit(solution)/shard_map/ppermute | solution.py:257
  32.5 0.9 %collective-permute-done.10.d_ref = bf16[96,128]{1,0:T(8,128)(2,1)S(1)} collective-permute-done((bf16[96,128]{1,0:T(8,128)(2,1)S(1)}, bf16[96,128]{1,0:T(8,128)(2,1)S(1)}, u32[]{:S(2)}, u32[]{:S(2)}) %collective-permute-start.10) | collective-permute-done | bytes 24608 | tf_op jit(solution)/shard_map/ppermute | solution.py:257
  33.4 0.0 copy-done
  33.4 1.0 %downward.1 = bf16[64,128]{1,0:T(8,128)(2,1)} custom-call(bf16[96,128]{1,0:T(8,128)(2,1)S(1)} %get-tuple-element.27.a_ref, bf16[96,128]{1,0:T(8,128)(2,1)S(1)} %collective-permute-done.8.b_ref, bf16[96,128]{1,0:T(8,128)(2,1)S(1)} %collective-permute-done.9.c_ref, bf16[96,128]{1,0:T(8,128)(2,1)S(1)} %collective-permute-done.10.d_ref, ...), custom_call_target="tpu_custom_call" | custom-call | tf_op jit(solution)/shard_map/downward/pallas_call | solution.py:304
  (6 shorter events, 0.0 us)
Async XLA Ops:
  0.0 4.4 %collective-permute-start = (bf16[64,128]{1,0:T(8,128)(2,1)}, bf16[64,128]{1,0:T(8,128)(2,1)S(1)}, u32[]{:S(2)}, u32[]{:S(2)}) collective-permute-start(bf16[64,128]{1,0:T(8,128)(2,1)} %m_hbm.1), channel_id=1, source_target_pairs={{0,1},{1,0},{2,3},{3,2},{4,5},{5,4},{6,7},{7,6},{8,9},{9,8},{10,11... | collective-permute-start | bytes 49160 | tf_op jit(solution)/shard_map/ppermute | solution.py:257
  0.7 3.7 %collective-permute-start.1 = (bf16[64,128]{1,0:T(8,128)(2,1)}, bf16[64,128]{1,0:T(8,128)(2,1)S(1)}, u32[]{:S(2)}, u32[]{:S(2)}) collective-permute-start(bf16[64,128]{1,0:T(8,128)(2,1)} %m_hbm.1), channel_id=1, source_target_pairs={{0,2},{1,3},{2,0},{3,1},{4,6},{5,7},{6,4},{7,5},{8,10},{9,11},{10,... | collective-permute-start | bytes 49160 | tf_op jit(solution)/shard_map/ppermute | solution.py:257
  1.9 3.4 %collective-permute-start.2 = (bf16[64,128]{1,0:T(8,128)(2,1)}, bf16[64,128]{1,0:T(8,128)(2,1)S(1)}, u32[]{:S(2)}, u32[]{:S(2)}) collective-permute-start(bf16[64,128]{1,0:T(8,128)(2,1)} %m_hbm.1), channel_id=1, source_target_pairs={{0,3},{1,2},{2,1},{3,0},{4,7},{5,6},{6,5},{7,4},{8,11},{9,10},{10,... | collective-permute-start | bytes 49160 | tf_op jit(solution)/shard_map/ppermute | solution.py:257
  5.8 12.3 %collective-permute-start.4 = (bf16[304,128]{1,0:T(8,128)(2,1)S(1)}, bf16[304,128]{1,0:T(8,128)(2,1)S(1)}, u32[]{:S(2)}, u32[]{:S(2)}) collective-permute-start(bf16[304,128]{1,0:T(8,128)(2,1)S(1)} %shard_map.128.own_ref.both_ref), channel_id=1, source_target_pairs={{0,28},{4,0},{8,4},{12,8},{16,12},{20,16},{24,20},{28,24},{1,29},{... | collective-permute-start | bytes 233480 | tf_op jit(solution)/shard_map/ppermute | solution.py:288
  11.3 6.7 %collective-permute-start.3 = (bf16[304,128]{1,0:T(8,128)(2,1)S(1)}, bf16[304,128]{1,0:T(8,128)(2,1)S(1)}, u32[]{:S(2)}, u32[]{:S(2)}) collective-permute-start(bf16[304,128]{1,0:T(8,128)(2,1)S(1)} %shard_map.128.own_ref.both_ref), channel_id=1, source_target_pairs={{0,4},{4,8},{8,12},{12,16},{16,20},{20,24},{24,28},{28,0},{1,5},{5... | collective-permute-start | bytes 233480 | tf_op jit(solution)/shard_map/ppermute | solution.py:288
  11.4 10.0 %collective-permute-start.5 = (bf16[256,128]{1,0:T(8,128)(2,1)S(1)}, bf16[256,128]{1,0:T(8,128)(2,1)S(1)}, u32[]{:S(2)}, u32[]{:S(2)}) collective-permute-start(bf16[256,128]{1,0:T(8,128)(2,1)S(1)} %slice.18), channel_id=1, source_target_pairs={{0,0},{4,4},{8,8},{12,12},{16,16},{20,20},{24,24},{28,32},{32,28},... | collective-permute-start | bytes 196616 | tf_op jit(solution)/shard_map/ppermute | solution.py:292
  18.1 8.5 %collective-permute-start.7 = (bf16[144,128]{1,0:T(8,128)(2,1)S(1)}, bf16[144,128]{1,0:T(8,128)(2,1)S(1)}, u32[]{:S(2)}, u32[]{:S(2)}) collective-permute-start(bf16[144,128]{1,0:T(8,128)(2,1)S(1)} %pad_maximum_fusion), channel_id=1, source_target_pairs={{0,20},{4,24},{8,28},{12,0},{16,4},{20,8},{24,12},{28,16},{1,21},{... | collective-permute-start | bytes 110600 | tf_op jit(solution)/shard_map/ppermute | solution.py:288
  18.2 8.4 %collective-permute-start.6 = (bf16[96,128]{1,0:T(8,128)(2,1)S(1)}, bf16[96,128]{1,0:T(8,128)(2,1)S(1)}, u32[]{:S(2)}, u32[]{:S(2)}) collective-permute-start(bf16[96,128]{1,0:T(8,128)(2,1)S(1)} %pad_maximum_fusion.1), channel_id=1, source_target_pairs={{0,12},{4,16},{8,20},{12,24},{16,28},{20,0},{24,4},{28,8},{1,13},{... | collective-permute-start | bytes 73736 | tf_op jit(solution)/shard_map/ppermute | solution.py:288
  21.4 11.9 %copy-start = (bf16[8,128,128]{2,1,0:T(8,128)(2,1)S(1)}, bf16[8,128,128]{2,1,0:T(8,128)(2,1)}, u32[]{:S(2)}) copy-start(bf16[8,128,128]{2,1,0:T(8,128)(2,1)} %dn_ref.1) | copy-start | bytes 786436
  28.1 3.5 %collective-permute-start.8 = (bf16[96,128]{1,0:T(8,128)(2,1)S(1)}, bf16[96,128]{1,0:T(8,128)(2,1)S(1)}, u32[]{:S(2)}, u32[]{:S(2)}) collective-permute-start(bf16[96,128]{1,0:T(8,128)(2,1)S(1)} %get-tuple-element.28), channel_id=1, source_target_pairs={{0,1},{1,0},{2,3},{3,2},{4,5},{5,4},{6,7},{7,6},{8,9},{9,8},{10,11... | collective-permute-start | bytes 73736 | tf_op jit(solution)/shard_map/ppermute | solution.py:257
  29.8 2.7 %collective-permute-start.9 = (bf16[96,128]{1,0:T(8,128)(2,1)S(1)}, bf16[96,128]{1,0:T(8,128)(2,1)S(1)}, u32[]{:S(2)}, u32[]{:S(2)}) collective-permute-start(bf16[96,128]{1,0:T(8,128)(2,1)S(1)} %get-tuple-element.29), channel_id=1, source_target_pairs={{0,2},{1,3},{2,0},{3,1},{4,6},{5,7},{6,4},{7,5},{8,10},{9,11},{10,... | collective-permute-start | bytes 73736 | tf_op jit(solution)/shard_map/ppermute | solution.py:257
  29.8 3.5 %collective-permute-start.10 = (bf16[96,128]{1,0:T(8,128)(2,1)S(1)}, bf16[96,128]{1,0:T(8,128)(2,1)S(1)}, u32[]{:S(2)}, u32[]{:S(2)}) collective-permute-start(bf16[96,128]{1,0:T(8,128)(2,1)S(1)} %get-tuple-element.30), channel_id=1, source_target_pairs={{0,3},{1,2},{2,1},{3,0},{4,7},{5,6},{6,5},{7,4},{8,11},{9,10},{10,... | collective-permute-start | bytes 73736 | tf_op jit(solution)/shard_map/ppermute | solution.py:257

commit v8 on v7

--- a/solution.py
+++ b/solution.py
@@ -201,12 +201,11 @@
         small = jnp.concatenate([five, four], axis=0)
         top = small.astype(BF)
         out[64:80] = top
-        out[80:96] = (small - top.astype(F32)).astype(BF)
 
 
 def final_kernel(a_ref, b_ref, c_ref, d_ref, dn_ref, out_ref, s_ref):
     total = (a_ref[...].astype(F32) + b_ref[...].astype(F32)) + (c_ref[...].astype(F32) + d_ref[...].astype(F32))
-    small = total[64:80] + total[80:96]
+    small = total[64:80]
     far5 = small[0:8]
     local4 = small[8:16].astype(BF)
     row = iota((8, R), 0)
@@ -296,7 +295,7 @@
     plus = shifted(pair, 3)
     (fine,) = call(fine_kernel, [((256, R), F32)], [pltpu.VMEM((256, 3 * R), BF)],
                    [*map(near_core, (both, before, after, far, held, low6, hi6, tgt))], [z, g])
-    parts = call(coarse_kernel, [((96, R), BF)] * 4, [pltpu.VMEM((256, 2 * R), BF), pltpu.VMEM((48, R), F32)],
+    parts = call(coarse_kernel, [((80, R), BF)] * 4, [pltpu.VMEM((256, 2 * R), BF), pltpu.VMEM((48, R), F32)],
                  [*map(near_core, (fine, both, before, after, plus, minus, held, low54, hi54, t54))], [q])
     received = []
     for k in (1, 2, 3):

time: 34.7 us -> 34.7 us (level)
  no operation moved by 1% of the time
where the time goes in v8:
time: 34.7 us; the launch traced here: 34.3 us
  starting transfers between devices  21.4 us (62%)
  Pallas kernels  10.1 us (29%)
  waiting for transfers between devices  2.62 us (8%)
    pallas_call x4, Pallas kernels, call(): pl.pallas_call(kernel, out_shape=tuple((pltpu.VMEM(dims, kind) for dims,...  9.18 us
    ppermute x4, starting transfers between devices, shifted(): return lax.ppermute(value, 'z', [(i, (i + by) % ring) for i in range(ring)])  8.92 us
    ppermute x1, starting transfers between devices, local(): lax.ppermute(both[0:256], MORTON, [(i, ends.get(i, i)) for i in range(gro...  6.63 us
    ppermute x6, starting transfers between devices, crossed(): return lax.ppermute(value, SUB, [(i, i ^ k) for i in range(4)])  5.81 us
    ppermute x6, waiting for transfers between devices, crossed(): return lax.ppermute(value, SUB, [(i, i ^ k) for i in range(4)])  2.6 us
    pallas_call x1, Pallas kernels, local(): pl.pallas_call(final_kernel, out_shape=jax.ShapeDtypeStruct((64, R), BF),...  0.96 us
  transfers between devices with their start and end apart: 11, of which 3 were waited for; matrix products, arithmetic and copies ran while one was open for 0% of the time, Pallas kernels for 21%

profile of v8, /device:TPU:9, one launch (start us, length us, event | category | flops | bytes accessed | tf_op | source)
XLA Modules:
  0.0 34.3 jit_solution(7363097951929444742)
XLA Ops:
  0.0 0.7 %collective-permute-start = (bf16[64,128]{1,0:T(8,128)(2,1)}, bf16[64,128]{1,0:T(8,128)(2,1)S(1)}, u32[]{:S(2)}, u32[]{:S(2)}) collective-permute-start(bf16[64,128]{1,0:T(8,128)(2,1)} %m_hbm.1), channel_id=1, source_target_pairs={{0,1},{1,0},{2,3},{3,2},{4,5},{5,4},{6,7},{7,6},{8,9},{9,8},{10,11... | collective-permute-start | bytes 49160 | tf_op jit(solution)/shard_map/ppermute | solution.py:256
  0.7 1.2 %collective-permute-start.1 = (bf16[64,128]{1,0:T(8,128)(2,1)}, bf16[64,128]{1,0:T(8,128)(2,1)S(1)}, u32[]{:S(2)}, u32[]{:S(2)}) collective-permute-start(bf16[64,128]{1,0:T(8,128)(2,1)} %m_hbm.1), channel_id=1, source_target_pairs={{0,2},{1,3},{2,0},{3,1},{4,6},{5,7},{6,4},{7,5},{8,10},{9,11},{10,... | collective-permute-start | bytes 49160 | tf_op jit(solution)/shard_map/ppermute | solution.py:256
  1.9 0.4 %collective-permute-start.2 = (bf16[64,128]{1,0:T(8,128)(2,1)}, bf16[64,128]{1,0:T(8,128)(2,1)S(1)}, u32[]{:S(2)}, u32[]{:S(2)}) collective-permute-start(bf16[64,128]{1,0:T(8,128)(2,1)} %m_hbm.1), channel_id=1, source_target_pairs={{0,3},{1,2},{2,1},{3,0},{4,7},{5,6},{6,5},{7,4},{8,11},{9,10},{10,... | collective-permute-start | bytes 49160 | tf_op jit(solution)/shard_map/ppermute | solution.py:256
  2.3 2.1 %shard_map.127 = (bf16[128,128]{1,0:T(8,128)(2,1)S(1)}, bf16[128,128]{1,0:T(8,128)(2,1)S(1)}, bf16[32,128]{1,0:T(8,128)(2,1)S(1)}, bf16[32,128]{1,0:T(8,128)(2,1...) custom-call(s32[1]{0:T(128)S(6)} %add.7.i_ref, ...), custom_call_target="tpu_custom_call" | custom-call | tf_op jit(solution)/shard_map/pallas_call | solution.py:237
  4.4 0.0 collective-permute-done.p1_ref
  4.4 0.0 collective-permute-done.1.p2_ref
  4.4 0.8 %collective-permute-done.2.p3_ref = bf16[64,128]{1,0:T(8,128)(2,1)S(1)} collective-permute-done((bf16[64,128]{1,0:T(8,128)(2,1)}, bf16[64,128]{1,0:T(8,128)(2,1)S(1)}, u32[]{:S(2)}, u32[]{:S(2)}) %collective-permute-start.2) | collective-permute-done | bytes 16416 | tf_op jit(solution)/shard_map/ppermute | solution.py:256
  5.3 0.5 %shard_map.128.own_ref.both_ref = bf16[304,128]{1,0:T(8,128)(2,1)S(1)} custom-call(bf16[64,128]{1,0:T(8,128)(2,1)S(1)} %get-tuple-element.18.m_ref, bf16[64,128]{1,0:T(8,128)(2,1)S(1)} %collective-permute-done.p1_ref, bf16[64,128]{1,0:T(8,128)(2,1)S(1)} %collective-permute-done.1.p2_ref, bf16[64,128]{1,0:T(8,128)(2,1)S(1)} %collective-permute-done.2.p3_ref, ...), custom_call_target="tpu_custom_call" | custom-call | tf_op jit(solution)/shard_map/pallas_call | solution.py:237
  5.8 5.6 %collective-permute-start.4 = (bf16[304,128]{1,0:T(8,128)(2,1)S(1)}, bf16[304,128]{1,0:T(8,128)(2,1)S(1)}, u32[]{:S(2)}, u32[]{:S(2)}) collective-permute-start(bf16[304,128]{1,0:T(8,128)(2,1)S(1)} %shard_map.128.own_ref.both_ref), channel_id=1, source_target_pairs={{0,28},{4,0},{8,4},{12,8},{16,12},{20,16},{24,20},{28,24},{1,29},{... | collective-permute-start | bytes 233480 | tf_op jit(solution)/shard_map/ppermute | solution.py:287
  11.3 0.0 collective-permute-start.3
  11.4 6.6 %collective-permute-start.5 = (bf16[256,128]{1,0:T(8,128)(2,1)S(1)}, bf16[256,128]{1,0:T(8,128)(2,1)S(1)}, u32[]{:S(2)}, u32[]{:S(2)}) collective-permute-start(bf16[256,128]{1,0:T(8,128)(2,1)S(1)} %slice.18), channel_id=1, source_target_pairs={{0,0},{4,4},{8,8},{12,12},{16,16},{20,20},{24,24},{28,32},{32,28},... | collective-permute-start | bytes 196616 | tf_op jit(solution)/shard_map/ppermute | solution.py:291
  18.0 0.0 collective-permute-done.4.next_ref
  18.0 0.0 collective-permute-done.3.prev_ref
  18.1 0.1 collective-permute-start.7
  18.2 3.2 %collective-permute-start.6 = (bf16[96,128]{1,0:T(8,128)(2,1)S(1)}, bf16[96,128]{1,0:T(8,128)(2,1)S(1)}, u32[]{:S(2)}, u32[]{:S(2)}) collective-permute-start(bf16[96,128]{1,0:T(8,128)(2,1)S(1)} %pad_maximum_fusion.1), channel_id=1, source_target_pairs={{0,12},{4,16},{8,20},{12,24},{16,28},{20,0},{24,4},{28,8},{1,13},{... | collective-permute-start | bytes 73736 | tf_op jit(solution)/shard_map/ppermute | solution.py:287
  21.4 0.0 collective-permute-done.5.far_ref
  21.4 0.0 copy-start
  21.4 5.1 %shard_map.129.acc_ref = f32[256,128]{1,0:T(8,128)S(1)} custom-call(s32[1]{0:T(128)} %bitcast.1.z_ref, s32[1]{0:T(128)} %bitcast.2.g_ref, bf16[304,128]{1,0:T(8,128)(2,1)S(1)} %shard_map.128.own_ref.both_ref, bf16[304,128]{1,0:T(8,128)(2,1)S(1)} %collective-permute-done.3.prev_ref, bf16[304,128]{1,0:T(8,128)(2,1)S(1)} %collective-permute-done.4.next_ref, ...), custom_call_target="tpu_custom_call" | custom-call | tf_op jit(solution)/shard_map/pallas_call | solution.py:237
  26.6 0.0 collective-permute-done.6.p_ref
  26.6 0.0 collective-permute-done.7.m_ref
  26.6 1.5 %shard_map.130 = (bf16[80,128]{1,0:T(8,128)(2,1)S(1)}, bf16[80,128]{1,0:T(8,128)(2,1)S(1)}, bf16[80,128]{1,0:T(8,128)(2,1)S(1)}, bf16[80,128]{1,0:T(8,128)(2,1)S(1)}) custom-call(s32[1]{0:T(128)} %bitcast.q_ref, f32[256,128]{1,0:T(8,128)S(1)} %shard_map.129.acc_ref, bf16[304,128]{1,0:T(8,128)(2,1)S(1)} %shard_map.128.own_ref.both_ref, ...), custom_call_target="tpu_custom_call" | custom-call | tf_op jit(solution)/shard_map/pallas_call | solution.py:237
  28.0 1.8 %collective-permute-start.8 = (bf16[80,128]{1,0:T(8,128)(2,1)S(1)}, bf16[80,128]{1,0:T(8,128)(2,1)S(1)}, u32[]{:S(2)}, u32[]{:S(2)}) collective-permute-start(bf16[80,128]{1,0:T(8,128)(2,1)S(1)} %get-tuple-element.28), channel_id=1, source_target_pairs={{0,1},{1,0},{2,3},{3,2},{4,5},{5,4},{6,7},{7,6},{8,9},{9,8},{10,11... | collective-permute-start | bytes 61448 | tf_op jit(solution)/shard_map/ppermute | solution.py:256
  29.8 0.0 collective-permute-start.9
  29.8 1.7 %collective-permute-start.10 = (bf16[80,128]{1,0:T(8,128)(2,1)S(1)}, bf16[80,128]{1,0:T(8,128)(2,1)S(1)}, u32[]{:S(2)}, u32[]{:S(2)}) collective-permute-start(bf16[80,128]{1,0:T(8,128)(2,1)S(1)} %get-tuple-element.30), channel_id=1, source_target_pairs={{0,3},{1,2},{2,1},{3,0},{4,7},{5,6},{6,5},{7,4},{8,11},{9,10},{10,... | collective-permute-start | bytes 61448 | tf_op jit(solution)/shard_map/ppermute | solution.py:256
  31.5 0.0 collective-permute-done.8.b_ref
  31.6 0.9 %collective-permute-done.9.c_ref = bf16[80,128]{1,0:T(8,128)(2,1)S(1)} collective-permute-done((bf16[80,128]{1,0:T(8,128)(2,1)S(1)}, bf16[80,128]{1,0:T(8,128)(2,1)S(1)}, u32[]{:S(2)}, u32[]{:S(2)}) %collective-permute-start.9) | collective-permute-done | bytes 20512 | tf_op jit(solution)/shard_map/ppermute | solution.py:256
  32.4 0.9 %collective-permute-done.10.d_ref = bf16[80,128]{1,0:T(8,128)(2,1)S(1)} collective-permute-done((bf16[80,128]{1,0:T(8,128)(2,1)S(1)}, bf16[80,128]{1,0:T(8,128)(2,1)S(1)}, u32[]{:S(2)}, u32[]{:S(2)}) %collective-permute-start.10) | collective-permute-done | bytes 20512 | tf_op jit(solution)/shard_map/ppermute | solution.py:256
  33.3 0.0 copy-done
  33.3 1.0 %downward.1 = bf16[64,128]{1,0:T(8,128)(2,1)} custom-call(bf16[80,128]{1,0:T(8,128)(2,1)S(1)} %get-tuple-element.27.a_ref, bf16[80,128]{1,0:T(8,128)(2,1)S(1)} %collective-permute-done.8.b_ref, bf16[80,128]{1,0:T(8,128)(2,1)S(1)} %collective-permute-done.9.c_ref, bf16[80,128]{1,0:T(8,128)(2,1)S(1)} %collective-permute-done.10.d_ref, ...), custom_call_target="tpu_custom_call" | custom-call | tf_op jit(solution)/shard_map/downward/pallas_call | solution.py:303
  (6 shorter events, 0.0 us)
Async XLA Ops:
  0.0 4.4 %collective-permute-start = (bf16[64,128]{1,0:T(8,128)(2,1)}, bf16[64,128]{1,0:T(8,128)(2,1)S(1)}, u32[]{:S(2)}, u32[]{:S(2)}) collective-permute-start(bf16[64,128]{1,0:T(8,128)(2,1)} %m_hbm.1), channel_id=1, source_target_pairs={{0,1},{1,0},{2,3},{3,2},{4,5},{5,4},{6,7},{7,6},{8,9},{9,8},{10,11... | collective-permute-start | bytes 49160 | tf_op jit(solution)/shard_map/ppermute | solution.py:256
  0.7 3.7 %collective-permute-start.1 = (bf16[64,128]{1,0:T(8,128)(2,1)}, bf16[64,128]{1,0:T(8,128)(2,1)S(1)}, u32[]{:S(2)}, u32[]{:S(2)}) collective-permute-start(bf16[64,128]{1,0:T(8,128)(2,1)} %m_hbm.1), channel_id=1, source_target_pairs={{0,2},{1,3},{2,0},{3,1},{4,6},{5,7},{6,4},{7,5},{8,10},{9,11},{10,... | collective-permute-start | bytes 49160 | tf_op jit(solution)/shard_map/ppermute | solution.py:256
  1.9 3.4 %collective-permute-start.2 = (bf16[64,128]{1,0:T(8,128)(2,1)}, bf16[64,128]{1,0:T(8,128)(2,1)S(1)}, u32[]{:S(2)}, u32[]{:S(2)}) collective-permute-start(bf16[64,128]{1,0:T(8,128)(2,1)} %m_hbm.1), channel_id=1, source_target_pairs={{0,3},{1,2},{2,1},{3,0},{4,7},{5,6},{6,5},{7,4},{8,11},{9,10},{10,... | collective-permute-start | bytes 49160 | tf_op jit(solution)/shard_map/ppermute | solution.py:256
  5.8 12.3 %collective-permute-start.4 = (bf16[304,128]{1,0:T(8,128)(2,1)S(1)}, bf16[304,128]{1,0:T(8,128)(2,1)S(1)}, u32[]{:S(2)}, u32[]{:S(2)}) collective-permute-start(bf16[304,128]{1,0:T(8,128)(2,1)S(1)} %shard_map.128.own_ref.both_ref), channel_id=1, source_target_pairs={{0,28},{4,0},{8,4},{12,8},{16,12},{20,16},{24,20},{28,24},{1,29},{... | collective-permute-start | bytes 233480 | tf_op jit(solution)/shard_map/ppermute | solution.py:287
  11.3 6.7 %collective-permute-start.3 = (bf16[304,128]{1,0:T(8,128)(2,1)S(1)}, bf16[304,128]{1,0:T(8,128)(2,1)S(1)}, u32[]{:S(2)}, u32[]{:S(2)}) collective-permute-start(bf16[304,128]{1,0:T(8,128)(2,1)S(1)} %shard_map.128.own_ref.both_ref), channel_id=1, source_target_pairs={{0,4},{4,8},{8,12},{12,16},{16,20},{20,24},{24,28},{28,0},{1,5},{5... | collective-permute-start | bytes 233480 | tf_op jit(solution)/shard_map/ppermute | solution.py:287
  11.4 10.0 %collective-permute-start.5 = (bf16[256,128]{1,0:T(8,128)(2,1)S(1)}, bf16[256,128]{1,0:T(8,128)(2,1)S(1)}, u32[]{:S(2)}, u32[]{:S(2)}) collective-permute-start(bf16[256,128]{1,0:T(8,128)(2,1)S(1)} %slice.18), channel_id=1, source_target_pairs={{0,0},{4,4},{8,8},{12,12},{16,16},{20,20},{24,24},{28,32},{32,28},... | collective-permute-start | bytes 196616 | tf_op jit(solution)/shard_map/ppermute | solution.py:291
  18.1 8.5 %collective-permute-start.7 = (bf16[144,128]{1,0:T(8,128)(2,1)S(1)}, bf16[144,128]{1,0:T(8,128)(2,1)S(1)}, u32[]{:S(2)}, u32[]{:S(2)}) collective-permute-start(bf16[144,128]{1,0:T(8,128)(2,1)S(1)} %pad_maximum_fusion), channel_id=1, source_target_pairs={{0,20},{4,24},{8,28},{12,0},{16,4},{20,8},{24,12},{28,16},{1,21},{... | collective-permute-start | bytes 110600 | tf_op jit(solution)/shard_map/ppermute | solution.py:287
  18.2 8.4 %collective-permute-start.6 = (bf16[96,128]{1,0:T(8,128)(2,1)S(1)}, bf16[96,128]{1,0:T(8,128)(2,1)S(1)}, u32[]{:S(2)}, u32[]{:S(2)}) collective-permute-start(bf16[96,128]{1,0:T(8,128)(2,1)S(1)} %pad_maximum_fusion.1), channel_id=1, source_target_pairs={{0,12},{4,16},{8,20},{12,24},{16,28},{20,0},{24,4},{28,8},{1,13},{... | collective-permute-start | bytes 73736 | tf_op jit(solution)/shard_map/ppermute | solution.py:287
  21.4 11.9 %copy-start = (bf16[8,128,128]{2,1,0:T(8,128)(2,1)S(1)}, bf16[8,128,128]{2,1,0:T(8,128)(2,1)}, u32[]{:S(2)}) copy-start(bf16[8,128,128]{2,1,0:T(8,128)(2,1)} %dn_ref.1) | copy-start | bytes 786436
  28.0 3.5 %collective-permute-start.8 = (bf16[80,128]{1,0:T(8,128)(2,1)S(1)}, bf16[80,128]{1,0:T(8,128)(2,1)S(1)}, u32[]{:S(2)}, u32[]{:S(2)}) collective-permute-start(bf16[80,128]{1,0:T(8,128)(2,1)S(1)} %get-tuple-element.28), channel_id=1, source_target_pairs={{0,1},{1,0},{2,3},{3,2},{4,5},{5,4},{6,7},{7,6},{8,9},{9,8},{10,11... | collective-permute-start | bytes 61448 | tf_op jit(solution)/shard_map/ppermute | solution.py:256
  29.8 2.6 %collective-permute-start.9 = (bf16[80,128]{1,0:T(8,128)(2,1)S(1)}, bf16[80,128]{1,0:T(8,128)(2,1)S(1)}, u32[]{:S(2)}, u32[]{:S(2)}) collective-permute-start(bf16[80,128]{1,0:T(8,128)(2,1)S(1)} %get-tuple-element.29), channel_id=1, source_target_pairs={{0,2},{1,3},{2,0},{3,1},{4,6},{5,7},{6,4},{7,5},{8,10},{9,11},{10,... | collective-permute-start | bytes 61448 | tf_op jit(solution)/shard_map/ppermute | solution.py:256
  29.8 3.5 %collective-permute-start.10 = (bf16[80,128]{1,0:T(8,128)(2,1)S(1)}, bf16[80,128]{1,0:T(8,128)(2,1)S(1)}, u32[]{:S(2)}, u32[]{:S(2)}) collective-permute-start(bf16[80,128]{1,0:T(8,128)(2,1)S(1)} %get-tuple-element.30), channel_id=1, source_target_pairs={{0,3},{1,2},{2,1},{3,0},{4,7},{5,6},{6,5},{7,4},{8,11},{9,10},{10,... | collective-permute-start | bytes 61448 | tf_op jit(solution)/shard_map/ppermute | solution.py:256
